TPU v7x, 32 devices: a whole 2x2x4 slice. The times are simulated.
32 devices in a mesh: seq: 8 (over z, y), tp: 4 (over x, core).
Axes of the slice: x: 2, y: 2, z: 4, core: 2. Of those that a mesh axis runs over, the one named last changes fastest.
Arguments:
- tokens: bfloat16 [16384, 1024], P(('seq', 'tp')), may hold values from -6 to 6
- query_weight: bfloat16 [1024, 1024], replicated, may hold values from -0.1875 to 0.1875
- key_weight: bfloat16 [1024, 1024], replicated, may hold values from -0.1875 to 0.1875
- value_weight: bfloat16 [1024, 1024], replicated, may hold values from -0.1875 to 0.1875
- modulate_weight: bfloat16 [1024, 1024], replicated, may hold values from -0.1875 to 0.1875
- output_weight: bfloat16 [1024, 1024], replicated, may hold values from -0.1875 to 0.1875
- gate_weight: bfloat16 [1024, 2816], P(None, 'tp'), may hold values from -0.1875 to 0.1875
- linear_weight: bfloat16 [1024, 2816], P(None, 'tp'), may hold values from -0.1875 to 0.1875
- down_weight: bfloat16 [2816, 1024], P('tp'), may hold values from -0.109375 to 0.109375
- cotangent: bfloat16 [16384, 1024], P(('seq', 'tp')), may hold values from -6 to 6
- decay_exponent: int32 [8], replicated, may hold values from 5 to 17
Outputs:
- mixed: bfloat16 [16384, 1024], P(('seq', 'tp'))
- tokens_grad: float32 [16384, 1024], P(('seq', 'tp'))
- query_grad: float32 [1024, 1024], replicated
- key_grad: float32 [1024, 1024], replicated
- value_grad: float32 [1024, 1024], replicated
- modulate_grad: float32 [1024, 1024], replicated
- output_grad: float32 [1024, 1024], replicated
- gate_grad: float32 [1024, 2816], P('seq', 'tp')
- linear_grad: float32 [1024, 2816], P('seq', 'tp')
- down_grad: float32 [2816, 1024], P('tp', 'seq')
Inputs may be any that keep to these rules, and one draw needn't show every extreme that they name: `decay_exponent`: head h decays by a factor 2 ** (-2 ** (-decay_exponent_h)) a token.
All inputs are finite; a program needn't handle non-finite values.
Results may differ from a plain program's by a relative error of at most 0.015.
Values may be sent and summed in bfloat16 or wider, within the bound.
No kernel may reach another device: no remote copies, remote signals or barrier semaphores. Data moves between devices by JAX's collectives and lax.ppermute only.
A program may use at most 320 MiB of HBM per device.

v0:
```python
import math

import jax
import jax.numpy as jnp
from jax import lax
from jax.sharding import PartitionSpec as P

BLOCK = 256
SEQ_LEN = 16384


EPS = 1e-06
HIGH = lax.Precision.HIGHEST
FLOAT = jnp.float32
BHALF = jnp.bfloat16


def prefix(part, axis, combine, identity, reverse):
    count = lax.axis_size(axis)
    place = lax.axis_index(axis)
    ahead = count - 1 - place if reverse else place
    gathered = jax.tree.map(lambda a: lax.all_gather(a, axis), part)
    state = jax.tree.map(lambda a, e: jnp.zeros_like(a) + jnp.asarray(e, a.dtype), part, identity)

    def one(lap, state):
        source = count - 1 - lap if reverse else lap
        return combine(
            state, jax.tree.map(lambda a: lax.dynamic_index_in_dim(a, source, 0, False), gathered)
        )

    return lax.fori_loop(0, ahead, one, state)


def srms(values):
    return values * lax.rsqrt(jnp.mean(values * values, axis=-1, keepdims=True) + EPS)


def srms_back(values, gradient):
    scaled = lax.rsqrt(jnp.mean(values * values, axis=-1, keepdims=True) + EPS)
    normed = values * scaled
    return scaled * (gradient - normed * jnp.mean(gradient * normed, axis=-1, keepdims=True))


def swish(values):
    return values * jax.nn.sigmoid(values)


def swish_slope(values):
    sigmoid = jax.nn.sigmoid(values)
    return sigmoid * (1.0 + values * (1.0 - sigmoid))


def angles(position, halves):
    column = jnp.arange(halves, dtype=jnp.int32)
    factor = 1 + jnp.right_shift(jnp.full((halves,), 16384, jnp.int32), column // 4)
    phase = position[:, None] * factor[None, :] % 65536
    turned = phase.astype(jnp.float32) * (2.0 * math.pi / 65536.0)
    return (jnp.cos(turned)[:, None, :], jnp.sin(turned)[:, None, :])


def rotate(values, cosine, sine):
    halves = values.shape[-1] // 2
    first = values[..., :halves]
    second = values[..., halves:]
    return jnp.concatenate(
        [first * cosine - second * sine, first * sine + second * cosine], axis=-1
    )


def unrotate(values, cosine, sine):
    halves = values.shape[-1] // 2
    first = values[..., :halves]
    second = values[..., halves:]
    return jnp.concatenate(
        [first * cosine + second * sine, second * cosine - first * sine], axis=-1
    )


def combine(earlier, latter):
    return (earlier[0] * latter[0], latter[0][:, None, None] * earlier[1] + latter[1])


def matmul(left, right):
    return jnp.dot(left, right, preferred_element_type=FLOAT)


def contract_rows(left, right):
    return lax.dot_general(left, right, (((0,), (0,)), ((), ())), preferred_element_type=FLOAT)


def contract_cols(left, right):
    return lax.dot_general(left, right, (((1,), (1,)), ((), ())), preferred_element_type=FLOAT)


def shards(
    tokens,
    query_weight,
    key_weight,
    value_weight,
    modulate_weight,
    output_weight,
    gate_weight,
    linear_weight,
    down_weight,
    cotangent,
    decay_exponent,
):
    tok_count, width = tokens.shape
    heads = decay_exponent.shape[0]
    head_dim = width // heads
    devices = lax.axis_size("seq") * lax.axis_size("tp")
    seq_length = min(SEQ_LEN, tok_count * devices)
    device_place = lax.axis_index("seq") * lax.axis_size("tp") + lax.axis_index("tp")
    first_token = device_place * tok_count
    position = (first_token + jnp.arange(tok_count, dtype=jnp.int32)) % seq_length
    is_start = first_token % seq_length == 0
    decay_rate = jnp.exp2(-decay_exponent.astype(FLOAT))
    cosine, sine = angles(position, head_dim // 2)
    offsets = jnp.arange(BLOCK, dtype=FLOAT)
    distance = offsets[:, None] - offsets[None, :]
    decay_matrix = jnp.where(
        distance[None] >= 0.0,
        jnp.exp2(-jnp.maximum(distance, 0.0)[None] * decay_rate[:, None, None]),
        0.0,
    )
    query_decay = jnp.exp2(-(offsets + 1.0)[:, None] * decay_rate[None, :])[:, :, None]
    key_decay = jnp.exp2(-(BLOCK - 1.0 - offsets)[:, None] * decay_rate[None, :])[:, :, None]
    block_decay = jnp.exp2(-BLOCK * decay_rate)[:, None, None]
    device_decay = jnp.where(is_start, 0.0, jnp.exp2(-tok_count * decay_rate))
    blocks = tok_count // BLOCK
    inputs = tokens.astype(FLOAT)
    normed = srms(inputs).astype(BHALF)
    pre_query = matmul(normed, query_weight)
    pre_key = matmul(normed, key_weight)
    modulate = matmul(normed, modulate_weight)
    query = rotate(swish(pre_query).reshape(tok_count, heads, head_dim), cosine, sine).astype(BHALF)
    keys = rotate(swish(pre_key).reshape(tok_count, heads, head_dim), cosine, sine).astype(BHALF)
    values = matmul(normed, value_weight).astype(BHALF).reshape(tok_count, heads, head_dim)
    key_states = []
    decayed_queries = []
    decayed_keys = []
    local_state = jnp.zeros((heads, head_dim, head_dim), FLOAT)
    for number in range(blocks):
        window = slice(number * BLOCK, (number + 1) * BLOCK)
        decayed_key = (keys[window].astype(FLOAT) * key_decay).astype(BHALF)
        decayed_query = (query[window].astype(FLOAT) * query_decay).astype(BHALF)
        decayed_keys.append(decayed_key)
        decayed_queries.append(decayed_query)
        contrib = jnp.einsum(
            "jhd,jhe->hde", decayed_key, values[window], preferred_element_type=FLOAT
        )
        key_states.append(contrib)
        local_state = block_decay * local_state + contrib
    identity = (jnp.ones_like(device_decay), jnp.zeros_like(local_state))
    carried = prefix((device_decay, local_state), ("seq", "tp"), combine, identity, False)
    state = jnp.where(is_start, 0.0, carried[1])
    pieces = []
    used_states = []
    for number in range(blocks):
        window = slice(number * BLOCK, (number + 1) * BLOCK)
        block_query = query[window]
        scores = jnp.einsum("ihd,jhd->hij", block_query, keys[window], preferred_element_type=FLOAT)
        probs = (scores * decay_matrix).astype(BHALF)
        intra = jnp.einsum("hij,jhd->ihd", probs, values[window], preferred_element_type=FLOAT)
        state_used = state.astype(BHALF)
        inter = jnp.einsum(
            "ihd,hde->ihe", decayed_queries[number], state_used, preferred_element_type=FLOAT
        )
        used_states.append(state_used)
        state = block_decay * state + key_states[number]
        pieces.append(intra + inter)
    attended = jnp.concatenate(pieces, axis=0).reshape(tok_count, width)
    normed_out = srms(attended)
    gated = (normed_out * modulate).astype(BHALF)
    resid = inputs + matmul(gated, output_weight)
    normed_two = srms(resid).astype(BHALF)
    gathered = lax.all_gather(normed_two, "tp", axis=0, tiled=True)
    gate_pre = matmul(gathered, gate_weight)
    linear_pre = matmul(gathered, linear_weight)
    hidden = (gate_pre * linear_pre).astype(BHALF)
    feed = lax.psum_scatter(
        matmul(hidden, down_weight).astype(jnp.bfloat16), "tp", scatter_dimension=0, tiled=True
    ).astype(jnp.float32)
    mixed = (resid + feed).astype(BHALF)
    cot_rows = lax.all_gather(cotangent, "tp", axis=0, tiled=True)
    down_part = contract_rows(hidden, cot_rows)
    hidden_cot = contract_cols(cot_rows, down_weight)
    gate_back = (hidden_cot * linear_pre).astype(BHALF)
    linear_back = (hidden_cot * gate_pre).astype(BHALF)
    gate_part = contract_rows(gathered, gate_back)
    linear_part = contract_rows(gathered, linear_back)
    normed_cot = lax.psum_scatter(
        contract_cols(gate_back, gate_weight) + contract_cols(linear_back, linear_weight),
        "tp",
        scatter_dimension=0,
        tiled=True,
    )
    gate_grad, linear_grad, down_grad = (
        lax.psum_scatter(
            gate_part.astype(jnp.bfloat16), "seq", scatter_dimension=0, tiled=True
        ).astype(jnp.float32),
        lax.psum_scatter(
            linear_part.astype(jnp.bfloat16), "seq", scatter_dimension=0, tiled=True
        ).astype(jnp.float32),
        lax.psum_scatter(
            down_part.astype(jnp.bfloat16), "seq", scatter_dimension=1, tiled=True
        ).astype(jnp.float32),
    )
    resid_cot = cotangent.astype(FLOAT) + srms_back(resid, normed_cot)
    branch_back = resid_cot.astype(BHALF)
    output_part = contract_rows(gated, branch_back)
    gated_cot = contract_cols(branch_back, output_weight)
    modulate_back = (gated_cot * normed_out).astype(BHALF)
    attended_back = (
        srms_back(attended, gated_cot * modulate).astype(BHALF).reshape(tok_count, heads, head_dim)
    )
    direct = []
    for number in range(blocks):
        window = slice(number * BLOCK, (number + 1) * BLOCK)
        direct.append(
            jnp.einsum(
                "ihd,ihe->hde",
                decayed_queries[number],
                attended_back[window],
                preferred_element_type=FLOAT,
            )
        )
    inbound = jnp.zeros_like(local_state)
    for number in reversed(range(blocks)):
        inbound = block_decay * inbound + direct[number]
    masked = jnp.where(is_start, 0.0, inbound)
    after = prefix((device_decay, masked), ("seq", "tp"), combine, identity, True)
    outer = after[1]
    accum = jnp.zeros_like(local_state)
    query_parts = []
    key_parts = []
    value_parts = []
    for number in reversed(range(blocks)):
        window = slice(number * BLOCK, (number + 1) * BLOCK)
        state_cot = outer + accum
        outer = block_decay * outer
        accum = block_decay * accum + direct[number]
        block_query = query[window]
        block_key = keys[window]
        block_value = values[window]
        block_back = attended_back[window]
        key_part = (
            jnp.einsum("hde,jhe->jhd", state_cot, block_value.astype(FLOAT), precision=HIGH)
            * key_decay
        )
        value_part = jnp.einsum(
            "jhd,hde->jhe", decayed_keys[number].astype(FLOAT), state_cot, precision=HIGH
        )
        scores = jnp.einsum("ihd,jhd->hij", block_query, block_key, preferred_element_type=FLOAT)
        probs = (scores * decay_matrix).astype(BHALF)
        prob_cot = jnp.einsum("ihe,jhe->hij", block_back, block_value, preferred_element_type=FLOAT)
        score_back = (prob_cot * decay_matrix).astype(BHALF)
        value_part = value_part + jnp.einsum(
            "hij,ihe->jhe", probs, block_back, preferred_element_type=FLOAT
        )
        key_part = key_part + jnp.einsum(
            "hij,ihd->jhd", score_back, block_query, preferred_element_type=FLOAT
        )
        query_part = jnp.einsum("hij,jhd->ihd", score_back, block_key, preferred_element_type=FLOAT)
        query_part = (
            query_part
            + jnp.einsum(
                "ihe,hde->ihd", block_back, used_states[number], preferred_element_type=FLOAT
            )
            * query_decay
        )
        query_parts.insert(0, query_part)
        key_parts.insert(0, key_part)
        value_parts.insert(0, value_part)
    query_cot = jnp.concatenate(query_parts, axis=0)
    key_cot = jnp.concatenate(key_parts, axis=0)
    value_cot = jnp.concatenate(value_parts, axis=0)
    query_back = (
        unrotate(query_cot, cosine, sine).reshape(tok_count, width) * swish_slope(pre_query)
    ).astype(BHALF)
    key_back = (
        unrotate(key_cot, cosine, sine).reshape(tok_count, width) * swish_slope(pre_key)
    ).astype(BHALF)
    value_back = value_cot.reshape(tok_count, width).astype(BHALF)
    normed_grad = contract_cols(query_back, query_weight) + contract_cols(key_back, key_weight)
    normed_grad = (
        normed_grad
        + contract_cols(value_back, value_weight)
        + contract_cols(modulate_back, modulate_weight)
    )
    tokens_grad = resid_cot + srms_back(inputs, normed_grad)
    query_grad, key_grad, value_grad, modulate_grad, output_grad = lax.psum(
        (
            contract_rows(normed, query_back),
            contract_rows(normed, key_back),
            contract_rows(normed, value_back),
            contract_rows(normed, modulate_back),
            output_part,
        ),
        ("seq", "tp"),
    )
    return (
        mixed,
        tokens_grad,
        query_grad,
        key_grad,
        value_grad,
        modulate_grad,
        output_grad,
        gate_grad,
        linear_grad,
        down_grad,
    )


def solution(mesh):
    return jax.shard_map(
        shards,
        mesh=mesh,
        in_specs=(
            P(("seq", "tp"), None),
            P(),
            P(),
            P(),
            P(),
            P(),
            P(None, "tp"),
            P(None, "tp"),
            P("tp", None),
            P(("seq", "tp"), None),
            P(),
        ),
        out_specs=(
            P(("seq", "tp"), None),
            P(("seq", "tp"), None),
            P(),
            P(),
            P(),
            P(),
            P(),
            P("seq", "tp"),
            P("seq", "tp"),
            P("tp", "seq"),
        ),
        check_vma=False,
    )
```

profile of v0, /device:TPU:1, one launch (start us, length us, event | category | flops | bytes accessed | tf_op | source)
XLA Modules:
  0.0 1146.1 jit_solution(10695310475397209086)
XLA Ops:
  8.1 1.5 fusion.7
  9.7 3.3 convolution_convert_fusion.4
  19.4 2.7 fusion.80
  22.1 2.7 fusion.79
  26.5 5.1 subtract_convert_fusion
  31.6 2.1 fusion.25
  36.3 1.5 convolution_add_fusion.7
  37.9 42.3 %all-reduce = f32[256]{0:T(256)S(1)} all-reduce(f32[256]{0:T(256)S(1)} %get-tuple-element.206), channel_id=2, replica_groups=mesh['seq'=8,'tp'=4] {'seq','tp'}, use_global_device_ids=true, to_apply=%add | all-reduce | flops 256 | bytes 2048
  80.5 2.0 multiply_convert_fusion.9
  86.8 69.9 %all-gather.12.cloned.1.call-done = f32[256,128,128]{2,1,0:T(8,128)} async-done(((f32[8,128,128]{2,1,0:T(8,128)}), f32[256,128,128]{2,1,0:T(8,128)}) %all-gather.12.cloned.1.call-update) | async-done | bytes 16777232 | tf_op jit(solution)/shard_map/all_gather | solution.py:22
  157.5 2.1 while.26
  157.5 2.1 bitcast_add_fusion.4
  161.1 2.2 fusion.19
  164.3 1.6 multiply_reduce_fusion.3
  165.9 2.9 copy.115
  168.7 4.8 multiply_convert_fusion.7
  178.4 95.7 %all-gather.8.cloned.1.call-done = bf16[2048,1024]{1,0:T(8,128)(2,1)} async-done(((bf16[512,1024]{1,0:T(8,128)(2,1)}), bf16[2048,1024]{1,0:T(8,128)(2,1)}) %all-gather.8.cloned.1.call-update) | async-done | bytes 4194320 | tf_op jit(solution)/shard_map/all_gather | solution.py:177
  274.1 8.4 fusion.83
  282.5 5.1 fusion.82
  287.6 22.6 %all-gather.10.cloned.1.call-done = bf16[2048,1024]{1,0:T(8,128)(2,1)} async-done(((bf16[512,1024]{1,0:T(8,128)(2,1)}), bf16[2048,1024]{1,0:T(8,128)(2,1)}) %all-gather.10.cloned.1.call-update) | async-done | bytes 4194320 | tf_op jit(solution)/shard_map/all_gather | solution.py:185
  310.1 11.0 multiply_convert_fusion
  321.2 3.5 fusion.84
  324.7 6.0 convolution_add_fusion
  331.0 7.7 convolution_convert_fusion
  338.8 63.4 %reduce-scatter.14.cloned.1.call-done = f32[512,1024]{1,0:T(8,128)} async-done(((f32[2048,1024]{1,0:T(8,128)}), f32[512,1024]{1,0:T(8,128)}) %reduce-scatter.14.cloned.1.call-update) | async-done | bytes 2097168 | tf_op jit(solution)/shard_map/reduce_scatter | solution.py:192
  402.2 2.6 multiply_reduce_fusion.1
  404.8 45.1 %reduce-scatter.12.cloned.1.call-done = bf16[512,1024]{1,0:T(8,128)(2,1)} async-done(((bf16[2048,1024]{1,0:T(8,128)(2,1)}), bf16[512,1024]{1,0:T(8,128)(2,1)}) %reduce-scatter.12.cloned.1.call-update) | async-done | bytes 1048592 | tf_op jit(solution)/shard_map/reduce_scatter | solution.py:181
  449.9 4.5 multiply_add_fusion.2
  454.4 2.5 multiply_reduce_fusion
  458.5 1.6 convolution_add_fusion.6
  461.4 2.8 fusion.24
  464.2 7.3 convolution_convert_fusion.3
  471.5 2.7 copy.166
  474.7 7.3 convolution_convert_fusion.1
  482.0 2.6 copy.164
  484.7 7.3 convolution_convert_fusion.2
  492.0 2.6 copy.162
  494.7 1.7 multiply_convert_fusion.5
  501.7 3.3 fusion.38
  505.1 1.5 fusion.17
  506.6 1.6 fusion.15
  508.1 3.4 fusion.64
  511.5 68.1 %all-gather.14.cloned.1.call-done = f32[256,128,128]{2,1,0:T(8,128)} async-done(((f32[8,128,128]{2,1,0:T(8,128)}), f32[256,128,128]{2,1,0:T(8,128)}) %all-gather.14.cloned.1.call-update) | async-done | bytes 16777232 | tf_op jit(solution)/shard_map/all_gather | solution.py:22
  579.7 37.3 %while.27 = (s32[]{:T(128)}, f32[8,128,128]{2,1,0:T(8,128)S(1)}, s32[]{:T(128)}, f32[32,8]{1,0:T(8,128)S(1)}, f32[32,8,128,128]{3,2,1,0:T(8,128)}, /*index=5*/s32[]{:T(128)}, s32[]{:T(128)}, s32[]{:T(128)}, s32[]{:T(128)}) while((s32[]{:T(128)}, f32[8,128,128]{2,1,0:T(8,128)S(1)}, s32[]{:T(128)}, f32[32,8]{1,0:T(8,128)S(1)}, ...), condition=%wide.region_10.11_spmd, body=%wide.region_9.10_spmd.sunk | while | flops 262150 | bytes 1573115 | solution.py:31
  617.0 2.2 fusion.42
  625.7 3.5 fusion.66
  629.2 1.6 multiply_add_fusion
  631.8 3.4 fusion.70
  637.2 3.4 fusion.68
  640.6 4.0 reduce-scatter.20.cloned.1.call-done
  646.4 65.8 %reduce-scatter.18.cloned.1.call-done = bf16[128,704]{1,0:T(8,128)(2,1)} async-done(((bf16[1024,704]{1,0:T(8,128)(2,1)}), bf16[128,704]{1,0:T(8,128)(2,1)}) %reduce-scatter.18.cloned.1.call-update) | async-done | bytes 180240
  714.1 66.0 %reduce-scatter.16.cloned.1.call-done = bf16[128,704]{1,0:T(8,128)(2,1)} async-done(((bf16[1024,704]{1,0:T(8,128)(2,1)}), bf16[128,704]{1,0:T(8,128)(2,1)}) %reduce-scatter.16.cloned.1.call-update) | async-done | bytes 180240
  781.9 3.0 fusion.87
  788.8 1.6 fusion.3
  790.4 1.8 fusion.6
  792.2 327.7 %all-reduce.4.cloned.1.call-done = (f32[1024,1024]{1,0:T(8,128)}, f32[1024,1024]{1,0:T(8,128)}, f32[1024,1024]{1,0:T(8,128)}, f32[1024,1024]{1,0:T(8,128)}, f32[1024,1024]{1,0:T(8,128)}) async-done(((f32[1024,1024]{1,0:T(8,128)}, f32[1024,1024]{1,0:T(8,128)}, f32[1024,1024]{1,0:T(8,128)}, f32[1024,1024]{1,0:T(8,128)}, f32[1024,1024]{1,0:T(8,128)}), (f32[1024,1024]{1,0:T(8,128)}, f32[1024,1024]{1,0:T(8,128)}, ...) | async-done | bytes 20971536 | tf_op jit(solution)/shard_map/psum | solution.py:292
  1120.0 4.9 copy.240
  1124.9 2.1 copy.241
  1127.0 1.6 copy-done.61
  1128.6 2.1 copy.242
  1130.7 1.6 copy-done.60
  1132.3 2.1 copy.243
  1134.4 1.6 copy-done.59
  1136.0 2.1 copy.244
  (301 shorter events, 89.1 us)
Async XLA Ops:
  7.2 166.4 %copy-start = (bf16[1024,1024]{1,0:T(8,128)(2,1)S(1)}, bf16[1024,1024]{1,0:T(8,128)(2,1)}, u32[]{:S(2)}) copy-start(bf16[1024,1024]{1,0:T(8,128)(2,1)} %param.20) | copy-start | bytes 6291460
  7.2 149.5 %all-gather.12.cloned.1.call-start = ((), (), s32[]{:S(2)}) async-start(), calls=%async_computation.9 | async-start | bytes 17301504 | tf_op jit(solution)/shard_map/all_gather | solution.py:22
  9.6 4.4 copy-start.2
  9.6 4.4 copy-start.77
  15.7 2.4 copy-start.18
  25.8 5.8 copy-start.66
  31.6 2.9 copy-start.27
  31.6 4.6 copy-start.36
  37.8 236.2 %all-gather.8.cloned.1.call-start = ((), (), s32[]{:S(2)}) async-start(), calls=%async_computation.5 | async-start | bytes 5242880 | tf_op jit(solution)/shard_map/all_gather | solution.py:177
  80.4 2.7 copy-start.72
  80.5 2.0 copy-start.23
  80.5 2.0 copy-start.32
  82.5 2.9 copy-start.55
  159.7 3.7 copy-start.24
  159.7 3.7 copy-start.65
  161.1 2.2 copy-start.68
  177.4 132.7 %all-gather.10.cloned.1.call-start = ((), (), s32[]{:S(2)}) async-start(), calls=%async_computation.7 | async-start | bytes 5242880 | tf_op jit(solution)/shard_map/all_gather | solution.py:185
  178.2 224.0 %reduce-scatter.14.cloned.1.call-start = ((), (), s32[]{:S(2)}) async-start(), calls=%async_computation.8 | async-start | bytes 10485760 | tf_op jit(solution)/shard_map/reduce_scatter | solution.py:192
  274.1 8.4 copy-start.74
  274.1 8.4 copy-start.79
  310.1 11.0 copy-start.80
  321.2 3.5 copy-start.14
  321.2 3.5 copy-start.15
  321.2 3.5 copy-start.81
  330.7 119.1 %reduce-scatter.12.cloned.1.call-start = ((), (), s32[]{:S(2)}) async-start(), calls=%async_computation.6 | async-start | bytes 5242880 | tf_op jit(solution)/shard_map/reduce_scatter | solution.py:181
  338.8 240.8 %all-gather.14.cloned.1.call-start = ((), (), s32[]{:S(2)}) async-start(), calls=%async_computation.10 | async-start | bytes 17301504 | tf_op jit(solution)/shard_map/all_gather | solution.py:22
  449.9 4.5 copy-start.3
  449.9 4.5 copy-start.9
  454.4 2.6 copy-start.5
  458.2 3.1 copy-start.35
  458.4 39.9 %copy-start.40 = (bf16[256,1024]{0,1:T(8,128)(2,1)}, bf16[256,1024]{0,1:T(8,128)(2,1)S(1)}, u32[]{:S(2)}) copy-start(bf16[256,1024]{0,1:T(8,128)(2,1)S(1)} %copy.173) | copy-start | bytes 1572868
  461.4 33.3 %copy-start.44 = (bf16[256,1024]{0,1:T(8,128)(2,1)}, bf16[256,1024]{0,1:T(8,128)(2,1)S(1)}, u32[]{:S(2)}) copy-start(bf16[256,1024]{0,1:T(8,128)(2,1)S(1)} %copy.172) | copy-start | bytes 1572868
  464.2 180.4 %reduce-scatter.20.cloned.1.call-start = ((), (), s32[]{:S(2)}) async-start(), calls=%async_computation.13 | async-start | bytes 1769472
  474.2 238.0 %reduce-scatter.18.cloned.1.call-start = ((), (), s32[]{:S(2)}) async-start(), calls=%async_computation.12 | async-start | bytes 1769472
  484.6 295.4 %reduce-scatter.16.cloned.1.call-start = ((), (), s32[]{:S(2)}) async-start(), calls=%async_computation.11 | async-start | bytes 1769472
  492.0 2.7 copy-start.29
  494.6 625.3 %all-reduce.4.cloned.1.call-start = ((), (), s32[]{:S(2)}) async-start(), calls=%async_computation.14 | async-start | bytes 41943040 | tf_op jit(solution)/shard_map/psum | solution.py:292
  496.4 1.9 copy-start.38
  496.4 1.9 copy-start.73
  498.4 2.5 copy-start.33
  499.4 1.9 copy-start.6
  499.4 2.3 copy-start.13
  501.7 3.3 copy-start.4
  501.7 3.3 copy-start.45
  579.6 37.3 %copy-start.22 = (bf16[256,8,128]{2,0,1:T(8,128)(2,1)S(1)}, bf16[256,8,128]{2,0,1:T(8,128)(2,1)}, u32[]{:S(2)}) copy-start(bf16[256,8,128]{2,0,1:T(8,128)(2,1)} %copy-done.20) | copy-start | bytes 1572868
  616.9 2.3 copy-start.34
  616.9 3.2 copy-start.30
  617.0 3.2 copy-start.47
  617.0 3.2 copy-start.64
  625.7 3.5 copy-start.57
  625.7 3.5 copy-start.63
  625.7 3.5 copy-start.67
  631.8 3.4 copy-start.49
  631.8 3.4 copy-start.17
  640.6 141.4 %copy-start.71 = (bf16[512,8,128]{0,2,1:T(8,128)(2,1)S(1)}, bf16[512,8,128]{0,2,1:T(8,128)(2,1)}, u32[]{:S(2)}) copy-start(bf16[512,8,128]{0,2,1:T(8,128)(2,1)} %copy-done.70) | copy-start | bytes 3145732
  781.9 3.0 copy-start.52
  781.9 3.1 copy-start.76
  785.0 1.9 copy-start.78
  786.9 1.9 copy-start.43
  1119.9 4.9 copy-start.62
  1124.9 3.7 copy-start.61
  1128.6 3.7 copy-start.60
  1132.3 3.7 copy-start.59
  1136.0 3.1 copy-start.1
  (28 other events, 36.6 us)
Sparse Core Ops, SparseCore 0:
  37.9 118.7 all-gather.11
  177.6 96.4 all-gather.7
  275.6 34.4 all-gather.9
  330.9 71.2 reduce-scatter.13
  405.3 44.5 reduce-scatter.11
  464.3 115.2 all-gather.13
  583.0 61.5 reduce-scatter.19
  648.4 63.7 reduce-scatter.17
  716.2 63.8 reduce-scatter.15
  788.0 331.8 all-reduce.3
where the time goes:
time: 1160 us; the launch traced here: 1150 us
  waiting for transfers between devices  829 us (71%)
  matrix products  132 us (11%)
  other arithmetic  70 us (6%)
  local copies, waits for them, and re-layouts  54.8 us (5%)
  blocking collectives  42.3 us (4%)
  between operations  15.3 us (1%)
    psum x1, waiting for transfers between devices, shards(): lax.psum((contract_rows(normed, query_back), contract_rows(normed, key_ba...  328 us
    all_gather x2, waiting for transfers between devices, prefix(): gathered = jax.tree.map(lambda a: lax.all_gather(a, axis), part)  138 us
    unnamed x13, waiting for transfers between devices  137 us
    all_gather x1, waiting for transfers between devices, shards(): gathered = lax.all_gather(normed_two, 'tp', axis=0, tiled=True)  95.7 us
    reduce_scatter x1, waiting for transfers between devices, shards(): lax.psum_scatter(contract_cols(gate_back, gate_weight) + contract_cols(li...  63.4 us
    reduce_scatter x1, waiting for transfers between devices, shards(): lax.psum_scatter(matmul(hidden, down_weight).astype(jnp.bfloat16), 'tp',...  45.1 us
    unnamed x179, local copies, waits for them, and re-layouts  43 us
    unnamed x1, blocking collectives  42.3 us
  transfers between devices with their start and end apart: 10, of which 10 were waited for; matrix products, arithmetic and copies ran while one was open for 13% of the time, Pallas kernels for 0%

commit v1 on v0

--- a/solution.py
+++ b/solution.py
@@ -15,20 +15,106 @@
 BHALF = jnp.bfloat16
 
 
-def prefix(part, axis, combine, identity, reverse):
-    count = lax.axis_size(axis)
-    place = lax.axis_index(axis)
-    ahead = count - 1 - place if reverse else place
-    gathered = jax.tree.map(lambda a: lax.all_gather(a, axis), part)
-    state = jax.tree.map(lambda a, e: jnp.zeros_like(a) + jnp.asarray(e, a.dtype), part, identity)
-
-    def one(lap, state):
-        source = count - 1 - lap if reverse else lap
-        return combine(
-            state, jax.tree.map(lambda a: lax.dynamic_index_in_dim(a, source, 0, False), gathered)
-        )
-
-    return lax.fori_loop(0, ahead, one, state)
+def bits_of(count):
+    return [1 << b for b in range(count.bit_length() - 1)]
+
+
+def swap(value, mask, axes=("seq", "tp")):
+    count = lax.axis_size(axes)
+    return lax.ppermute(value, axes, [(s, s ^ mask) for s in range(count)])
+
+
+def flat_place():
+    return lax.axis_index("seq") * lax.axis_size("tp") + lax.axis_index("tp")
+
+
+def bit_of(place, mask):
+    return (place // mask) % 2
+
+
+def halve(value, masks, place):
+    for mask in masks:
+        halves = value.reshape((2, value.shape[0] // 2) + value.shape[1:])
+        bit = bit_of(place, mask)
+        keep = lax.dynamic_index_in_dim(halves, bit, 0, False)
+        send = lax.dynamic_index_in_dim(halves, 1 - bit, 0, False)
+        value = (keep.astype(FLOAT) + swap(send.astype(BHALF), mask).astype(FLOAT)).astype(BHALF)
+    return value
+
+
+def double(value, masks, place):
+    for mask in masks:
+        other = swap(value, mask)
+        bit = bit_of(place, mask)
+        first = jnp.where(bit == 0, value, other)
+        second = jnp.where(bit == 0, other, value)
+        value = jnp.concatenate([first, second], axis=0)
+    return value
+
+
+def all_reduce(value, masks, place):
+    part = halve(value, masks, place)
+    return double(part, list(reversed(masks)), place).astype(FLOAT)
+
+
+def decayed_scan(state, device_decay, span, place, reverse):
+    heads = state.shape[0]
+    half = heads // 2
+    bit = bit_of(place, 1)
+    halves = state.reshape((2, half) + state.shape[1:])
+    mine = lax.dynamic_index_in_dim(halves, bit, 0, False)
+    theirs = lax.dynamic_index_in_dim(halves, 1 - bit, 0, False)
+    other = swap(theirs.astype(BHALF), 1).astype(FLOAT)
+    decay = lax.dynamic_index_in_dim(device_decay.reshape(2, half), bit, 0, False)
+    later = 1 - bit if reverse else bit
+
+    def power(count):
+        return (decay ** count)[:, None, None]
+
+    core_later = jnp.where(later == 1, mine, other)
+    core_first = jnp.where(later == 1, other, mine)
+    total = power(1.0) * core_first + core_later
+    prefix = jnp.zeros_like(total)
+    for mask in bits_of(span)[1:]:
+        bit = bit_of(place, mask)
+        later = 1 - bit if reverse else bit
+        got = swap(total.astype(BHALF), mask).astype(FLOAT)
+        within = (place % mask) // 2
+        if reverse:
+            within = mask // 2 - 1 - within
+        scale = power(2.0 * within.astype(FLOAT))
+        prefix = prefix + jnp.where(later == 1, scale * got, 0.0)
+        total = jnp.where(later == 1, power(float(mask)) * got + total, power(float(mask)) * total + got)
+    first_pre = prefix
+    second_pre = power(1.0) * prefix + core_first
+    bit = bit_of(place, 1)
+    later = 1 - bit if reverse else bit
+    own = jnp.where(later == 1, second_pre, first_pre)
+    away = jnp.where(later == 1, first_pre, second_pre)
+    got = swap(away.astype(BHALF), 1).astype(FLOAT)
+    low = jnp.where(bit == 0, own, got)
+    high = jnp.where(bit == 0, got, own)
+    return jnp.concatenate([low, high], axis=0)
+
+
+def gather_group(value, masks):
+    rows = {0: value}
+    for mask in masks:
+        for r in list(rows):
+            rows[r | mask] = swap(rows[r], mask)
+    return [rows[r] for r in range(len(rows))]
+
+
+def scatter_group(parts, masks):
+    parts = list(parts)
+    rows = dict(enumerate(parts))
+    for mask in masks:
+        for r in sorted(rows):
+            if r & mask:
+                got = swap(rows[r].astype(BHALF), mask)
+                rows[r ^ mask] = rows[r ^ mask] + got.astype(FLOAT)
+        rows = {r: v for r, v in rows.items() if not r & mask}
+    return rows[0]
 
 
 def srms(values):
@@ -74,10 +160,6 @@
     return jnp.concatenate(
         [first * cosine + second * sine, second * cosine - first * sine], axis=-1
     )
-
-
-def combine(earlier, latter):
-    return (earlier[0] * latter[0], latter[0][:, None, None] * earlier[1] + latter[1])
 
 
 def matmul(left, right):
@@ -113,7 +195,10 @@
     device_place = lax.axis_index("seq") * lax.axis_size("tp") + lax.axis_index("tp")
     first_token = device_place * tok_count
     position = (first_token + jnp.arange(tok_count, dtype=jnp.int32)) % seq_length
-    is_start = first_token % seq_length == 0
+    span = seq_length // tok_count
+    members = lax.axis_size("tp")
+    ring = bits_of(members)
+    order = ring[1:] + ring[:1]
     decay_rate = jnp.exp2(-decay_exponent.astype(FLOAT))
     cosine, sine = angles(position, head_dim // 2)
     offsets = jnp.arange(BLOCK, dtype=FLOAT)
@@ -126,7 +211,7 @@
     query_decay = jnp.exp2(-(offsets + 1.0)[:, None] * decay_rate[None, :])[:, :, None]
     key_decay = jnp.exp2(-(BLOCK - 1.0 - offsets)[:, None] * decay_rate[None, :])[:, :, None]
     block_decay = jnp.exp2(-BLOCK * decay_rate)[:, None, None]
-    device_decay = jnp.where(is_start, 0.0, jnp.exp2(-tok_count * decay_rate))
+    device_decay = jnp.exp2(-tok_count * decay_rate)
     blocks = tok_count // BLOCK
     inputs = tokens.astype(FLOAT)
     normed = srms(inputs).astype(BHALF)
@@ -151,9 +236,7 @@
         )
         key_states.append(contrib)
         local_state = block_decay * local_state + contrib
-    identity = (jnp.ones_like(device_decay), jnp.zeros_like(local_state))
-    carried = prefix((device_decay, local_state), ("seq", "tp"), combine, identity, False)
-    state = jnp.where(is_start, 0.0, carried[1])
+    state = decayed_scan(local_state, device_decay, span, device_place, False)
     pieces = []
     used_states = []
     for number in range(blocks):
@@ -174,38 +257,32 @@
     gated = (normed_out * modulate).astype(BHALF)
     resid = inputs + matmul(gated, output_weight)
     normed_two = srms(resid).astype(BHALF)
-    gathered = lax.all_gather(normed_two, "tp", axis=0, tiled=True)
+    gathered = jnp.concatenate(gather_group(normed_two, order), axis=0)
     gate_pre = matmul(gathered, gate_weight)
     linear_pre = matmul(gathered, linear_weight)
     hidden = (gate_pre * linear_pre).astype(BHALF)
-    feed = lax.psum_scatter(
-        matmul(hidden, down_weight).astype(jnp.bfloat16), "tp", scatter_dimension=0, tiled=True
-    ).astype(jnp.float32)
+    feed = scatter_group(
+        matmul(hidden, down_weight).reshape(members, tok_count, width), list(reversed(order))
+    )
     mixed = (resid + feed).astype(BHALF)
-    cot_rows = lax.all_gather(cotangent, "tp", axis=0, tiled=True)
-    down_part = contract_rows(hidden, cot_rows)
+    cot_rows = jnp.concatenate(gather_group(cotangent, order), axis=0)
+    down_part = contract_rows(cot_rows, hidden)
     hidden_cot = contract_cols(cot_rows, down_weight)
     gate_back = (hidden_cot * linear_pre).astype(BHALF)
     linear_back = (hidden_cot * gate_pre).astype(BHALF)
     gate_part = contract_rows(gathered, gate_back)
     linear_part = contract_rows(gathered, linear_back)
-    normed_cot = lax.psum_scatter(
-        contract_cols(gate_back, gate_weight) + contract_cols(linear_back, linear_weight),
-        "tp",
-        scatter_dimension=0,
-        tiled=True,
-    )
+    normed_parts = contract_cols(gate_back, gate_weight) + contract_cols(linear_back, linear_weight)
+    normed_cot = scatter_group(
+        normed_parts.reshape(members, tok_count, width), list(reversed(order))
+    )
+    spread = [members * mask for mask in bits_of(lax.axis_size("seq"))]
+    spread = list(reversed(spread))
     gate_grad, linear_grad, down_grad = (
-        lax.psum_scatter(
-            gate_part.astype(jnp.bfloat16), "seq", scatter_dimension=0, tiled=True
-        ).astype(jnp.float32),
-        lax.psum_scatter(
-            linear_part.astype(jnp.bfloat16), "seq", scatter_dimension=0, tiled=True
-        ).astype(jnp.float32),
-        lax.psum_scatter(
-            down_part.astype(jnp.bfloat16), "seq", scatter_dimension=1, tiled=True
-        ).astype(jnp.float32),
-    )
+        halve(part.astype(BHALF), spread, device_place).astype(FLOAT)
+        for part in (gate_part, linear_part, down_part)
+    )
+    down_grad = down_grad.T
     resid_cot = cotangent.astype(FLOAT) + srms_back(resid, normed_cot)
     branch_back = resid_cot.astype(BHALF)
     output_part = contract_rows(gated, branch_back)
@@ -228,9 +305,7 @@
     inbound = jnp.zeros_like(local_state)
     for number in reversed(range(blocks)):
         inbound = block_decay * inbound + direct[number]
-    masked = jnp.where(is_start, 0.0, inbound)
-    after = prefix((device_decay, masked), ("seq", "tp"), combine, identity, True)
-    outer = after[1]
+    outer = decayed_scan(inbound, device_decay, span, device_place, True)
     accum = jnp.zeros_like(local_state)
     query_parts = []
     key_parts = []
@@ -245,11 +320,11 @@
         block_value = values[window]
         block_back = attended_back[window]
         key_part = (
-            jnp.einsum("hde,jhe->jhd", state_cot, block_value.astype(FLOAT), precision=HIGH)
+            jnp.einsum("hde,jhe->jhd", state_cot.astype(BHALF), block_value, preferred_element_type=FLOAT)
             * key_decay
         )
         value_part = jnp.einsum(
-            "jhd,hde->jhe", decayed_keys[number].astype(FLOAT), state_cot, precision=HIGH
+            "jhd,hde->jhe", decayed_keys[number], state_cot.astype(BHALF), preferred_element_type=FLOAT
         )
         scores = jnp.einsum("ihd,jhd->hij", block_query, block_key, preferred_element_type=FLOAT)
         probs = (scores * decay_matrix).astype(BHALF)
@@ -289,15 +364,22 @@
         + contract_cols(modulate_back, modulate_weight)
     )
     tokens_grad = resid_cot + srms_back(inputs, normed_grad)
-    query_grad, key_grad, value_grad, modulate_grad, output_grad = lax.psum(
-        (
+    everyone = bits_of(devices)
+    rest = everyone[1:]
+    across = members // 2
+    lines = [[m for m in rest if m < members], [m for m in rest if members <= m < members * across],
+             [m for m in rest if m >= members * across]]
+    def turn(k):
+        return [1] + [m for i in range(3) for m in lines[(i + k) % 3]]
+    query_grad, key_grad, value_grad, modulate_grad, output_grad = (
+        all_reduce(part.astype(BHALF), turn(k), device_place)
+        for k, part in enumerate((
             contract_rows(normed, query_back),
             contract_rows(normed, key_back),
             contract_rows(normed, value_back),
             contract_rows(normed, modulate_back),
             output_part,
-        ),
-        ("seq", "tp"),
+        ))
     )
     return (
         mixed,

time: 1160 us -> 580 us (0.50)
  waiting for transfers between devices: 829 us -> 157 us
  starting transfers between devices: 1.27 us -> 94.6 us
  local copies, waits for them, and re-layouts: 54.8 us -> 106 us
  blocking collectives: 42.3 us -> 0 us
  other arithmetic: 70 us -> 94.9 us
  matrix products: 132 us -> 115 us
  between operations: 15.3 us -> 3.05 us
    psum x1 -> x0, waiting for transfers between devices: 328 us -> none  [shards(): lax.psum((contract_rows(normed, query_back), contract_rows(normed, key_ba...]
    all_gather x4 -> x0, waiting for transfers between devices: 256 us -> none  [the longest x2 138 us: prefix(): gathered = jax.tree.map(lambda a: lax.all_gather(a, axis), part)]
    ppermute x0 -> x83, waiting for transfers between devices: none -> 157 us  [swap(): return lax.ppermute(value, axes, [(s, s ^ mask) for s in range(count)])]
    unnamed x13 -> x0, waiting for transfers between devices: 137 us -> none
    reduce_scatter x2 -> x0, waiting for transfers between devices: 108 us -> none  [the longest x1 63.4 us: shards(): lax.psum_scatter(contract_cols(gate_back, gate_weight) + contract_cols(li...]
    ppermute x0 -> x83, starting transfers between devices: none -> 94.6 us  [swap(): return lax.ppermute(value, axes, [(s, s ^ mask) for s in range(count)])]
    convert_element_type x3 -> x51, other arithmetic: 2.31 us -> 47.9 us  [the longest x31 18.4 us: halve(): (keep.astype(FLOAT) + swap(send.astype(BHALF), mask).astype(FLOAT)).astyp...]
    unnamed x1 -> x0, blocking collectives: 42.3 us -> none
  transfers between devices with their start and end apart: 10 -> 83, of which waited for: 10 -> 32; matrix products, arithmetic and copies ran while one was open for 13% -> 37% of each run, Pallas kernels for 0% -> 0%
where the time goes in v1:
time: 580 us; the launch traced here: 571 us
  waiting for transfers between devices  157 us (27%)
  matrix products  115 us (20%)
  local copies, waits for them, and re-layouts  106 us (18%)
  other arithmetic  94.9 us (16%)
  starting transfers between devices  94.6 us (16%)
    ppermute x83, waiting for transfers between devices, swap(): return lax.ppermute(value, axes, [(s, s ^ mask) for s in range(count)])  157 us
    ppermute x83, starting transfers between devices, swap(): return lax.ppermute(value, axes, [(s, s ^ mask) for s in range(count)])  94.6 us
    dot_general x8, matrix products, matmul(): return jnp.dot(left, right, preferred_element_type=FLOAT)  32.6 us
    dynamic_slice x6, local copies, waits for them, and re-layouts, halve(): keep = lax.dynamic_index_in_dim(halves, bit, 0, False)  29.7 us
    reshape x9, local copies, waits for them, and re-layouts, halve(): halves = value.reshape((2, value.shape[0] // 2) + value.shape[1:])  28.6 us
    dot_general x8, matrix products, contract_cols(): lax.dot_general(left, right, (((1,), (1,)), ((), ())), preferred_element_...  27.8 us
    dot_general x8, matrix products, contract_rows(): lax.dot_general(left, right, (((0,), (0,)), ((), ())), preferred_element_...  26.7 us
    unnamed x213, local copies, waits for them, and re-layouts  26 us
  transfers between devices with their start and end apart: 83, of which 32 were waited for; matrix products, arithmetic and copies ran while one was open for 37% of the time, Pallas kernels for 0%

profile of v1, /device:TPU:1, one launch (start us, length us, event | category | flops | bytes accessed | tf_op | source)
XLA Modules:
  0.0 571.1 jit_solution(11579613344272105594)
XLA Ops:
  2.4 3.2 fusion.153
  14.1 2.9 convolution_convert_fusion.8
  18.1 4.8 fusion.167
  24.0 3.0 subtract_convert_fusion
  31.5 2.7 collective-permute-start.13
  37.6 3.0 fusion.47
  40.6 20.1 %collective-permute-done.1 = bf16[4,128,128]{2,1,0:T(8,128)(2,1)S(1)} collective-permute-done((bf16[4,128,128]{2,1,0:T(8,128)(2,1)S(1)}, bf16[4,128,128]{2,1,0:T(8,128)(2,1)S(1)}, u32[]{:S(2)}, u32[]{:S(2)}) %collective-permute-start.1) | collective-permute-done | bytes 131104 | tf_op jit(solution)/shard_map/ppermute | solution.py:24
  69.8 2.8 fusion.53
  76.8 2.9 multiply_convert_fusion.8
  83.0 3.8 collective-permute-start.5
  86.8 2.8 fusion.48
  96.1 2.9 copy.131
  98.9 4.8 multiply_convert_fusion.7
  109.7 23.0 %collective-permute-done.7 = bf16[512,1024]{1,0:T(8,128)(2,1)} collective-permute-done((bf16[512,1024]{1,0:T(8,128)(2,1)}, bf16[512,1024]{1,0:T(8,128)(2,1)}, u32[]{:S(2)}, u32[]{:S(2)}) %collective-permute-start.7) | collective-permute-done | bytes 1048608 | tf_op jit(solution)/shard_map/ppermute | solution.py:24
  138.9 6.1 %fusion.156 = f32[2048,704]{0,1:T(8,128)S(1)} fusion(bf16[1024,704]{0,1:T(8,128)(2,1)S(1)} %copy-done.64, bf16[512,1024]{1,0:T(8,128)(2,1)} %collective-permute-done.8, bf16[512,1024]{1,0:T(8,128)(2,1)} %collective-permute-done.7, bf16[512,1024]{1,0:T(8,128)(2,1)} %collective-permute-done.6, bf16[512,1024]{1,0:T(8,128)(2,1)} %multiply_convert_fusion.10), kind=kOutput, calls=%fused_computation.476 | convolution fusion | flops 2969567232 | bytes 11403264 | tf_op jit(solution)/shard_map/dot_general | solution.py:166
  145.0 6.5 %fusion.157 = f32[2048,704]{0,1:T(8,128)S(1)} fusion(bf16[1024,704]{0,1:T(8,128)(2,1)S(1)} %copy-done.96, bf16[512,1024]{1,0:T(8,128)(2,1)} %collective-permute-done.8, bf16[512,1024]{1,0:T(8,128)(2,1)} %collective-permute-done.7, bf16[512,1024]{1,0:T(8,128)(2,1)} %collective-permute-done.6, bf16[512,1024]{1,0:T(8,128)(2,1)} %multiply_convert_fusion.10), kind=kOutput, calls=%fused_computation.477 | convolution fusion | flops 2969567232 | bytes 11403264 | tf_op jit(solution)/shard_map/dot_general | solution.py:166
  151.5 6.8 %multiply_convert_fusion = (bf16[2048,704]{0,1:T(8,128)(2,1)}, bf16[2048,704]{0,1:T(8,128)(2,1)S(1)}, bf16[2048,704]{0,1:T(8,128)(2,1)}) fusion(f32[2048,704]{0,1:T(8,128)S(1)} %fusion.157, f32[2048,704]{0,1:T(8,128)S(1)} %fusion.156, bf16[2048,1024]{1,0:T(8,128)(2,1)S(1)} %constant_dynamic-update-slice_fusion, bf16[704,1024]{1,0:T(8,128)(2,1)} %param.19), kind=kOutput, calls=%fused_computation | convolution fusion | flops 2961440768 | bytes 25821184 | tf_op jit(solution)/shard_map/dot_general | solution.py:174
  158.3 4.3 convolution_convert_fusion.5
  162.5 6.5 %fusion.171 = (bf16[2048,1024]{1,0:T(8,128)(2,1)}, f32[2048,1024]{1,0:T(8,128)}) fusion(bf16[2048,704]{0,1:T(8,128)(2,1)S(1)} %get-tuple-element.25, bf16[704,1024]{1,0:T(8,128)(2,1)S(1)} %copy-done.63), kind=kOutput, calls=%fused_computation.486 | convolution fusion | flops 2954887168 | bytes 16908288 | tf_op jit(solution)/shard_map/dot_general | solution.py:166
  169.0 4.9 reshape.559
  173.9 6.1 %constant_dynamic-slice_fusion.4 = (bf16[1,512,704]{1,0,2:T(2,128)(2,1)}, bf16[1,512,704]{1,0,2:T(2,128)(2,1)S(1)}) fusion(bf16[2,512,704]{1,0,2:T(2,128)(2,1)} %reshape.559, s32[]{:T(128)S(6)} %select_n.849, s32[]{:T(128)S(6)} %select_n.850), kind=kLoop, calls=%fused_computation.418 | loop fusion | bytes 2883592 | tf_op jit(solution)/shard_map/jit(dynamic_index_in_dim)/dynamic_slice | solution.py:39
  182.1 6.4 %convolution_convert_fusion.6 = bf16[1024,704]{0,1:T(8,128)(2,1)} fusion(bf16[2048,704]{0,1:T(8,128)(2,1)S(1)} %copy-done.2, bf16[512,1024]{1,0:T(8,128)(2,1)} %collective-permute-done.8, bf16[512,1024]{1,0:T(8,128)(2,1)} %collective-permute-done.7, bf16[512,1024]{1,0:T(8,128)(2,1)} %collective-permute-done.6, bf16[512,1024]{1,0:T(8,128)(2,1)} %multiply_convert_fusion.10), kind=kOutput, calls=%fused_computation.85 | convolution fusion | flops 2970288128 | bytes 8519680 | tf_op jit(solution)/shard_map/dot_general | solution.py:170
  188.5 4.7 reshape.556
  193.2 6.0 %constant_dynamic-slice_fusion.9 = (bf16[1,512,704]{1,0,2:T(2,128)(2,1)}, bf16[1,512,704]{1,0,2:T(2,128)(2,1)S(1)}) fusion(bf16[2,512,704]{1,0,2:T(2,128)(2,1)} %reshape.556, s32[]{:T(128)S(6)} %select_n.849, s32[]{:T(128)S(6)} %select_n.850), kind=kLoop, calls=%fused_computation.423 | loop fusion | bytes 2883592 | tf_op jit(solution)/shard_map/jit(dynamic_index_in_dim)/dynamic_slice | solution.py:39
  201.6 5.9 %fusion.172 = f32[2048,1024]{1,0:T(8,128)} fusion(bf16[2048,704]{0,1:T(8,128)(2,1)S(1)} %copy-done.11, bf16[1024,704]{0,1:T(8,128)(2,1)S(1)} %copy-done.97), kind=kOutput, calls=%fused_computation.487 | convolution fusion | flops 2952790016 | bytes 12713984 | tf_op jit(solution)/shard_map/dot_general | solution.py:174
  207.6 6.4 %convolution_convert_fusion.7 = bf16[1024,704]{0,1:T(8,128)(2,1)} fusion(bf16[2048,704]{0,1:T(8,128)(2,1)S(1)} %copy-done.11, bf16[512,1024]{1,0:T(8,128)(2,1)} %collective-permute-done.8, bf16[512,1024]{1,0:T(8,128)(2,1)} %collective-permute-done.7, bf16[512,1024]{1,0:T(8,128)(2,1)} %collective-permute-done.6, bf16[512,1024]{1,0:T(8,128)(2,1)} %multiply_convert_fusion.10), kind=kOutput, calls=%fused_computation.86 | convolution fusion | flops 2970288128 | bytes 8519680 | tf_op jit(solution)/shard_map/dot_general | solution.py:170
  214.0 4.7 reshape.553
  218.7 6.0 %constant_dynamic-slice_fusion.14 = (bf16[1,512,704]{1,0,2:T(2,128)(2,1)}, bf16[1,512,704]{1,0,2:T(2,128)(2,1)S(1)}) fusion(bf16[2,512,704]{1,0,2:T(2,128)(2,1)} %reshape.553, s32[]{:T(128)S(6)} %select_n.849, s32[]{:T(128)S(6)} %select_n.850), kind=kLoop, calls=%fused_computation.428 | loop fusion | bytes 2883592 | tf_op jit(solution)/shard_map/jit(dynamic_index_in_dim)/dynamic_slice | solution.py:39
  226.9 3.2 fusion.166
  230.9 7.2 %fusion.170 = (bf16[2048,1024]{1,0:T(8,128)(2,1)S(1)}, f32[2048,1024]{1,0:T(8,128)}) fusion(f32[2048,1024]{1,0:T(8,128)S(1)} %copy-done.5, bf16[2048,704]{0,1:T(8,128)(2,1)S(1)} %copy-done.3, bf16[1024,704]{0,1:T(8,128)(2,1)} %param.18), kind=kOutput, calls=%fused_computation.485 | convolution fusion | flops 2956984320 | bytes 25296896 | tf_op jit(solution)/shard_map/dot_general | solution.py:174
  239.7 7.8 %collective-permute-start.15 = (bf16[512,1024]{1,0:T(8,128)(2,1)}, bf16[512,1024]{1,0:T(8,128)(2,1)}, u32[]{:S(2)}, u32[]{:S(2)}) collective-permute-start(bf16[512,1024]{1,0:T(8,128)(2,1)} %get-tuple-element.32), channel_id=1, source_target_pairs={{0,1},{1,0},{2,3},{3,2},{4,5},{5,4},{6,7},{7,6},{8,9},{9,8},{10,11... | collective-permute-start | bytes 3145736 | tf_op jit(solution)/shard_map/ppermute | solution.py:24
  249.8 3.2 reshape.560
  252.9 3.8 constant_dynamic-slice_fusion.2
  257.6 4.2 collective-permute-done.77
  265.2 2.8 reshape.557
  268.0 3.8 constant_dynamic-slice_fusion.7
  272.6 4.6 collective-permute-done.74
  279.5 2.9 reshape.554
  282.4 3.9 constant_dynamic-slice_fusion.12
  288.6 3.2 fusion.12
  291.7 3.2 fusion.10
  299.9 2.6 constant_dynamic-slice_fusion
  319.1 3.0 collective-permute-done.79
  323.0 3.8 collective-permute-done.76
  327.6 13.4 %collective-permute-done.17 = bf16[512,1024]{1,0:T(8,128)(2,1)} collective-permute-done((bf16[512,1024]{1,0:T(8,128)(2,1)}, bf16[512,1024]{1,0:T(8,128)(2,1)}, u32[]{:S(2)}, u32[]{:S(2)}) %collective-permute-start.17) | collective-permute-done | bytes 1048608 | tf_op jit(solution)/shard_map/ppermute | solution.py:24
  341.1 2.8 multiply_reduce_fusion.1
  343.9 5.9 %multiply_add_fusion.2 = (f32[512,1024]{1,0:T(8,128)S(1)}, bf16[512,1024]{1,0:T(8,128)(2,1)}) fusion(bf16[512,1024]{1,0:T(8,128)(2,1)} %param.20, f32[512,1024]{1,0:T(8,128)S(1)} %copy-done.9, f32[512]{0:T(512)S(1)} %broadcast_multiply_fusion.2, f32[512]{0:T(512)S(1)} %add_rsqrt_fusion, bf16[512,1024]{1,0:T(8,128)(2,1)} %collective-permute-done.17, ...), kind=kLoop, calls=%fused_computation.62 | loop fusion | flops 8388608 | bytes 14684160 | tf_op jit(solution)/shard_map/add | solution.py:286
  349.8 2.6 convolution_convert_fusion
  359.5 2.8 convolution_add_fusion.6
  362.3 3.3 multiply_convert_fusion.4
  368.9 2.7 convolution_convert_fusion.1
  380.5 2.9 collective-permute-done.19
  389.2 2.7 collective-permute-start.54
  394.9 3.4 collective-permute-done.22
  398.6 4.6 collective-permute-start.23
  433.1 7.5 %collective-permute-done.65 = bf16[256,1024]{1,0:T(8,128)(2,1)S(1)} collective-permute-done((bf16[256,1024]{1,0:T(8,128)(2,1)S(1)}, bf16[256,1024]{1,0:T(8,128)(2,1)S(1)}, u32[]{:S(2)}, u32[]{:S(2)}) %collective-permute-start.65) | collective-permute-done | bytes 524320 | tf_op jit(solution)/shard_map/ppermute | solution.py:24
  444.2 3.5 collective-permute-done.66
  457.3 8.9 %collective-permute-done.68 = bf16[32,1024]{1,0:T(8,128)(2,1)S(1)} collective-permute-done((bf16[32,1024]{1,0:T(8,128)(2,1)S(1)}, bf16[32,1024]{1,0:T(8,128)(2,1)S(1)}, u32[]{:S(2)}, u32[]{:S(2)}) %collective-permute-start.68) | collective-permute-done | bytes 65568 | tf_op jit(solution)/shard_map/ppermute | solution.py:24
  473.1 4.8 collective-permute-done.70
  483.2 6.1 %collective-permute-done.71 = bf16[128,1024]{1,0:T(8,128)(2,1)S(1)} collective-permute-done((bf16[128,1024]{1,0:T(8,128)(2,1)S(1)}, bf16[128,1024]{1,0:T(8,128)(2,1)S(1)}, u32[]{:S(2)}, u32[]{:S(2)}) %collective-permute-start.71) | collective-permute-done | bytes 262176 | tf_op jit(solution)/shard_map/ppermute | solution.py:24
  495.4 7.4 %collective-permute-done.47 = bf16[64,1024]{1,0:T(8,128)(2,1)S(1)} collective-permute-done((bf16[64,1024]{1,0:T(8,128)(2,1)S(1)}, bf16[64,1024]{1,0:T(8,128)(2,1)S(1)}, u32[]{:S(2)}, u32[]{:S(2)}) %collective-permute-start.47) | collective-permute-done | bytes 131104 | tf_op jit(solution)/shard_map/ppermute | solution.py:24
  515.0 9.6 %collective-permute-start.73 = (bf16[512,1024]{1,0:T(8,128)(2,1)S(1)}, bf16[512,1024]{1,0:T(8,128)(2,1)S(1)}, u32[]{:S(2)}, u32[]{:S(2)}) collective-permute-start(bf16[512,1024]{1,0:T(8,128)(2,1)S(1)} %pad_maximum_fusion.9), channel_id=1, source_target_pairs={{0,1},{1,0},{2,3},{3,2},{4,5},{5,4},{6,7},{7,6},{8,9},{9,8},{10,11... | collective-permute-start | bytes 3145736 | tf_op jit(solution)/shard_map/ppermute | solution.py:24
  528.2 10.9 %collective-permute-done.51 = bf16[128,1024]{1,0:T(8,128)(2,1)S(1)} collective-permute-done((bf16[128,1024]{1,0:T(8,128)(2,1)S(1)}, bf16[128,1024]{1,0:T(8,128)(2,1)S(1)}, u32[]{:S(2)}, u32[]{:S(2)}) %collective-permute-start.51) | collective-permute-done | bytes 262176 | tf_op jit(solution)/shard_map/ppermute | solution.py:24
  541.2 10.3 %collective-permute-done.52 = bf16[256,1024]{1,0:T(8,128)(2,1)S(1)} collective-permute-done((bf16[256,1024]{1,0:T(8,128)(2,1)S(1)}, bf16[256,1024]{1,0:T(8,128)(2,1)S(1)}, u32[]{:S(2)}, u32[]{:S(2)}) %collective-permute-start.52) | collective-permute-done | bytes 524320 | tf_op jit(solution)/shard_map/ppermute | solution.py:24
  (550 shorter events, 224.4 us)
Async XLA Ops:
  31.5 77.7 %collective-permute-start.13 = (bf16[512,1024]{1,0:T(8,128)(2,1)}, bf16[512,1024]{1,0:T(8,128)(2,1)}, u32[]{:S(2)}, u32[]{:S(2)}) collective-permute-start(bf16[512,1024]{1,0:T(8,128)(2,1)} %param.20), channel_id=1, source_target_pairs={{0,2},{1,3},{2,0},{3,1},{4,6},{5,7},{6,4},{7,5},{8,10},{9,11},{10,... | collective-permute-start | bytes 3145736 | tf_op jit(solution)/shard_map/ppermute | solution.py:24
  37.5 23.1 %collective-permute-start.1 = (bf16[4,128,128]{2,1,0:T(8,128)(2,1)S(1)}, bf16[4,128,128]{2,1,0:T(8,128)(2,1)S(1)}, u32[]{:S(2)}, u32[]{:S(2)}) collective-permute-start(bf16[4,128,128]{2,1,0:T(8,128)(2,1)S(1)} %fusion.132), channel_id=1, source_target_pairs={{0,2},{1,3},{2,0},{3,1},{4,6},{5,7},{6,4},{7,5},{8,10},{9,11},{10,... | collective-permute-start | bytes 393224 | tf_op jit(solution)/shard_map/ppermute | solution.py:24
  74.6 6.3 %collective-permute-start.4 = (bf16[4,128,128]{2,1,0:T(8,128)(2,1)}, bf16[4,128,128]{2,1,0:T(8,128)(2,1)S(1)}, u32[]{:S(2)}, u32[]{:S(2)}) collective-permute-start(bf16[4,128,128]{2,1,0:T(8,128)(2,1)} %fusion.95), channel_id=1, source_target_pairs={{0,16},{1,17},{2,18},{3,19},{4,20},{5,21},{6,22},{7,23},{8,24},{9,... | collective-permute-start | bytes 393224 | tf_op jit(solution)/shard_map/ppermute | solution.py:24
  83.0 6.7 %collective-permute-start.5 = (bf16[4,128,128]{2,1,0:T(8,128)(2,1)}, bf16[4,128,128]{2,1,0:T(8,128)(2,1)S(1)}, u32[]{:S(2)}, u32[]{:S(2)}) collective-permute-start(bf16[4,128,128]{2,1,0:T(8,128)(2,1)} %get-tuple-element.18), channel_id=1, source_target_pairs={{0,1},{1,0},{2,3},{3,2},{4,5},{5,4},{6,7},{7,6},{8,9},{9,8},{10,11... | collective-permute-start | bytes 393224 | tf_op jit(solution)/shard_map/ppermute | solution.py:24
  107.6 25.1 %collective-permute-start.7 = (bf16[512,1024]{1,0:T(8,128)(2,1)}, bf16[512,1024]{1,0:T(8,128)(2,1)}, u32[]{:S(2)}, u32[]{:S(2)}) collective-permute-start(bf16[512,1024]{1,0:T(8,128)(2,1)} %multiply_convert_fusion.10), channel_id=1, source_target_pairs={{0,2},{1,3},{2,0},{3,1},{4,6},{5,7},{6,4},{7,5},{8,10},{9,11},{10,... | collective-permute-start | bytes 3145736 | tf_op jit(solution)/shard_map/ppermute | solution.py:24
  108.9 25.9 %collective-permute-start.12 = (bf16[512,1024]{1,0:T(8,128)(2,1)}, bf16[512,1024]{1,0:T(8,128)(2,1)}, u32[]{:S(2)}, u32[]{:S(2)}) collective-permute-start(bf16[512,1024]{1,0:T(8,128)(2,1)} %param.20), channel_id=1, source_target_pairs={{0,1},{1,0},{2,3},{3,2},{4,5},{5,4},{6,7},{7,6},{8,9},{9,8},{10,11... | collective-permute-start | bytes 3145736 | tf_op jit(solution)/shard_map/ppermute | solution.py:24
  109.2 28.3 %collective-permute-start.14 = (bf16[512,1024]{1,0:T(8,128)(2,1)}, bf16[512,1024]{1,0:T(8,128)(2,1)}, u32[]{:S(2)}, u32[]{:S(2)}) collective-permute-start(bf16[512,1024]{1,0:T(8,128)(2,1)} %collective-permute-done.13), channel_id=1, source_target_pairs={{0,1},{1,0},{2,3},{3,2},{4,5},{5,4},{6,7},{7,6},{8,9},{9,8},{10,11... | collective-permute-start | bytes 3145736 | tf_op jit(solution)/shard_map/ppermute | solution.py:24
  109.4 29.4 %collective-permute-start.6 = (bf16[512,1024]{1,0:T(8,128)(2,1)}, bf16[512,1024]{1,0:T(8,128)(2,1)}, u32[]{:S(2)}, u32[]{:S(2)}) collective-permute-start(bf16[512,1024]{1,0:T(8,128)(2,1)} %multiply_convert_fusion.10), channel_id=1, source_target_pairs={{0,1},{1,0},{2,3},{3,2},{4,5},{5,4},{6,7},{7,6},{8,9},{9,8},{10,11... | collective-permute-start | bytes 3145736 | tf_op jit(solution)/shard_map/ppermute | solution.py:24
  181.0 58.7 %collective-permute-start.80 = (bf16[512,704]{0,1:T(8,128)(2,1)}, bf16[512,704]{0,1:T(8,128)(2,1)}, u32[]{:S(2)}, u32[]{:S(2)}) collective-permute-start(bf16[512,704]{0,1:T(8,128)(2,1)} %bitcast.414), channel_id=1, source_target_pairs={{0,16},{1,17},{2,18},{3,19},{4,20},{5,21},{6,22},{7,23},{8,24},{9,... | collective-permute-start | bytes 2162696 | tf_op jit(solution)/shard_map/ppermute | solution.py:24
  200.4 61.4 %collective-permute-start.77 = (bf16[512,704]{0,1:T(8,128)(2,1)}, bf16[512,704]{0,1:T(8,128)(2,1)}, u32[]{:S(2)}, u32[]{:S(2)}) collective-permute-start(bf16[512,704]{0,1:T(8,128)(2,1)} %bitcast.415), channel_id=1, source_target_pairs={{0,16},{1,17},{2,18},{3,19},{4,20},{5,21},{6,22},{7,23},{8,24},{9,... | collective-permute-start | bytes 2162696 | tf_op jit(solution)/shard_map/ppermute | solution.py:24
  225.8 51.5 %collective-permute-start.74 = (bf16[512,704]{0,1:T(8,128)(2,1)}, bf16[512,704]{0,1:T(8,128)(2,1)}, u32[]{:S(2)}, u32[]{:S(2)}) collective-permute-start(bf16[512,704]{0,1:T(8,128)(2,1)} %bitcast.416), channel_id=1, source_target_pairs={{0,16},{1,17},{2,18},{3,19},{4,20},{5,21},{6,22},{7,23},{8,24},{9,... | collective-permute-start | bytes 2162696 | tf_op jit(solution)/shard_map/ppermute | solution.py:24
  230.1 57.0 %collective-permute-start.10 = (bf16[512,1024]{1,0:T(8,128)(2,1)}, bf16[512,1024]{1,0:T(8,128)(2,1)}, u32[]{:S(2)}, u32[]{:S(2)}) collective-permute-start(bf16[512,1024]{1,0:T(8,128)(2,1)} %get-tuple-element.35), channel_id=1, source_target_pairs={{0,1},{1,0},{2,3},{3,2},{4,5},{5,4},{6,7},{7,6},{8,9},{9,8},{10,11... | collective-permute-start | bytes 3145736 | tf_op jit(solution)/shard_map/ppermute | solution.py:24
  239.7 52.1 %collective-permute-start.16 = (bf16[512,1024]{1,0:T(8,128)(2,1)}, bf16[512,1024]{1,0:T(8,128)(2,1)}, u32[]{:S(2)}, u32[]{:S(2)}) collective-permute-start(bf16[512,1024]{1,0:T(8,128)(2,1)} %get-tuple-element.33), channel_id=1, source_target_pairs={{0,1},{1,0},{2,3},{3,2},{4,5},{5,4},{6,7},{7,6},{8,9},{9,8},{10,11... | collective-permute-start | bytes 3145736 | tf_op jit(solution)/shard_map/ppermute | solution.py:24
  239.7 87.9 %collective-permute-start.15 = (bf16[512,1024]{1,0:T(8,128)(2,1)}, bf16[512,1024]{1,0:T(8,128)(2,1)}, u32[]{:S(2)}, u32[]{:S(2)}) collective-permute-start(bf16[512,1024]{1,0:T(8,128)(2,1)} %get-tuple-element.32), channel_id=1, source_target_pairs={{0,1},{1,0},{2,3},{3,2},{4,5},{5,4},{6,7},{7,6},{8,9},{9,8},{10,11... | collective-permute-start | bytes 3145736 | tf_op jit(solution)/shard_map/ppermute | solution.py:24
  261.8 82.1 %collective-permute-start.9 = (bf16[512,1024]{1,0:T(8,128)(2,1)}, bf16[512,1024]{1,0:T(8,128)(2,1)}, u32[]{:S(2)}, u32[]{:S(2)}) collective-permute-start(bf16[512,1024]{1,0:T(8,128)(2,1)} %get-tuple-element.34), channel_id=1, source_target_pairs={{0,1},{1,0},{2,3},{3,2},{4,5},{5,4},{6,7},{7,6},{8,9},{9,8},{10,11... | collective-permute-start | bytes 3145736 | tf_op jit(solution)/shard_map/ppermute | solution.py:24
  277.2 17.8 %collective-permute-start.81 = (bf16[256,704]{0,1:T(8,128)(2,1)}, bf16[256,704]{0,1:T(8,128)(2,1)}, u32[]{:S(2)}, u32[]{:S(2)}) collective-permute-start(bf16[256,704]{0,1:T(8,128)(2,1)} %bitcast.417), channel_id=1, source_target_pairs={{0,8},{1,9},{2,10},{3,11},{4,12},{5,13},{6,14},{7,15},{8,0},{9,1},... | collective-permute-start | bytes 1081352 | tf_op jit(solution)/shard_map/ppermute | solution.py:24
  287.1 16.1 %collective-permute-start.78 = (bf16[256,704]{0,1:T(8,128)(2,1)}, bf16[256,704]{0,1:T(8,128)(2,1)}, u32[]{:S(2)}, u32[]{:S(2)}) collective-permute-start(bf16[256,704]{0,1:T(8,128)(2,1)} %bitcast.418), channel_id=1, source_target_pairs={{0,8},{1,9},{2,10},{3,11},{4,12},{5,13},{6,14},{7,15},{8,0},{9,1},... | collective-permute-start | bytes 1081352 | tf_op jit(solution)/shard_map/ppermute | solution.py:24
  291.7 13.5 %collective-permute-start.75 = (bf16[256,704]{0,1:T(8,128)(2,1)}, bf16[256,704]{0,1:T(8,128)(2,1)}, u32[]{:S(2)}, u32[]{:S(2)}) collective-permute-start(bf16[256,704]{0,1:T(8,128)(2,1)} %bitcast.419), channel_id=1, source_target_pairs={{0,8},{1,9},{2,10},{3,11},{4,12},{5,13},{6,14},{7,15},{8,0},{9,1},... | collective-permute-start | bytes 1081352 | tf_op jit(solution)/shard_map/ppermute | solution.py:24
  295.0 48.9 %collective-permute-start.11 = (bf16[512,1024]{1,0:T(8,128)(2,1)}, bf16[512,1024]{1,0:T(8,128)(2,1)}, u32[]{:S(2)}, u32[]{:S(2)}) collective-permute-start(bf16[512,1024]{1,0:T(8,128)(2,1)} %fusion.12), channel_id=1, source_target_pairs={{0,2},{1,3},{2,0},{3,1},{4,6},{5,7},{6,4},{7,5},{8,10},{9,11},{10,... | collective-permute-start | bytes 3145736 | tf_op jit(solution)/shard_map/ppermute | solution.py:24
  303.2 37.8 %collective-permute-start.17 = (bf16[512,1024]{1,0:T(8,128)(2,1)}, bf16[512,1024]{1,0:T(8,128)(2,1)}, u32[]{:S(2)}, u32[]{:S(2)}) collective-permute-start(bf16[512,1024]{1,0:T(8,128)(2,1)} %fusion.10), channel_id=1, source_target_pairs={{0,2},{1,3},{2,0},{3,1},{4,6},{5,7},{6,4},{7,5},{8,10},{9,11},{10,... | collective-permute-start | bytes 3145736 | tf_op jit(solution)/shard_map/ppermute | solution.py:24
  305.2 11.9 %collective-permute-start.82 = (bf16[128,704]{0,1:T(8,128)(2,1)}, bf16[128,704]{0,1:T(8,128)(2,1)}, u32[]{:S(2)}, u32[]{:S(2)}) collective-permute-start(bf16[128,704]{0,1:T(8,128)(2,1)} %bitcast.420), channel_id=1, source_target_pairs={{0,4},{1,5},{2,6},{3,7},{4,0},{5,1},{6,2},{7,3},{8,12},{9,13},{10,... | collective-permute-start | bytes 540680 | tf_op jit(solution)/shard_map/ppermute | solution.py:24
  366.6 58.6 %collective-permute-start.64 = (bf16[512,1024]{1,0:T(8,128)(2,1)}, bf16[512,1024]{1,0:T(8,128)(2,1)}, u32[]{:S(2)}, u32[]{:S(2)}) collective-permute-start(bf16[512,1024]{1,0:T(8,128)(2,1)} %dynamic-slice_bitcast_fusion), channel_id=1, source_target_pairs={{0,1},{1,0},{2,3},{3,2},{4,5},{5,4},{6,7},{7,6},{8,9},{9,8},{10,11... | collective-permute-start | bytes 3145736 | tf_op jit(solution)/shard_map/ppermute | solution.py:24
  389.2 39.2 %collective-permute-start.54 = (bf16[512,1024]{1,0:T(8,128)(2,1)S(1)}, bf16[512,1024]{1,0:T(8,128)(2,1)}, u32[]{:S(2)}, u32[]{:S(2)}) collective-permute-start(bf16[512,1024]{1,0:T(8,128)(2,1)S(1)} %dynamic-slice_bitcast_fusion.1), channel_id=1, source_target_pairs={{0,1},{1,0},{2,3},{3,2},{4,5},{5,4},{6,7},{7,6},{8,9},{9,8},{10,11... | collective-permute-start | bytes 3145736 | tf_op jit(solution)/shard_map/ppermute | solution.py:24
  392.1 6.2 %collective-permute-start.22 = (bf16[4,128,128]{2,1,0:T(8,128)(2,1)S(1)}, bf16[4,128,128]{2,1,0:T(8,128)(2,1)S(1)}, u32[]{:S(2)}, u32[]{:S(2)}) collective-permute-start(bf16[4,128,128]{2,1,0:T(8,128)(2,1)S(1)} %fusion.108), channel_id=1, source_target_pairs={{0,16},{1,17},{2,18},{3,19},{4,20},{5,21},{6,22},{7,23},{8,24},{9,... | collective-permute-start | bytes 393224 | tf_op jit(solution)/shard_map/ppermute | solution.py:24
  420.4 29.8 %collective-permute-start.44 = (bf16[512,1024]{1,0:T(8,128)(2,1)S(1)}, bf16[512,1024]{1,0:T(8,128)(2,1)S(1)}, u32[]{:S(2)}, u32[]{:S(2)}) collective-permute-start(bf16[512,1024]{1,0:T(8,128)(2,1)S(1)} %dynamic-slice_bitcast_fusion.2), channel_id=1, source_target_pairs={{0,1},{1,0},{2,3},{3,2},{4,5},{5,4},{6,7},{7,6},{8,9},{9,8},{10,11... | collective-permute-start | bytes 3145736 | tf_op jit(solution)/shard_map/ppermute | solution.py:24
  420.9 31.3 %collective-permute-start.34 = (bf16[512,1024]{1,0:T(8,128)(2,1)S(1)}, bf16[512,1024]{1,0:T(8,128)(2,1)S(1)}, u32[]{:S(2)}, u32[]{:S(2)}) collective-permute-start(bf16[512,1024]{1,0:T(8,128)(2,1)S(1)} %dynamic-slice_bitcast_fusion.3), channel_id=1, source_target_pairs={{0,1},{1,0},{2,3},{3,2},{4,5},{5,4},{6,7},{7,6},{8,9},{9,8},{10,11... | collective-permute-start | bytes 3145736 | tf_op jit(solution)/shard_map/ppermute | solution.py:24
  421.2 32.5 %collective-permute-start.24 = (bf16[512,1024]{1,0:T(8,128)(2,1)S(1)}, bf16[512,1024]{1,0:T(8,128)(2,1)S(1)}, u32[]{:S(2)}, u32[]{:S(2)}) collective-permute-start(bf16[512,1024]{1,0:T(8,128)(2,1)S(1)} %dynamic-slice_bitcast_fusion.4), channel_id=1, source_target_pairs={{0,1},{1,0},{2,3},{3,2},{4,5},{5,4},{6,7},{7,6},{8,9},{9,8},{10,11... | collective-permute-start | bytes 3145736 | tf_op jit(solution)/shard_map/ppermute | solution.py:24
  427.2 13.4 %collective-permute-start.65 = (bf16[256,1024]{1,0:T(8,128)(2,1)S(1)}, bf16[256,1024]{1,0:T(8,128)(2,1)S(1)}, u32[]{:S(2)}, u32[]{:S(2)}) collective-permute-start(bf16[256,1024]{1,0:T(8,128)(2,1)S(1)} %dynamic-slice_bitcast_fusion.5), channel_id=1, source_target_pairs={{0,4},{1,5},{2,6},{3,7},{4,0},{5,1},{6,2},{7,3},{8,12},{9,13},{10,... | collective-permute-start | bytes 1572872 | tf_op jit(solution)/shard_map/ppermute | solution.py:24
  430.1 13.1 %collective-permute-start.55 = (bf16[256,1024]{1,0:T(8,128)(2,1)S(1)}, bf16[256,1024]{1,0:T(8,128)(2,1)S(1)}, u32[]{:S(2)}, u32[]{:S(2)}) collective-permute-start(bf16[256,1024]{1,0:T(8,128)(2,1)S(1)} %dynamic-slice_bitcast_fusion.6), channel_id=1, source_target_pairs={{0,2},{1,3},{2,0},{3,1},{4,6},{5,7},{6,4},{7,5},{8,10},{9,11},{10,... | collective-permute-start | bytes 1572872 | tf_op jit(solution)/shard_map/ppermute | solution.py:24
  440.9 6.9 %collective-permute-start.66 = (bf16[128,1024]{1,0:T(8,128)(2,1)S(1)}, bf16[128,1024]{1,0:T(8,128)(2,1)S(1)}, u32[]{:S(2)}, u32[]{:S(2)}) collective-permute-start(bf16[128,1024]{1,0:T(8,128)(2,1)S(1)} %dynamic-slice_bitcast_fusion.10), channel_id=1, source_target_pairs={{0,8},{1,9},{2,10},{3,11},{4,12},{5,13},{6,14},{7,15},{8,0},{9,1},... | collective-permute-start | bytes 786440 | tf_op jit(solution)/shard_map/ppermute | solution.py:24
  443.4 6.6 %collective-permute-start.56 = (bf16[128,1024]{1,0:T(8,128)(2,1)S(1)}, bf16[128,1024]{1,0:T(8,128)(2,1)S(1)}, u32[]{:S(2)}, u32[]{:S(2)}) collective-permute-start(bf16[128,1024]{1,0:T(8,128)(2,1)S(1)} %dynamic-slice_bitcast_fusion.11), channel_id=1, source_target_pairs={{0,4},{1,5},{2,6},{3,7},{4,0},{5,1},{6,2},{7,3},{8,12},{9,13},{10,... | collective-permute-start | bytes 786440 | tf_op jit(solution)/shard_map/ppermute | solution.py:24
  447.9 8.3 %collective-permute-start.67 = (bf16[64,1024]{1,0:T(8,128)(2,1)S(1)}, bf16[64,1024]{1,0:T(8,128)(2,1)S(1)}, u32[]{:S(2)}, u32[]{:S(2)}) collective-permute-start(bf16[64,1024]{1,0:T(8,128)(2,1)S(1)} %dynamic-slice_bitcast_fusion.15), channel_id=1, source_target_pairs={{0,16},{1,17},{2,18},{3,19},{4,20},{5,21},{6,22},{7,23},{8,24},{9,... | collective-permute-start | bytes 393224 | tf_op jit(solution)/shard_map/ppermute | solution.py:24
  450.1 7.1 %collective-permute-start.57 = (bf16[64,1024]{1,0:T(8,128)(2,1)S(1)}, bf16[64,1024]{1,0:T(8,128)(2,1)S(1)}, u32[]{:S(2)}, u32[]{:S(2)}) collective-permute-start(bf16[64,1024]{1,0:T(8,128)(2,1)S(1)} %dynamic-slice_bitcast_fusion.16), channel_id=1, source_target_pairs={{0,8},{1,9},{2,10},{3,11},{4,12},{5,13},{6,14},{7,15},{8,0},{9,1},... | collective-permute-start | bytes 393224 | tf_op jit(solution)/shard_map/ppermute | solution.py:24
  450.7 28.3 %collective-permute-start.45 = (bf16[256,1024]{1,0:T(8,128)(2,1)S(1)}, bf16[256,1024]{1,0:T(8,128)(2,1)S(1)}, u32[]{:S(2)}, u32[]{:S(2)}) collective-permute-start(bf16[256,1024]{1,0:T(8,128)(2,1)S(1)} %dynamic-slice_bitcast_fusion.7), channel_id=1, source_target_pairs={{0,8},{1,9},{2,10},{3,11},{4,12},{5,13},{6,14},{7,15},{8,0},{9,1},... | collective-permute-start | bytes 1572872 | tf_op jit(solution)/shard_map/ppermute | solution.py:24
  452.6 28.3 %collective-permute-start.35 = (bf16[256,1024]{1,0:T(8,128)(2,1)S(1)}, bf16[256,1024]{1,0:T(8,128)(2,1)S(1)}, u32[]{:S(2)}, u32[]{:S(2)}) collective-permute-start(bf16[256,1024]{1,0:T(8,128)(2,1)S(1)} %dynamic-slice_bitcast_fusion.8), channel_id=1, source_target_pairs={{0,4},{1,5},{2,6},{3,7},{4,0},{5,1},{6,2},{7,3},{8,12},{9,13},{10,... | collective-permute-start | bytes 1572872 | tf_op jit(solution)/shard_map/ppermute | solution.py:24
  454.1 28.7 %collective-permute-start.25 = (bf16[256,1024]{1,0:T(8,128)(2,1)S(1)}, bf16[256,1024]{1,0:T(8,128)(2,1)S(1)}, u32[]{:S(2)}, u32[]{:S(2)}) collective-permute-start(bf16[256,1024]{1,0:T(8,128)(2,1)S(1)} %dynamic-slice_bitcast_fusion.9), channel_id=1, source_target_pairs={{0,2},{1,3},{2,0},{3,1},{4,6},{5,7},{6,4},{7,5},{8,10},{9,11},{10,... | collective-permute-start | bytes 1572872 | tf_op jit(solution)/shard_map/ppermute | solution.py:24
  456.2 10.0 %collective-permute-start.68 = (bf16[32,1024]{1,0:T(8,128)(2,1)S(1)}, bf16[32,1024]{1,0:T(8,128)(2,1)S(1)}, u32[]{:S(2)}, u32[]{:S(2)}) collective-permute-start(bf16[32,1024]{1,0:T(8,128)(2,1)S(1)} %dynamic-slice_bitcast_fusion.20), channel_id=1, source_target_pairs={{0,2},{1,3},{2,0},{3,1},{4,6},{5,7},{6,4},{7,5},{8,10},{9,11},{10,... | collective-permute-start | bytes 196616 | tf_op jit(solution)/shard_map/ppermute | solution.py:24
  457.2 9.9 %collective-permute-start.58 = (bf16[32,1024]{1,0:T(8,128)(2,1)S(1)}, bf16[32,1024]{1,0:T(8,128)(2,1)S(1)}, u32[]{:S(2)}, u32[]{:S(2)}) collective-permute-start(bf16[32,1024]{1,0:T(8,128)(2,1)S(1)} %dynamic-slice_bitcast_fusion.21), channel_id=1, source_target_pairs={{0,16},{1,17},{2,18},{3,19},{4,20},{5,21},{6,22},{7,23},{8,24},{9,... | collective-permute-start | bytes 196616 | tf_op jit(solution)/shard_map/ppermute | solution.py:24
  470.3 7.6 %collective-permute-start.70 = (bf16[64,1024]{1,0:T(8,128)(2,1)S(1)}, bf16[64,1024]{1,0:T(8,128)(2,1)S(1)}, u32[]{:S(2)}, u32[]{:S(2)}) collective-permute-start(bf16[64,1024]{1,0:T(8,128)(2,1)S(1)} %pad_maximum_fusion.28), channel_id=1, source_target_pairs={{0,16},{1,17},{2,18},{3,19},{4,20},{5,21},{6,22},{7,23},{8,24},{9,... | collective-permute-start | bytes 393224 | tf_op jit(solution)/shard_map/ppermute | solution.py:24
  471.4 6.6 %collective-permute-start.60 = (bf16[64,1024]{1,0:T(8,128)(2,1)S(1)}, bf16[64,1024]{1,0:T(8,128)(2,1)S(1)}, u32[]{:S(2)}, u32[]{:S(2)}) collective-permute-start(bf16[64,1024]{1,0:T(8,128)(2,1)S(1)} %pad_maximum_fusion.27), channel_id=1, source_target_pairs={{0,8},{1,9},{2,10},{3,11},{4,12},{5,13},{6,14},{7,15},{8,0},{9,1},... | collective-permute-start | bytes 393224 | tf_op jit(solution)/shard_map/ppermute | solution.py:24
  478.0 11.3 %collective-permute-start.71 = (bf16[128,1024]{1,0:T(8,128)(2,1)S(1)}, bf16[128,1024]{1,0:T(8,128)(2,1)S(1)}, u32[]{:S(2)}, u32[]{:S(2)}) collective-permute-start(bf16[128,1024]{1,0:T(8,128)(2,1)S(1)} %pad_maximum_fusion.23), channel_id=1, source_target_pairs={{0,8},{1,9},{2,10},{3,11},{4,12},{5,13},{6,14},{7,15},{8,0},{9,1},... | collective-permute-start | bytes 786440 | tf_op jit(solution)/shard_map/ppermute | solution.py:24
  478.1 12.6 %collective-permute-start.61 = (bf16[128,1024]{1,0:T(8,128)(2,1)S(1)}, bf16[128,1024]{1,0:T(8,128)(2,1)S(1)}, u32[]{:S(2)}, u32[]{:S(2)}) collective-permute-start(bf16[128,1024]{1,0:T(8,128)(2,1)S(1)} %pad_maximum_fusion.22), channel_id=1, source_target_pairs={{0,4},{1,5},{2,6},{3,7},{4,0},{5,1},{6,2},{7,3},{8,12},{9,13},{10,... | collective-permute-start | bytes 786440 | tf_op jit(solution)/shard_map/ppermute | solution.py:24
  479.2 13.0 %collective-permute-start.46 = (bf16[128,1024]{1,0:T(8,128)(2,1)S(1)}, bf16[128,1024]{1,0:T(8,128)(2,1)S(1)}, u32[]{:S(2)}, u32[]{:S(2)}) collective-permute-start(bf16[128,1024]{1,0:T(8,128)(2,1)S(1)} %dynamic-slice_bitcast_fusion.12), channel_id=1, source_target_pairs={{0,16},{1,17},{2,18},{3,19},{4,20},{5,21},{6,22},{7,23},{8,24},{9,... | collective-permute-start | bytes 786440 | tf_op jit(solution)/shard_map/ppermute | solution.py:24
  481.2 13.8 %collective-permute-start.36 = (bf16[128,1024]{1,0:T(8,128)(2,1)S(1)}, bf16[128,1024]{1,0:T(8,128)(2,1)S(1)}, u32[]{:S(2)}, u32[]{:S(2)}) collective-permute-start(bf16[128,1024]{1,0:T(8,128)(2,1)S(1)} %dynamic-slice_bitcast_fusion.13), channel_id=1, source_target_pairs={{0,8},{1,9},{2,10},{3,11},{4,12},{5,13},{6,14},{7,15},{8,0},{9,1},... | collective-permute-start | bytes 786440 | tf_op jit(solution)/shard_map/ppermute | solution.py:24
  483.1 12.1 %collective-permute-start.26 = (bf16[128,1024]{1,0:T(8,128)(2,1)S(1)}, bf16[128,1024]{1,0:T(8,128)(2,1)S(1)}, u32[]{:S(2)}, u32[]{:S(2)}) collective-permute-start(bf16[128,1024]{1,0:T(8,128)(2,1)S(1)} %dynamic-slice_bitcast_fusion.14), channel_id=1, source_target_pairs={{0,4},{1,5},{2,6},{3,7},{4,0},{5,1},{6,2},{7,3},{8,12},{9,13},{10,... | collective-permute-start | bytes 786440 | tf_op jit(solution)/shard_map/ppermute | solution.py:24
  489.5 25.2 %collective-permute-start.72 = (bf16[256,1024]{1,0:T(8,128)(2,1)S(1)}, bf16[256,1024]{1,0:T(8,128)(2,1)S(1)}, u32[]{:S(2)}, u32[]{:S(2)}) collective-permute-start(bf16[256,1024]{1,0:T(8,128)(2,1)S(1)} %pad_maximum_fusion.18), channel_id=1, source_target_pairs={{0,4},{1,5},{2,6},{3,7},{4,0},{5,1},{6,2},{7,3},{8,12},{9,13},{10,... | collective-permute-start | bytes 1572872 | tf_op jit(solution)/shard_map/ppermute | solution.py:24
  490.9 33.8 %collective-permute-start.62 = (bf16[256,1024]{1,0:T(8,128)(2,1)S(1)}, bf16[256,1024]{1,0:T(8,128)(2,1)S(1)}, u32[]{:S(2)}, u32[]{:S(2)}) collective-permute-start(bf16[256,1024]{1,0:T(8,128)(2,1)S(1)} %pad_maximum_fusion.17), channel_id=1, source_target_pairs={{0,2},{1,3},{2,0},{3,1},{4,6},{5,7},{6,4},{7,5},{8,10},{9,11},{10,... | collective-permute-start | bytes 1572872 | tf_op jit(solution)/shard_map/ppermute | solution.py:24
  492.4 10.5 %collective-permute-start.47 = (bf16[64,1024]{1,0:T(8,128)(2,1)S(1)}, bf16[64,1024]{1,0:T(8,128)(2,1)S(1)}, u32[]{:S(2)}, u32[]{:S(2)}) collective-permute-start(bf16[64,1024]{1,0:T(8,128)(2,1)S(1)} %dynamic-slice_bitcast_fusion.17), channel_id=1, source_target_pairs={{0,2},{1,3},{2,0},{3,1},{4,6},{5,7},{6,4},{7,5},{8,10},{9,11},{10,... | collective-permute-start | bytes 393224 | tf_op jit(solution)/shard_map/ppermute | solution.py:24
  495.1 7.8 %collective-permute-start.37 = (bf16[64,1024]{1,0:T(8,128)(2,1)S(1)}, bf16[64,1024]{1,0:T(8,128)(2,1)S(1)}, u32[]{:S(2)}, u32[]{:S(2)}) collective-permute-start(bf16[64,1024]{1,0:T(8,128)(2,1)S(1)} %dynamic-slice_bitcast_fusion.18), channel_id=1, source_target_pairs={{0,16},{1,17},{2,18},{3,19},{4,20},{5,21},{6,22},{7,23},{8,24},{9,... | collective-permute-start | bytes 393224 | tf_op jit(solution)/shard_map/ppermute | solution.py:24
  495.3 9.5 %collective-permute-start.27 = (bf16[64,1024]{1,0:T(8,128)(2,1)S(1)}, bf16[64,1024]{1,0:T(8,128)(2,1)S(1)}, u32[]{:S(2)}, u32[]{:S(2)}) collective-permute-start(bf16[64,1024]{1,0:T(8,128)(2,1)S(1)} %dynamic-slice_bitcast_fusion.19), channel_id=1, source_target_pairs={{0,8},{1,9},{2,10},{3,11},{4,12},{5,13},{6,14},{7,15},{8,0},{9,1},... | collective-permute-start | bytes 393224 | tf_op jit(solution)/shard_map/ppermute | solution.py:24
  510.6 14.5 %collective-permute-start.50 = (bf16[64,1024]{1,0:T(8,128)(2,1)S(1)}, bf16[64,1024]{1,0:T(8,128)(2,1)S(1)}, u32[]{:S(2)}, u32[]{:S(2)}) collective-permute-start(bf16[64,1024]{1,0:T(8,128)(2,1)S(1)} %pad_maximum_fusion.26), channel_id=1, source_target_pairs={{0,2},{1,3},{2,0},{3,1},{4,6},{5,7},{6,4},{7,5},{8,10},{9,11},{10,... | collective-permute-start | bytes 393224 | tf_op jit(solution)/shard_map/ppermute | solution.py:24
  512.0 15.4 %collective-permute-start.40 = (bf16[64,1024]{1,0:T(8,128)(2,1)S(1)}, bf16[64,1024]{1,0:T(8,128)(2,1)S(1)}, u32[]{:S(2)}, u32[]{:S(2)}) collective-permute-start(bf16[64,1024]{1,0:T(8,128)(2,1)S(1)} %pad_maximum_fusion.25), channel_id=1, source_target_pairs={{0,16},{1,17},{2,18},{3,19},{4,20},{5,21},{6,22},{7,23},{8,24},{9,... | collective-permute-start | bytes 393224 | tf_op jit(solution)/shard_map/ppermute | solution.py:24
  514.6 12.9 %collective-permute-start.30 = (bf16[64,1024]{1,0:T(8,128)(2,1)S(1)}, bf16[64,1024]{1,0:T(8,128)(2,1)S(1)}, u32[]{:S(2)}, u32[]{:S(2)}) collective-permute-start(bf16[64,1024]{1,0:T(8,128)(2,1)S(1)} %pad_maximum_fusion.24), channel_id=1, source_target_pairs={{0,8},{1,9},{2,10},{3,11},{4,12},{5,13},{6,14},{7,15},{8,0},{9,1},... | collective-permute-start | bytes 393224 | tf_op jit(solution)/shard_map/ppermute | solution.py:24
  515.0 40.4 %collective-permute-start.73 = (bf16[512,1024]{1,0:T(8,128)(2,1)S(1)}, bf16[512,1024]{1,0:T(8,128)(2,1)S(1)}, u32[]{:S(2)}, u32[]{:S(2)}) collective-permute-start(bf16[512,1024]{1,0:T(8,128)(2,1)S(1)} %pad_maximum_fusion.9), channel_id=1, source_target_pairs={{0,1},{1,0},{2,3},{3,2},{4,5},{5,4},{6,7},{7,6},{8,9},{9,8},{10,11... | collective-permute-start | bytes 3145736 | tf_op jit(solution)/shard_map/ppermute | solution.py:24
  525.0 33.5 %collective-permute-start.63 = (bf16[512,1024]{1,0:T(8,128)(2,1)S(1)}, bf16[512,1024]{1,0:T(8,128)(2,1)S(1)}, u32[]{:S(2)}, u32[]{:S(2)}) collective-permute-start(bf16[512,1024]{1,0:T(8,128)(2,1)S(1)} %pad_maximum_fusion.8), channel_id=1, source_target_pairs={{0,1},{1,0},{2,3},{3,2},{4,5},{5,4},{6,7},{7,6},{8,9},{9,8},{10,11... | collective-permute-start | bytes 3145736 | tf_op jit(solution)/shard_map/ppermute | solution.py:24
  525.2 14.0 %collective-permute-start.51 = (bf16[128,1024]{1,0:T(8,128)(2,1)S(1)}, bf16[128,1024]{1,0:T(8,128)(2,1)S(1)}, u32[]{:S(2)}, u32[]{:S(2)}) collective-permute-start(bf16[128,1024]{1,0:T(8,128)(2,1)S(1)} %pad_maximum_fusion.21), channel_id=1, source_target_pairs={{0,16},{1,17},{2,18},{3,19},{4,20},{5,21},{6,22},{7,23},{8,24},{9,... | collective-permute-start | bytes 786440 | tf_op jit(solution)/shard_map/ppermute | solution.py:24
  527.5 11.9 %collective-permute-start.41 = (bf16[128,1024]{1,0:T(8,128)(2,1)S(1)}, bf16[128,1024]{1,0:T(8,128)(2,1)S(1)}, u32[]{:S(2)}, u32[]{:S(2)}) collective-permute-start(bf16[128,1024]{1,0:T(8,128)(2,1)S(1)} %pad_maximum_fusion.20), channel_id=1, source_target_pairs={{0,8},{1,9},{2,10},{3,11},{4,12},{5,13},{6,14},{7,15},{8,0},{9,1},... | collective-permute-start | bytes 786440 | tf_op jit(solution)/shard_map/ppermute | solution.py:24
  527.6 12.6 %collective-permute-start.31 = (bf16[128,1024]{1,0:T(8,128)(2,1)S(1)}, bf16[128,1024]{1,0:T(8,128)(2,1)S(1)}, u32[]{:S(2)}, u32[]{:S(2)}) collective-permute-start(bf16[128,1024]{1,0:T(8,128)(2,1)S(1)} %pad_maximum_fusion.19), channel_id=1, source_target_pairs={{0,4},{1,5},{2,6},{3,7},{4,0},{5,1},{6,2},{7,3},{8,12},{9,13},{10,... | collective-permute-start | bytes 786440 | tf_op jit(solution)/shard_map/ppermute | solution.py:24
  539.3 12.1 %collective-permute-start.52 = (bf16[256,1024]{1,0:T(8,128)(2,1)S(1)}, bf16[256,1024]{1,0:T(8,128)(2,1)S(1)}, u32[]{:S(2)}, u32[]{:S(2)}) collective-permute-start(bf16[256,1024]{1,0:T(8,128)(2,1)S(1)} %pad_maximum_fusion.16), channel_id=1, source_target_pairs={{0,8},{1,9},{2,10},{3,11},{4,12},{5,13},{6,14},{7,15},{8,0},{9,1},... | collective-permute-start | bytes 1572872 | tf_op jit(solution)/shard_map/ppermute | solution.py:24
  539.6 14.5 %collective-permute-start.42 = (bf16[256,1024]{1,0:T(8,128)(2,1)S(1)}, bf16[256,1024]{1,0:T(8,128)(2,1)S(1)}, u32[]{:S(2)}, u32[]{:S(2)}) collective-permute-start(bf16[256,1024]{1,0:T(8,128)(2,1)S(1)} %pad_maximum_fusion.15), channel_id=1, source_target_pairs={{0,4},{1,5},{2,6},{3,7},{4,0},{5,1},{6,2},{7,3},{8,12},{9,13},{10,... | collective-permute-start | bytes 1572872 | tf_op jit(solution)/shard_map/ppermute | solution.py:24
  540.5 14.1 %collective-permute-start.32 = (bf16[256,1024]{1,0:T(8,128)(2,1)S(1)}, bf16[256,1024]{1,0:T(8,128)(2,1)S(1)}, u32[]{:S(2)}, u32[]{:S(2)}) collective-permute-start(bf16[256,1024]{1,0:T(8,128)(2,1)S(1)} %pad_maximum_fusion.14), channel_id=1, source_target_pairs={{0,2},{1,3},{2,0},{3,1},{4,6},{5,7},{6,4},{7,5},{8,10},{9,11},{10,... | collective-permute-start | bytes 1572872 | tf_op jit(solution)/shard_map/ppermute | solution.py:24
  551.8 9.9 %collective-permute-start.53 = (bf16[512,1024]{1,0:T(8,128)(2,1)S(1)}, bf16[512,1024]{1,0:T(8,128)(2,1)S(1)}, u32[]{:S(2)}, u32[]{:S(2)}) collective-permute-start(bf16[512,1024]{1,0:T(8,128)(2,1)S(1)} %pad_maximum_fusion.7), channel_id=1, source_target_pairs={{0,1},{1,0},{2,3},{3,2},{4,5},{5,4},{6,7},{7,6},{8,9},{9,8},{10,11... | collective-permute-start | bytes 3145736 | tf_op jit(solution)/shard_map/ppermute | solution.py:24
  554.4 10.3 %collective-permute-start.43 = (bf16[512,1024]{1,0:T(8,128)(2,1)S(1)}, bf16[512,1024]{1,0:T(8,128)(2,1)S(1)}, u32[]{:S(2)}, u32[]{:S(2)}) collective-permute-start(bf16[512,1024]{1,0:T(8,128)(2,1)S(1)} %pad_maximum_fusion.6), channel_id=1, source_target_pairs={{0,1},{1,0},{2,3},{3,2},{4,5},{5,4},{6,7},{7,6},{8,9},{9,8},{10,11... | collective-permute-start | bytes 3145736 | tf_op jit(solution)/shard_map/ppermute | solution.py:24
  554.9 12.9 %collective-permute-start.33 = (bf16[512,1024]{1,0:T(8,128)(2,1)S(1)}, bf16[512,1024]{1,0:T(8,128)(2,1)S(1)}, u32[]{:S(2)}, u32[]{:S(2)}) collective-permute-start(bf16[512,1024]{1,0:T(8,128)(2,1)S(1)} %pad_maximum_fusion.5), channel_id=1, source_target_pairs={{0,1},{1,0},{2,3},{3,2},{4,5},{5,4},{6,7},{7,6},{8,9},{9,8},{10,11... | collective-permute-start | bytes 3145736 | tf_op jit(solution)/shard_map/ppermute | solution.py:24
  (118 other events, 795.8 us)

commit v2 on v1

v2 whole, which is shorter than its diff:
```python
import functools
import math

import jax
import jax.numpy as jnp
from jax import lax
from jax.experimental import pallas as pl
from jax.experimental.pallas import tpu as pltpu
from jax.sharding import PartitionSpec as P

BLOCK = 256
SEQ_LEN = 16384
EPS = 1e-06
FLOAT = jnp.float32
BHALF = jnp.bfloat16
VMEM_BYTES = 60 * 1024 * 1024


def bits_of(count):
    return [1 << b for b in range(count.bit_length() - 1)]


def swap(value, mask, axes=("seq", "tp")):
    count = lax.axis_size(axes)
    return lax.ppermute(value, axes, [(s, s ^ mask) for s in range(count)])


def bit_of(place, mask):
    return (place // mask) % 2


def after(value, *others):
    return lax.optimization_barrier((value,) + others)[0]


def halve(value, masks, place):
    for mask in masks:
        halves = value.reshape((2, value.shape[0] // 2) + value.shape[1:])
        bit = bit_of(place, mask)
        keep = lax.dynamic_index_in_dim(halves, bit, 0, False)
        send = lax.dynamic_index_in_dim(halves, 1 - bit, 0, False)
        value = (keep.astype(FLOAT) + swap(send, mask).astype(FLOAT)).astype(BHALF)
    return value


def double(value, masks, place):
    for mask in masks:
        other = swap(value, mask)
        bit = bit_of(place, mask)
        first = jnp.where(bit == 0, value, other)
        second = jnp.where(bit == 0, other, value)
        value = jnp.concatenate([first, second], axis=0)
    return value


def fold(value, masks):
    for mask in masks:
        half = value.shape[0] // 2
        got = swap(value[half:], mask)
        value = (value[:half].astype(FLOAT) + got.astype(FLOAT)).astype(BHALF)
    return value[0]


def decayed_scan(state, rate, unit, span, place, reverse):
    heads = state.shape[0]
    half = heads // 2
    bit = bit_of(place, 1)
    halves = state.reshape((2, half) + state.shape[1:])
    mine = lax.dynamic_index_in_dim(halves, bit, 0, False)
    theirs = lax.dynamic_index_in_dim(halves, 1 - bit, 0, False)
    other = swap(theirs.astype(BHALF), 1).astype(FLOAT)
    own_rate = lax.dynamic_index_in_dim(rate.reshape(2, half), bit, 0, False)

    def power(count):
        return jnp.exp2(-unit * count * own_rate)[:, None, None]

    later = 1 - bit if reverse else bit
    core_later = jnp.where(later == 1, mine, other)
    core_first = jnp.where(later == 1, other, mine)
    total = power(1.0) * core_first + core_later
    prefix = jnp.zeros_like(total)
    mark = None
    for mask in bits_of(span)[1:]:
        bit = bit_of(place, mask)
        later = 1 - bit if reverse else bit
        sent = swap(total.astype(BHALF), mask)
        mark = sent if mark is None else mark
        got = sent.astype(FLOAT)
        within = (place % mask) // 2
        if reverse:
            within = mask // 2 - 1 - within
        scale = power(2.0 * within.astype(FLOAT))
        prefix = prefix + jnp.where(later == 1, scale * got, 0.0)
        low = jnp.where(later == 1, got, total)
        high = jnp.where(later == 1, total, got)
        total = power(float(mask)) * low + high
    second_pre = power(1.0) * prefix + core_first
    bit = bit_of(place, 1)
    later = 1 - bit if reverse else bit
    own = jnp.where(later == 1, second_pre, prefix)
    away = jnp.where(later == 1, prefix, second_pre)
    got = swap(away.astype(BHALF), 1).astype(FLOAT)
    first = jnp.where(bit == 0, own, got)
    second = jnp.where(bit == 0, got, own)
    return jnp.concatenate([first, second], axis=0), mark


def gather_group(value, masks):
    rows = {0: value}
    for mask in masks:
        for r in list(rows):
            rows[r | mask] = swap(rows[r], mask)
    return [rows[r] for r in range(len(rows))]


def dot_nn(left, right):
    return jnp.dot(left, right, preferred_element_type=FLOAT)


def dot_tn(left, right):
    return lax.dot_general(left, right, (((0,), (0,)), ((), ())), preferred_element_type=FLOAT)


def dot_nt(left, right):
    return lax.dot_general(left, right, (((1,), (1,)), ((), ())), preferred_element_type=FLOAT)


def srms(values):
    return values * lax.rsqrt(jnp.mean(values * values, axis=-1, keepdims=True) + EPS)


def srms_back(values, gradient):
    scaled = lax.rsqrt(jnp.mean(values * values, axis=-1, keepdims=True) + EPS)
    normed = values * scaled
    return scaled * (gradient - normed * jnp.mean(gradient * normed, axis=-1, keepdims=True))


def swish(values):
    return values * jax.nn.sigmoid(values)


def swish_slope(values):
    sigmoid = jax.nn.sigmoid(values)
    return sigmoid * (1.0 + values * (1.0 - sigmoid))


def half_turn(values):
    return pltpu.roll(values, values.shape[-1] // 2, 1)


def rotate(values, cosine, sine):
    return values * cosine + half_turn(values) * sine


def unrotate(values, cosine, sine):
    return values * cosine - half_turn(values) * sine


def row_decay(rate, size, start, sign):
    offset = lax.broadcasted_iota(jnp.int32, (BLOCK, size), 0).astype(FLOAT)
    return jnp.exp2(-(start + sign * offset) * rate)


def query_decay(rate, size):
    return row_decay(rate, size, 1.0, 1.0)


def key_decay(rate, size):
    return row_decay(rate, size, BLOCK - 1.0, -1.0)


def decay_matrix(rate):
    row = lax.broadcasted_iota(jnp.int32, (BLOCK, BLOCK), 0)
    column = lax.broadcasted_iota(jnp.int32, (BLOCK, BLOCK), 1)
    distance = (row - column).astype(FLOAT)
    return jnp.where(distance >= 0.0, jnp.exp2(-jnp.maximum(distance, 0.0) * rate), 0.0)


def scaled_by(factor_exponent, values):
    return jnp.exp2(jnp.full(values.shape, factor_exponent, FLOAT)) * values


def shape_of(shape, dtype):
    return jax.ShapeDtypeStruct(shape, dtype)


SMEM_SPEC = pl.BlockSpec(memory_space=pltpu.SMEM)


def call(body, grid, in_specs, out_specs, out_shape, flops, moved, scratch=()):
    return pl.pallas_call(
        body,
        grid=grid,
        in_specs=in_specs,
        out_specs=out_specs,
        out_shape=out_shape,
        scratch_shapes=scratch,
        cost_estimate=pl.CostEstimate(flops=flops, bytes_accessed=moved, transcendentals=0),
        compiler_params=pltpu.CompilerParams(vmem_limit_bytes=VMEM_BYTES),
    )


def kv_body(heads, rate, x, wk, wv, cosine, sine, normed, pre_key, keys, values, contrib, local):
    step = pl.program_id(0)
    size = cosine.shape[1]
    blocks = x.shape[0] // BLOCK

    @pl.when(step == 0)
    def _():
        normed[...] = srms(x[...].astype(FLOAT)).astype(BHALF)

    rows = normed[...]
    pre = dot_nn(rows, wk[...])
    pre_key[...] = pre
    val = dot_nn(rows, wv[...]).astype(BHALF)
    values[...] = val
    for h in range(heads):
        part = slice(h * size, (h + 1) * size)
        own_rate = rate[step * heads + h]
        key = rotate(swish(pre[:, part]), cosine[...], sine[...]).astype(BHALF)
        keys[:, part] = key
        decay = key_decay(own_rate, size)
        total = None
        for b in range(blocks):
            span = slice(b * BLOCK, (b + 1) * BLOCK)
            decayed = (key[span].astype(FLOAT) * decay).astype(BHALF)
            state = dot_tn(decayed, val[span, part])
            contrib[b, h] = state
            total = state if total is None else scaled_by(-BLOCK * own_rate, total) + state
        local[h] = total


def kv(rate, x, wk, wv, cosine, sine, steps):
    tokens, width = x.shape
    heads = rate.shape[0]
    size = width // heads
    group = heads // steps
    cols = group * size
    blocks = tokens // BLOCK
    tile = lambda n: pl.BlockSpec((n, cols), lambda i: (0, i))
    whole = lambda a: pl.BlockSpec(a.shape, lambda i: (0, 0))
    return call(
        functools.partial(kv_body, group),
        (steps,),
        [SMEM_SPEC, whole(x), tile(width), tile(width), whole(cosine), whole(sine)],
        [
            whole(x),
            tile(tokens),
            tile(tokens),
            tile(tokens),
            pl.BlockSpec((blocks, group, size, size), lambda i: (0, i, 0, 0)),
            pl.BlockSpec((group, size, size), lambda i: (i, 0, 0)),
        ],
        [
            shape_of(x.shape, BHALF),
            shape_of(x.shape, FLOAT),
            shape_of(x.shape, BHALF),
            shape_of(x.shape, BHALF),
            shape_of((blocks, heads, size, size), FLOAT),
            shape_of((heads, size, size), FLOAT),
        ],
        4 * tokens * width * width,
        12 * tokens * width + 4 * width * width,
    )(rate, x, wk, wv, cosine, sine)


def qu_body(heads, rate, rows, wq, wu, cosine, sine, keys, values, pre_query, query, gate, intra):
    step = pl.program_id(0)
    size = cosine.shape[1]
    blocks = rows.shape[0] // BLOCK
    pre = dot_nn(rows[...], wq[...])
    pre_query[...] = pre
    gate[...] = dot_nn(rows[...], wu[...])
    for h in range(heads):
        part = slice(h * size, (h + 1) * size)
        q = rotate(swish(pre[:, part]), cosine[...], sine[...]).astype(BHALF)
        query[:, part] = q
        decay = decay_matrix(rate[step * heads + h])
        for b in range(blocks):
            span = slice(b * BLOCK, (b + 1) * BLOCK)
            weights = (dot_nt(q[span], keys[span, part]) * decay).astype(BHALF)
            intra[span, part] = dot_nn(weights, values[span, part])


def qu(rate, rows, wq, wu, cosine, sine, keys, values, steps):
    tokens, width = rows.shape
    heads = rate.shape[0]
    group = heads // steps
    cols = group * (width // heads)
    tile = lambda n: pl.BlockSpec((n, cols), lambda i: (0, i))
    whole = lambda a: pl.BlockSpec(a.shape, lambda i: (0, 0))
    return call(
        functools.partial(qu_body, group),
        (steps,),
        [SMEM_SPEC, whole(rows), tile(width), tile(width), whole(cosine), whole(sine)]
        + [tile(tokens)] * 2,
        [tile(tokens)] * 4,
        [shape_of(rows.shape, d) for d in (FLOAT, BHALF, FLOAT, FLOAT)],
        4 * tokens * width * width,
        20 * tokens * width + 4 * width * width,
    )(rate, rows, wq, wu, cosine, sine, keys, values)


def join_body(heads, use_next, rate, x, intra, query, gate, state, before, wo, *outs):
    attended, gated, resid, normed, used = outs
    size = state.shape[1]
    pieces = []
    for h in range(heads):
        part = slice(h * size, (h + 1) * size)
        own_rate = rate[h]
        here = state[h]
        if use_next:
            here = scaled_by(-BLOCK * own_rate, here) + before[h]
        here = here.astype(BHALF)
        used[h] = here
        q = (query[:, part].astype(FLOAT) * query_decay(own_rate, size)).astype(BHALF)
        pieces.append(intra[:, part] + dot_nn(q, here))
    full = jnp.concatenate(pieces, axis=1)
    attended[...] = full
    g = (srms(full) * gate[...]).astype(BHALF)
    gated[...] = g
    r = x[...].astype(FLOAT) + dot_nn(g, wo[...])
    resid[...] = r
    normed[...] = srms(r).astype(BHALF)


def join(block, rate, x, intra, query, gate, state, contrib, wo):
    width = x.shape[1]
    heads, size = state.shape[0], state.shape[1]
    before = contrib
    if block > 1:
        for b in range(block - 1):
            state = jnp.exp2(-BLOCK * rate)[:, None, None] * state + contrib[b]
    row = pl.BlockSpec((BLOCK, width), lambda i: (block, 0))
    out_row = pl.BlockSpec((BLOCK, width), lambda i: (0, 0))
    cube = pl.BlockSpec((heads, size, size), lambda i: (0, 0, 0))
    earlier = max(block - 1, 0)
    return call(
        functools.partial(join_body, heads, block > 0),
        (1,),
        [SMEM_SPEC, row, row, row, row, cube]
        + [pl.BlockSpec((None, heads, size, size), lambda i: (earlier, 0, 0, 0))]
        + [pl.BlockSpec(wo.shape, lambda i: (0, 0))],
        [out_row] * 4 + [cube],
        [shape_of((BLOCK, width), d) for d in (FLOAT, BHALF, FLOAT, BHALF)]
        + [shape_of((heads, size, size), BHALF)],
        2 * BLOCK * width * (width + size),
        24 * BLOCK * width + 2 * width * width,
    )(rate, x, intra, query, gate, state, before, wo)


def unit_body(n0, n1, c0, c1, gate_t, linear_t, down, keep, ship, hidden, gate_back, linear_back):
    rows = jnp.concatenate([n0[...], n1[...]], axis=0)
    cots = jnp.concatenate([c0[...], c1[...]], axis=0)
    gate = dot_nt(rows, gate_t[...])
    linear = dot_nt(rows, linear_t[...])
    inner = (gate * linear).astype(BHALF)
    hidden[...] = inner
    inner_cot = dot_nt(cots, down[...])
    gb = (inner_cot * linear).astype(BHALF)
    lb = (inner_cot * gate).astype(BHALF)
    gate_back[...] = gb
    linear_back[...] = lb
    feed = dot_nn(inner, down[...])
    cot = dot_nn(gb, gate_t[...]) + dot_nn(lb, linear_t[...])
    keep[0] = cot[:BLOCK]
    keep[1] = feed[:BLOCK]
    ship[0] = cot[BLOCK:].astype(BHALF)
    ship[1] = feed[BLOCK:].astype(BHALF)


def unit(block, rows, cots, gate_t, linear_t, down):
    width = rows[0].shape[1]
    inner = down.shape[0]
    piece = pl.BlockSpec((BLOCK, width), lambda i: (0, 0))
    cot = pl.BlockSpec((BLOCK, width), lambda i: (block, 0))
    whole = lambda s: pl.BlockSpec(s, lambda i: (0,) * len(s))
    wide = (2 * BLOCK, inner)
    pair = (2, BLOCK, width)
    return call(
        unit_body,
        (1,),
        [piece] * 2 + [cot] * 2 + [whole(down.shape)] * 3,
        [whole(pair)] * 2 + [whole(wide)] * 3,
        [shape_of(pair, FLOAT), shape_of(pair, BHALF)] + [shape_of(wide, BHALF)] * 3,
        24 * BLOCK * width * inner,
        6 * width * inner + 20 * BLOCK * width,
    )(*rows, *cots, gate_t, linear_t, down)


def place_in(order, count, shard, place):
    relative = jnp.bitwise_xor(shard, place)
    position = 0
    for mask in order:
        position = position * 2 + jnp.bitwise_and(relative // mask, 1)
    return position


def unit_grads_body(groups, orders, place, *refs):
    per = 2 + 2 + 3
    ins = refs[: groups * per]
    pair_out, down_out = refs[groups * per : groups * per + 2]
    rows, cots, hidden, gate_back, linear_back, sems = refs[groups * per + 2 :]
    copies = [[] for _ in range(groups)]
    for g in range(groups):
        n0, n1, c0, c1, h, gb, lb = ins[g * per : (g + 1) * per]
        block = g % 2
        span = pl.ds(block * BLOCK, BLOCK)
        moves = [
            (gb, gate_back.at[g]),
            (n0, rows.at[g, pl.ds(0, BLOCK)]),
            (n1, rows.at[g, pl.ds(BLOCK, BLOCK)]),
            (lb, linear_back.at[g]),
            (h, hidden.at[g]),
            (c0.at[span], cots.at[g, pl.ds(0, BLOCK)]),
            (c1.at[span], cots.at[g, pl.ds(BLOCK, BLOCK)]),
        ]
        for k, (source, target) in enumerate(moves):
            copies[g].append(pltpu.make_async_copy(source, target, sems.at[g, k]))
    for first, last in ((0, 3), (3, 4), (4, 7)):
        for g in range(groups):
            for copy in copies[g][first:last]:
                copy.start()
    count = pair_out.shape[0]
    here = place[0]

    def total(left, right, first, last):
        acc = None
        for g in range(groups):
            for copy in copies[g][first:last]:
                copy.wait()
            term = dot_tn(left[g], right[g])
            acc = term if acc is None else acc + term
        return acc

    def store(acc, put, order):
        size = acc.shape[1] // count
        for shard in range(count):
            put(place_in(order, count, shard, here), acc[:, shard * size : (shard + 1) * size])

    def put_pair(k):
        def put(position, value):
            pair_out[position, k] = value.astype(BHALF)
        return put

    def put_down(position, value):
        down_out[position] = value.astype(BHALF)

    store(total(gate_back, rows, 0, 3), put_pair(0), orders[0])
    store(total(linear_back, rows, 3, 4), put_pair(1), orders[0])
    store(total(hidden, cots, 4, 7), put_down, orders[1])


def unit_grads(place, groups, orders, count):
    inner = groups[0][4].shape[1]
    width = groups[0][0].shape[1]
    flat = [a for group in groups for a in group]
    any_spec = pl.BlockSpec(memory_space=pl.ANY)
    size = width // count
    pair = (count, 2, inner, size)
    single = (count, inner, size)
    n = len(groups)
    whole = lambda s: pl.BlockSpec(s, lambda i: (0,) * len(s))
    return call(
        functools.partial(unit_grads_body, n, orders),
        (1,),
        [SMEM_SPEC] + [any_spec] * len(flat),
        [whole(pair), whole(single)],
        [shape_of(pair, BHALF), shape_of(single, BHALF)],
        12 * n * BLOCK * width * inner,
        n * 2 * BLOCK * (4 * width + 6 * inner) + 6 * width * inner,
        scratch=[
            pltpu.VMEM((n, 2 * BLOCK, width), BHALF),
            pltpu.VMEM((n, 2 * BLOCK, width), BHALF),
            pltpu.VMEM((n, 2 * BLOCK, inner), BHALF),
            pltpu.VMEM((n, 2 * BLOCK, inner), BHALF),
            pltpu.VMEM((n, 2 * BLOCK, inner), BHALF),
            pltpu.SemaphoreType.DMA((n, 7)),
        ],
    )(place, *flat)


def turn_body(heads, rate, keep, got, far, resid, cot, attended, gate, query, wo, *outs):
    resid_cot, branch, modulate, back, direct = outs
    size = direct.shape[1]
    normed_cot = keep[0] + got[0].astype(FLOAT)
    for k in range(far.shape[0]):
        normed_cot = normed_cot + far[k].astype(FLOAT)
    rc = cot[...].astype(FLOAT) + srms_back(resid[...], normed_cot)
    resid_cot[...] = rc
    bb = rc.astype(BHALF)
    branch[...] = bb
    gated_cot = dot_nt(bb, wo[...])
    att = attended[...]
    modulate[...] = (gated_cot * srms(att)).astype(BHALF)
    ab = srms_back(att, gated_cot * gate[...]).astype(BHALF)
    back[...] = ab
    for h in range(heads):
        part = slice(h * size, (h + 1) * size)
        q = (query[:, part].astype(FLOAT) * query_decay(rate[h], size)).astype(BHALF)
        direct[h] = dot_tn(q, ab[:, part])


def turn(block, rate, keep, got, far, resid, cot, attended, gate, query, wo):
    width = resid.shape[1]
    heads = rate.shape[0]
    size = width // heads
    row = pl.BlockSpec((BLOCK, width), lambda i: (block, 0))
    own = pl.BlockSpec((BLOCK, width), lambda i: (0, 0))
    first = pl.BlockSpec((1, BLOCK, width), lambda i: (0, 0, 0))
    cube = pl.BlockSpec((heads, size, size), lambda i: (0, 0, 0))
    return call(
        functools.partial(turn_body, heads),
        (1,),
        [SMEM_SPEC, first, first, pl.BlockSpec(far.shape, lambda i: (0, 0, 0)), own, row, own]
        + [row, row, pl.BlockSpec(wo.shape, lambda i: (0, 0))],
        [own] * 4 + [cube],
        [shape_of((BLOCK, width), d) for d in (FLOAT, BHALF, BHALF, BHALF)]
        + [shape_of((heads, size, size), FLOAT)],
        2 * BLOCK * width * (width + size),
        32 * BLOCK * width + 2 * width * width,
    )(rate, keep, got, far, resid, cot, attended, gate, query, wo)


def query_body(heads, blocks, rate, pre_query, query, keys, values, cosine, sine, *refs):
    backs = refs[:blocks]
    used = refs[blocks : 2 * blocks]
    query_back, key_part, value_part = refs[2 * blocks :]
    step = pl.program_id(0)
    size = cosine.shape[1]
    for h in range(heads):
        part = slice(h * size, (h + 1) * size)
        own_rate = rate[step * heads + h]
        decay = decay_matrix(own_rate)
        row = query_decay(own_rate, size)
        for b in range(blocks):
            span = slice(b * BLOCK, (b + 1) * BLOCK)
            q, k, v = query[span, part], keys[span, part], values[span, part]
            ab = backs[b][:, part]
            weights = (dot_nt(q, k) * decay).astype(BHALF)
            weights_back = (dot_nt(ab, v) * decay).astype(BHALF)
            value_part[span, part] = dot_tn(weights, ab)
            key_part[span, part] = dot_tn(weights_back, q)
            cot = dot_nn(weights_back, k) + row * dot_nt(ab, used[b][h])
            cot = unrotate(cot, cosine[span], sine[span])
            query_back[span, part] = (cot * swish_slope(pre_query[span, part])).astype(BHALF)


def query_side(rate, pre_query, query, keys, values, cosine, sine, backs, used, steps):
    tokens, width = query.shape
    heads = rate.shape[0]
    size = width // heads
    group = heads // steps
    cols = group * size
    blocks = len(backs)
    tile = pl.BlockSpec((tokens, cols), lambda i: (0, i))
    whole = lambda a: pl.BlockSpec(a.shape, lambda i: (0, 0))
    return call(
        functools.partial(query_body, group, blocks),
        (steps,),
        [SMEM_SPEC] + [tile] * 4 + [whole(cosine), whole(sine)]
        + [pl.BlockSpec((BLOCK, cols), lambda i: (0, i))] * blocks
        + [pl.BlockSpec((group, size, size), lambda i: (i, 0, 0))] * blocks,
        [tile] * 3,
        [shape_of(query.shape, d) for d in (BHALF, FLOAT, FLOAT)],
        12 * tokens * width * BLOCK,
        24 * tokens * width,
    )(rate, pre_query, query, keys, values, cosine, sine, *backs, *used)


def key_body(heads, blocks, rate, pre_key, keys, values, key_part, value_part, *refs):
    cosine, sine, state = refs[:3]
    direct = refs[3 : 3 + blocks]
    key_back, value_back = refs[3 + blocks :]
    step = pl.program_id(0)
    size = cosine.shape[1]
    for h in range(heads):
        part = slice(h * size, (h + 1) * size)
        own_rate = rate[step * heads + h]
        decay = key_decay(own_rate, size)
        here = state[h]
        for b in reversed(range(blocks)):
            span = slice(b * BLOCK, (b + 1) * BLOCK)
            used = here.astype(BHALF)
            cot = key_part[span, part] + decay * dot_nt(values[span, part], used)
            decayed = (keys[span, part].astype(FLOAT) * decay).astype(BHALF)
            vcot = value_part[span, part] + dot_nn(decayed, used)
            cot = unrotate(cot, cosine[span], sine[span])
            key_back[span, part] = (cot * swish_slope(pre_key[span, part])).astype(BHALF)
            value_back[span, part] = vcot.astype(BHALF)
            if b:
                here = scaled_by(-BLOCK * own_rate, here) + direct[b][h]


def key_side(rate, pre_key, keys, values, key_part, value_part, cosine, sine, state, direct, steps):
    tokens, width = keys.shape
    heads = rate.shape[0]
    size = width // heads
    group = heads // steps
    cols = group * size
    blocks = len(direct)
    tile = pl.BlockSpec((tokens, cols), lambda i: (0, i))
    whole = lambda a: pl.BlockSpec(a.shape, lambda i: (0, 0))
    cube = pl.BlockSpec((group, size, size), lambda i: (i, 0, 0))
    return call(
        functools.partial(key_body, group, blocks),
        (steps,),
        [SMEM_SPEC] + [tile] * 5 + [whole(cosine), whole(sine), cube] + [cube] * blocks,
        [tile] * 2,
        [shape_of(keys.shape, BHALF)] * 2,
        4 * tokens * width * size,
        20 * tokens * width,
    )(rate, pre_key, keys, values, key_part, value_part, cosine, sine, state, *direct)


def grads_body(lefts, pairs, core, *refs):
    left = refs[:lefts]
    right = refs[lefts:-1]
    out = refs[-1]
    for k, (l, rs) in enumerate(pairs):
        acc = None
        start = 0
        for piece in rs:
            r = right[piece]
            rows = r.shape[0]
            term = dot_tn(left[l][start : start + rows], r[...])
            start += rows
            acc = term if acc is None else acc + term
        out[0, k] = acc.astype(BHALF)


def grads(core, lefts, rights, pairs):
    tokens, width = lefts[0].shape
    cols = rights[0].shape[1]
    half = width // 2
    spec = pltpu.PrefetchScalarGridSpec(
        num_scalar_prefetch=1,
        grid=(2,),
        in_specs=[pl.BlockSpec((tokens, half), lambda i, c: (0, i ^ c[0]))] * len(lefts)
        + [pl.BlockSpec(r.shape, lambda i, c: (0, 0)) for r in rights],
        out_specs=pl.BlockSpec((1, len(pairs), half, cols), lambda i, c: (i, 0, 0, 0)),
    )
    n = len(pairs)
    body = functools.partial(grads_body, len(lefts), pairs)
    return pl.pallas_call(
        body,
        grid_spec=spec,
        out_shape=shape_of((2, n, half, cols), BHALF),
        cost_estimate=pl.CostEstimate(
            flops=2 * n * tokens * width * cols, bytes_accessed=4 * n * width * cols, transcendentals=0
        ),
        compiler_params=pltpu.CompilerParams(vmem_limit_bytes=VMEM_BYTES),
    )(core, *lefts, *rights)


def tokens_body(x, rc, qb, kb, vb, mb, wq, wk, wv, wm, out):
    grad = dot_nt(qb[...], wq[...]) + dot_nt(kb[...], wk[...])
    grad = grad + dot_nt(vb[...], wv[...]) + dot_nt(mb[...], wm[...])
    out[...] = rc[...] + srms_back(x[...].astype(FLOAT), grad)


def tokens_side(block, x, rc, qb, kb, vb, mb, weights):
    tokens, width = x.shape
    row = pl.BlockSpec((BLOCK, width), lambda i: (block, 0))
    own = pl.BlockSpec((BLOCK, width), lambda i: (0, 0))
    whole = pl.BlockSpec((width, width), lambda i: (0, 0))
    return call(
        tokens_body,
        (1,),
        [row, own, row, row, row, own] + [whole] * 4,
        own,
        shape_of((BLOCK, width), FLOAT),
        8 * BLOCK * width * width,
        8 * width * width + 20 * BLOCK * width,
    )(x, rc, qb, kb, vb, mb, *weights)


def angle_tables(position, halves):
    column = jnp.arange(halves, dtype=jnp.int32)
    factor = 1 + jnp.right_shift(jnp.full((halves,), 16384, jnp.int32), column // 4)
    phase = position[:, None] * factor[None, :] % 65536
    turned = phase.astype(FLOAT) * (2.0 * math.pi / 65536.0)
    cosine, sine = jnp.cos(turned), jnp.sin(turned)
    return jnp.concatenate([cosine, cosine], 1), jnp.concatenate([-sine, sine], 1)


def shards(
    tokens,
    query_weight,
    key_weight,
    value_weight,
    modulate_weight,
    output_weight,
    gate_weight,
    linear_weight,
    down_weight,
    cotangent,
    decay_exponent,
):
    count, width = tokens.shape
    heads = decay_exponent.shape[0]
    size = width // heads
    runs, members = lax.axis_size("seq"), lax.axis_size("tp")
    devices = runs * members
    length = min(SEQ_LEN, count * devices)
    span = length // count
    blocks = count // BLOCK
    seq_place = lax.axis_index("seq")
    place = seq_place * members + lax.axis_index("tp")
    core = bit_of(place, 1).astype(jnp.int32).reshape(1)
    position = (place * count + jnp.arange(count, dtype=jnp.int32)) % length
    rate = jnp.exp2(-decay_exponent.astype(FLOAT))
    cosine, sine = angle_tables(position, size // 2)
    ring = bits_of(members)
    far = ring[1:]

    normed, pre_key, keys, values, contrib, local = kv(
        rate, tokens, key_weight, value_weight, cosine, sine, 2
    )
    state, mark = decayed_scan(local, rate, float(count), span, place, False)
    pre_query, query, gate, intra = qu(
        rate, normed, query_weight, modulate_weight, cosine, sine, keys, values, 2
    )
    cots = gather_group(after(cotangent, mark), far + [1])
    joined = [
        join(b, rate, tokens, intra, query, gate, state, contrib, output_weight)
        for b in range(blocks)
    ]

    gate_t, linear_t = gate_weight.T, linear_weight.T
    gathered = [gather_group(joined[b][3], far + [1]) for b in range(blocks)]
    results = {}
    for r in range(0, members, 2):
        for b in range(blocks):
            results[r, b] = unit(
                b, gathered[b][r : r + 2], cots[r : r + 2], gate_t, linear_t, down_weight
            )
    groups = [
        tuple(gathered[b][r : r + 2]) + tuple(cots[r : r + 2]) + tuple(results[r, b][2:])
        for r in range(0, members, 2)
        for b in range(blocks)
    ]
    near = {}
    for key, value in results.items():
        near[key] = (value[0], swap(value[1], 1))
    arrived = {}
    for part in range(2):
        for b in range(blocks):
            rows = {
                r: near[r, b][0][part] + near[r, b][1][part].astype(FLOAT)
                for r in range(2, members, 2)
            }
            got = []
            for mask in reversed(far):
                for r in [r for r in rows if r & mask]:
                    value = swap(rows.pop(r).astype(BHALF), mask)
                    if r == mask:
                        got.append(value)
                    else:
                        rows[r ^ mask] = rows[r ^ mask] + value.astype(FLOAT)
            arrived[b, part] = got

    turned = [
        turn(
            b, rate, near[0, b][0], near[0, b][1], jnp.stack(arrived[b, 0]), joined[b][2],
            cotangent, joined[b][0], gate, query, output_weight,
        )
        for b in range(blocks)
    ]
    line = bits_of(runs)
    across = max(members // 2, 1)
    orders = (line, [m for m in line if m >= across] + [m for m in line if m < across])
    seq_scalar = seq_place.astype(jnp.int32).reshape(1)
    pair_part, down_part = unit_grads(seq_scalar, groups, orders, runs)

    decays = jnp.exp2(-BLOCK * rate)[:, None, None]
    inbound = turned[blocks - 1][4]
    for b in reversed(range(blocks - 1)):
        inbound = decays * inbound + turned[b][4]
    outer, _ = decayed_scan(inbound, rate, float(count), span, place, True)
    backs = [t[3] for t in turned]
    query_back, key_part, value_part = query_side(
        rate, pre_query, query, keys, values, cosine, sine, backs, [j[4] for j in joined], 2
    )
    gated = jnp.concatenate([j[1] for j in joined], axis=0)
    early = grads(
        core,
        [gated, normed],
        [t[1] for t in turned] + [t[2] for t in turned] + [query_back],
        [
            (0, list(range(blocks))),
            (1, list(range(blocks, 2 * blocks))),
            (1, [2 * blocks]),
        ],
    )
    key_back, value_back = key_side(
        rate, pre_key, keys, values, key_part, value_part, cosine, sine, outer,
        [t[4] for t in turned], 2,
    )
    late = grads(core, [normed], [key_back, value_back], [(0, [0]), (0, [1])])
    weights = (query_weight, key_weight, value_weight, modulate_weight)
    tokens_grad = jnp.concatenate(
        [
            tokens_side(
                b, tokens, turned[b][0], query_back, key_back, value_back, turned[b][2], weights
            )
            for b in range(blocks)
        ],
        axis=0,
    )

    mixed = jnp.concatenate(
        [
            (
                joined[b][2] + near[0, b][0][1] + near[0, b][1][1].astype(FLOAT)
                + sum(a.astype(FLOAT) for a in arrived[b, 1])
            ).astype(BHALF)
            for b in range(blocks)
        ],
        axis=0,
    )
    masks = [[members * m for m in order] for order in orders]
    pair_grad = fold(pair_part, masks[0]).astype(FLOAT)
    down_grad = fold(down_part, masks[1]).astype(FLOAT)
    gate_grad, linear_grad = pair_grad[0].T, pair_grad[1].T

    rest = bits_of(devices)[1:]
    lines = [
        [m for m in rest if m < members],
        [m for m in rest if members <= m < members * across],
        [m for m in rest if m >= members * across],
    ]

    def reduced(part):
        kept = (part[0].astype(FLOAT) + swap(part[1], 1).astype(FLOAT)).astype(BHALF)
        outs = []
        for k in range(kept.shape[0]):
            order = [m for i in range(3) for m in lines[(i + k) % 3]]
            piece = double(halve(kept[k], order, place), list(reversed(order)), place)
            outs.append(double(piece, [1], place).astype(FLOAT))
        return outs

    output_grad, modulate_grad, query_grad = reduced(early)
    key_grad, value_grad = reduced(late)
    return (
        mixed,
        tokens_grad,
        query_grad,
        key_grad,
        value_grad,
        modulate_grad,
        output_grad,
        gate_grad,
        linear_grad,
        down_grad,
    )


def solution(mesh):
    return jax.shard_map(
        shards,
        mesh=mesh,
        in_specs=(
            P(("seq", "tp"), None),
            P(),
            P(),
            P(),
            P(),
            P(),
            P(None, "tp"),
            P(None, "tp"),
            P("tp", None),
            P(("seq", "tp"), None),
            P(),
        ),
        out_specs=(
            P(("seq", "tp"), None),
            P(("seq", "tp"), None),
            P(),
            P(),
            P(),
            P(),
            P(),
            P("seq", "tp"),
            P("seq", "tp"),
            P("tp", "seq"),
        ),
        check_vma=False,
    )
```

time: 580 us -> 412 us (0.71)
  Pallas kernels: 0 us -> 139 us
  matrix products: 115 us -> 0 us
  local copies, waits for them, and re-layouts: 106 us -> 18.1 us
  waiting for transfers between devices: 157 us -> 87.7 us
  other arithmetic: 94.9 us -> 58.5 us
  starting transfers between devices: 94.6 us -> 102 us
    pallas_call x0 -> x17, Pallas kernels: none -> 139 us  [the longest x4 39.9 us: unit(): call(unit_body, (1,), [piece] * 2 + [cot] * 2 + [whole(down.shape)] * 3,...]
    dot_general x48 -> x0, matrix products: 115 us -> none  [the longest x8 32.6 us: matmul(): return jnp.dot(left, right, preferred_element_type=FLOAT)]
    ppermute x83 -> x82, waiting for transfers between devices: 157 us -> 87.7 us  [swap(): return lax.ppermute(value, axes, [(s, s ^ mask) for s in range(count)])]
    reshape x11 -> x1, local copies, waits for them, and re-layouts: 31.5 us -> 0.08 us  [decayed_scan(): own_rate = lax.dynamic_index_in_dim(rate.reshape(2, half), bit, 0, False)]
    dynamic_slice x6 -> x0, local copies, waits for them, and re-layouts: 29.7 us -> none  [halve(): keep = lax.dynamic_index_in_dim(halves, bit, 0, False)]
    unnamed x213 -> x46, local copies, waits for them, and re-layouts: 26 us -> 4.59 us
    convert_element_type x54 -> x45, other arithmetic: 50.3 us -> 38.5 us  [the longest x5 12.2 us: reduced(): outs.append(double(piece, [1], place).astype(FLOAT))]
    add x4 -> x2, other arithmetic: 9.65 us -> 1.16 us  [the longest x1 1.16 us: shards(): inbound = decays * inbound + turned[b][4]]
  transfers between devices with their start and end apart: 83 -> 82, of which waited for: 32 -> 26; matrix products, arithmetic and copies ran while one was open for 37% -> 15% of each run, Pallas kernels for 0% -> 32%
where the time goes in v2:
time: 412 us; the launch traced here: 407 us
  Pallas kernels  139 us (34%)
  starting transfers between devices  102 us (25%)
  waiting for transfers between devices  87.7 us (21%)
  other arithmetic  58.5 us (14%)
  local copies, waits for them, and re-layouts  18.1 us (4%)
    ppermute x82, starting transfers between devices, swap(): return lax.ppermute(value, axes, [(s, s ^ mask) for s in range(count)])  102 us
    ppermute x82, waiting for transfers between devices, swap(): return lax.ppermute(value, axes, [(s, s ^ mask) for s in range(count)])  87.7 us
    pallas_call x4, Pallas kernels, unit(): call(unit_body, (1,), [piece] * 2 + [cot] * 2 + [whole(down.shape)] * 3,...  39.9 us
    pallas_call x2, Pallas kernels, tokens_side(): call(tokens_body, (1,), [row, own, row, row, row, own] + [whole] * 4, own...  16.2 us
    pallas_call x1, Pallas kernels, unit_grads(): call(functools.partial(unit_grads_body, n, orders), (1,), [SMEM_SPEC] + [...  14.7 us
    pallas_call x2, Pallas kernels, grads(): pl.pallas_call(body, grid_spec=spec, out_shape=shape_of((2, n, half, cols...  13.7 us
    pallas_call x2, Pallas kernels, turn(): call(functools.partial(turn_body, heads), (1,), [SMEM_SPEC, first, first,...  12.3 us
    convert_element_type x5, other arithmetic, reduced(): outs.append(double(piece, [1], place).astype(FLOAT))  12.2 us
  transfers between devices with their start and end apart: 82, of which 26 were waited for; matrix products, arithmetic and copies ran while one was open for 15% of the time, Pallas kernels for 32%

profile of v2, /device:TPU:1, one launch (start us, length us, event | category | flops | bytes accessed | tf_op | source)
XLA Modules:
  0.0 407.0 jit_solution(3015165272857111076)
XLA Ops:
  4.0 7.0 %shard_map.186 = (bf16[512,1024]{1,0:T(8,128)(2,1)}, f32[512,1024]{1,0:T(8,128)}, bf16[512,1024]{1,0:T(8,128)(2,1)}, bf16[512,1024]{1,0:T(8,128)(2,1)}, f32[2,8,...) custom-call(f32[8]{0:T(128)} %get-tuple-element.216.rate, bf16[512,1024]{1,0:T(8,128)(2,1)} %x.9, bf16[1024,1024]{1,0:T(8,128)(2,1)} %wk.5, ...), custom_call_target="tpu_custom_call" | custom-call | flops 2147483648 | bytes 10485760 | tf_op jit(solution)/shard_map/pallas_call | solution.py:242
  14.6 2.4 collective-permute-start.1
  17.0 3.6 collective-permute-done.1
  22.9 3.0 collective-permute-done.2
  27.0 2.9 collective-permute-done.3
  30.0 2.0 collective-permute-start.4
  33.2 3.0 collective-permute-done.4
  36.5 4.2 %collective-permute-start.5 = (bf16[4,128,128]{2,1,0:T(8,128)(2,1)S(1)}, bf16[4,128,128]{2,1,0:T(8,128)(2,1)S(1)}, u32[]{:S(2)}, u32[]{:S(2)}) collective-permute-start(bf16[4,128,128]{2,1,0:T(8,128)(2,1)S(1)} %get-tuple-element.132), channel_id=1, source_target_pairs={{0,1},{1,0},{2,3},{3,2},{4,5},{5,4},{6,7},{7,6},{8,9},{9,8},{10,11... | collective-permute-start | bytes 393224 | tf_op jit(solution)/shard_map/ppermute | solution.py:25
  40.8 8.3 %shard_map.187 = (f32[512,1024]{1,0:T(8,128)}, bf16[512,1024]{1,0:T(8,128)(2,1)}, f32[512,1024]{1,0:T(8,128)}, f32[512,1024]{1,0:T(8,128)}) custom-call(f32[8]{0:T(128)} %get-tuple-element.216.rate, bf16[512,1024]{1,0:T(8,128)(2,1)} %get-tuple-element.68.rows.refs_1_.refs_0_, bf16[1024,1024]{1,0:T(8,128)(2,1)} %wq.5, bf16[1024,1024]{1,0:T(8,128)(2,1)} %wm.3, ...), custom_call_target="tpu_custom_call" | custom-call | flops 2147483648 | bytes 14680064 | tf_op jit(solution)/shard_map/pallas_call | solution.py:292
  50.2 5.3 %shard_map.191 = (f32[256,1024]{1,0:T(8,128)}, bf16[256,1024]{1,0:T(8,128)(2,1)}, f32[256,1024]{1,0:T(8,128)}, bf16[256,1024]{1,0:T(8,128)(2,1)}, bf16[8,128,128]{2,1,0:T(8,128)(2,1)}) custom-call(f32[8]{0:T(128)} %get-tuple-element.216.rate, bf16[512,1024]{1,0:T(8,128)(2,1)} %x.9, f32[512,1024]{1,0:T(8,128)} %get-tuple-element.71.intra, ...), custom_call_target="tpu_custom_call" | custom-call | flops 603979776 | bytes 8388608 | tf_op jit(solution)/shard_map/pallas_call | solution.py:338
  57.7 5.2 %shard_map.188 = (f32[256,1024]{1,0:T(8,128)}, bf16[256,1024]{1,0:T(8,128)(2,1)}, f32[256,1024]{1,0:T(8,128)}, bf16[256,1024]{1,0:T(8,128)(2,1)}, bf16[8,128,128]{2,1,0:T(8,128)(2,1)}) custom-call(f32[8]{0:T(128)} %get-tuple-element.216.rate, bf16[512,1024]{1,0:T(8,128)(2,1)} %x.9, f32[512,1024]{1,0:T(8,128)} %get-tuple-element.71.intra, ...), custom_call_target="tpu_custom_call" | custom-call | flops 603979776 | bytes 8388608 | tf_op jit(solution)/shard_map/pallas_call | solution.py:338
  64.1 4.6 %collective-permute-done.17.n0.refs_21_ = bf16[256,1024]{1,0:T(8,128)(2,1)S(1)} collective-permute-done((bf16[256,1024]{1,0:T(8,128)(2,1)}, bf16[256,1024]{1,0:T(8,128)(2,1)S(1)}, u32[]{:S(2)}, u32[]{:S(2)}) %collective-permute-start.17) | collective-permute-done | bytes 524320 | tf_op jit(solution)/shard_map/ppermute | solution.py:25
  68.7 2.3 collective-permute-start.6
  72.0 9.8 %shard_map.192 = (f32[2,256,1024]{2,1,0:T(8,128)}, bf16[2,256,1024]{2,1,0:T(8,128)(2,1)}, bf16[512,704]{1,0:T(8,128)(2,1)}, bf16[512,704]{1,0:T(8,128)(2,1)}, bf16[512,704]{1,0:T(8,128)(2,1)}) custom-call(bf16[256,1024]{1,0:T(8,128)(2,1)} %get-tuple-element.84.n0.refs_7_, bf16[256,1024]{1,0:T(8,128)(2,1)} %collective-permute-done.15.n1.refs_8_, ...), custom_call_target="tpu_custom_call" | custom-call | flops 4429185024 | bytes 9568256 | tf_op jit(solution)/shard_map/pallas_call | solution.py:380
  82.3 9.9 %shard_map.189 = (f32[2,256,1024]{2,1,0:T(8,128)}, bf16[2,256,1024]{2,1,0:T(8,128)(2,1)}, bf16[512,704]{1,0:T(8,128)(2,1)}, bf16[512,704]{1,0:T(8,128)(2,1)}, bf16[512,704]{1,0:T(8,128)(2,1)}) custom-call(bf16[256,1024]{1,0:T(8,128)(2,1)} %get-tuple-element.77.n0.refs_0_, bf16[256,1024]{1,0:T(8,128)(2,1)} %collective-permute-done.6.n1.refs_1_, ...), custom_call_target="tpu_custom_call" | custom-call | flops 4429185024 | bytes 9568256 | tf_op jit(solution)/shard_map/pallas_call | solution.py:380
  93.7 10.2 %shard_map.193 = (f32[2,256,1024]{2,1,0:T(8,128)}, bf16[2,256,1024]{2,1,0:T(8,128)(2,1)}, bf16[512,704]{1,0:T(8,128)(2,1)}, bf16[512,704]{1,0:T(8,128)(2,1)}, bf16[512,704]{1,0:T(8,128)(2,1)}) custom-call(bf16[256,1024]{1,0:T(8,128)(2,1)} %copy-done.19, bf16[256,1024]{1,0:T(8,128)(2,1)} %collective-permute-done.18.n1.refs_22_, ...), custom_call_target="tpu_custom_call" | custom-call | flops 4429185024 | bytes 9568256 | tf_op jit(solution)/shard_map/pallas_call | solution.py:380
  104.8 9.9 %shard_map.190 = (f32[2,256,1024]{2,1,0:T(8,128)}, bf16[2,256,1024]{2,1,0:T(8,128)(2,1)}, bf16[512,704]{1,0:T(8,128)(2,1)}, bf16[512,704]{1,0:T(8,128)(2,1)}, bf16[512,704]{1,0:T(8,128)(2,1)}) custom-call(bf16[256,1024]{1,0:T(8,128)(2,1)} %collective-permute-done.9.n0.refs_14_, bf16[256,1024]{1,0:T(8,128)(2,1)} %copy-done.20, ...), custom_call_target="tpu_custom_call" | custom-call | flops 4429185024 | bytes 9568256 | tf_op jit(solution)/shard_map/pallas_call | solution.py:380
  115.1 14.7 %shard_map.202 = (bf16[8,2,704,128]{3,2,1,0:T(8,128)(2,1)}, bf16[8,704,128]{2,1,0:T(8,128)(2,1)}) custom-call(s32[1]{0:T(128)} %bitcast.95.place, bf16[256,1024]{1,0:T(8,128)(2,1)} %get-tuple-element.77.n0.refs_0_, bf16[256,1024]{1,0:T(8,128)(2,1)} %collective-permute-done.6.n1.refs_1_, bf16[512,1024]{1,0:T(8,128)(2,1)} %refs_9_, ...), custom_call_target="tpu_custom_call" | custom-call | flops 8858370048 | bytes 21364736 | tf_op jit(solution)/shard_map/pallas_call | solution.py:464
  129.9 2.0 slice.137
  132.5 2.7 fusion.14
  137.4 2.7 fusion.13
  140.4 2.4 pad_maximum_fusion.2.refs_0_
  143.9 6.0 %collective-permute-done.79 = bf16[4,704,128]{2,1,0:T(8,128)(2,1)} collective-permute-done((bf16[4,704,128]{2,1,0:T(8,128)(2,1)}, bf16[4,704,128]{2,1,0:T(8,128)(2,1)}, u32[]{:S(2)}, u32[]{:S(2)}) %collective-permute-start.79) | collective-permute-done | bytes 720928 | tf_op jit(solution)/shard_map/ppermute | solution.py:25
  152.6 2.4 collective-permute-start.80
  156.2 6.1 %shard_map.195 = (f32[256,1024]{1,0:T(8,128)}, bf16[256,1024]{1,0:T(8,128)(2,1)}, bf16[256,1024]{1,0:T(8,128)(2,1)}, bf16[256,1024]{1,0:T(8,128)(2,1)}, f32[8,128,128]{2,1,0:T(8,128)}) custom-call(f32[8]{0:T(128)} %get-tuple-element.216.rate, f32[2,256,1024]{2,1,0:T(8,128)} %get-tuple-element.85.keep, bf16[2,256,1024]{2,1,0:T(8,128)(2,1)} %collective-permute-done.16.got, ...), custom_call_target="tpu_custom_call" | custom-call | flops 603979776 | bytes 10485760 | tf_op jit(solution)/shard_map/pallas_call | solution.py:512
  163.4 6.2 %shard_map.194 = (f32[256,1024]{1,0:T(8,128)}, bf16[256,1024]{1,0:T(8,128)(2,1)}, bf16[256,1024]{1,0:T(8,128)(2,1)}, bf16[256,1024]{1,0:T(8,128)(2,1)}, f32[8,128,128]{2,1,0:T(8,128)}) custom-call(f32[8]{0:T(128)} %get-tuple-element.216.rate, f32[2,256,1024]{2,1,0:T(8,128)} %get-tuple-element.79.keep, bf16[2,256,1024]{2,1,0:T(8,128)(2,1)} %collective-permute-done.8.got, ...), custom_call_target="tpu_custom_call" | custom-call | flops 603979776 | bytes 10485760 | tf_op jit(solution)/shard_map/pallas_call | solution.py:512
  175.0 11.3 %collective-permute-done.81 = bf16[1,704,128]{2,1,0:T(8,128)(2,1)S(1)} collective-permute-done((bf16[1,704,128]{2,1,0:T(8,128)(2,1)S(1)}, bf16[1,704,128]{2,1,0:T(8,128)(2,1)S(1)}, u32[]{:S(2)}, u32[]{:S(2)}) %collective-permute-start.81) | collective-permute-done | bytes 180256 | tf_op jit(solution)/shard_map/ppermute | solution.py:25
  192.6 10.3 %shard_map.196 = (bf16[512,1024]{1,0:T(8,128)(2,1)}, f32[512,1024]{1,0:T(8,128)}, f32[512,1024]{1,0:T(8,128)}) custom-call(f32[8]{0:T(128)} %get-tuple-element.216.rate, f32[512,1024]{1,0:T(8,128)} %get-tuple-element.91.pre_query, bf16[512,1024]{1,0:T(8,128)(2,1)} %get-tuple-element.72.query, bf16[512,1024]{1,0:T(8,128)(2,1)} %get-tuple-element.69.keys, ...), custom_call_target="tpu_custom_call" | custom-call | flops 1610612736 | bytes 12582912 | tf_op jit(solution)/shard_map/pallas_call | solution.py:558
  202.9 5.9 %collective-permute-done.26 = bf16[4,128,128]{2,1,0:T(8,128)(2,1)} collective-permute-done((bf16[4,128,128]{2,1,0:T(8,128)(2,1)}, bf16[4,128,128]{2,1,0:T(8,128)(2,1)}, u32[]{:S(2)}, u32[]{:S(2)}) %collective-permute-start.26) | collective-permute-done | bytes 131104 | tf_op jit(solution)/shard_map/ppermute | solution.py:25
  210.5 2.8 collective-permute-start.27
  213.3 7.6 %shard_map.200 = bf16[2,3,512,1024]{3,2,1,0:T(8,128)(2,1)} custom-call(s32[1]{0:T(128)} %bitcast.30.core, bf16[512,1024]{1,0:T(8,128)(2,1)} %pad_maximum_fusion.2.refs_0_, bf16[512,1024]{1,0:T(8,128)(2,1)} %get-tuple-element.68.rows.refs_1_.refs_0_, bf16[256,1024]{1,0:T(8,128)(2,1)} %get-tuple-element.110.refs_2_, ...), custom_call_target="tpu_custom_call" | custom-call | flops 3221225472 | bytes 12582912 | tf_op jit(solution)/shard_map/pallas_call | solution.py:645
  222.1 3.2 collective-permute-start.28
  225.3 3.9 slice_bitcast_fusion
  230.2 5.7 %shard_map.197 = (bf16[512,1024]{1,0:T(8,128)(2,1)}, bf16[512,1024]{1,0:T(8,128)(2,1)}) custom-call(f32[8]{0:T(128)} %get-tuple-element.216.rate, f32[512,1024]{1,0:T(8,128)} %get-tuple-element.98.pre_key, bf16[512,1024]{1,0:T(8,128)(2,1)} %get-tuple-element.69.keys, bf16[512,1024]{1,0:T(8,128)(2,1)} %get-tuple-element.70.values, ...), custom_call_target="tpu_custom_call" | custom-call | flops 268435456 | bytes 10485760 | tf_op jit(solution)/shard_map/pallas_call | solution.py:605
  235.9 6.0 %shard_map.201 = bf16[2,2,512,1024]{3,2,1,0:T(8,128)(2,1)} custom-call(s32[1]{0:T(128)} %bitcast.30.core, bf16[512,1024]{1,0:T(8,128)(2,1)} %get-tuple-element.68.rows.refs_1_.refs_0_, bf16[512,1024]{1,0:T(8,128)(2,1)} %get-tuple-element.103.kb.refs_1_, bf16[512,1024]{1,0:T(8,128)(2,1)} %get-tuple-element.104.vb.refs_2_), custom_call_target="tpu_custom_call" | custom-call | flops 2147483648 | bytes 8388608 | tf_op jit(solution)/shard_map/pallas_call | solution.py:645
  242.0 3.2 slice_bitcast_fusion.2
  250.5 8.1 %shard_map.199 = f32[256,1024]{1,0:T(8,128)} custom-call(bf16[512,1024]{1,0:T(8,128)(2,1)} %x.9, f32[256,1024]{1,0:T(8,128)} %get-tuple-element.106.rc, bf16[512,1024]{1,0:T(8,128)(2,1)} %get-tuple-element.97.qb.refs_6_, bf16[512,1024]{1,0:T(8,128)(2,1)} %get-tuple-element.103.kb.refs_1_, bf16[512,1024]{1,0:T(8,128)(2,1)} %get-tuple-element.104.vb.refs_2_, ...), custom_call_target="tpu_custom_call" | custom-call | flops 2147483648 | bytes 13631488 | tf_op jit(solution)/shard_map/pallas_call | solution.py:667
  258.6 8.1 %shard_map.198 = f32[256,1024]{1,0:T(8,128)} custom-call(bf16[512,1024]{1,0:T(8,128)(2,1)} %x.9, f32[256,1024]{1,0:T(8,128)} %get-tuple-element.90.rc, bf16[512,1024]{1,0:T(8,128)(2,1)} %get-tuple-element.97.qb.refs_6_, bf16[512,1024]{1,0:T(8,128)(2,1)} %get-tuple-element.103.kb.refs_1_, bf16[512,1024]{1,0:T(8,128)(2,1)} %get-tuple-element.104.vb.refs_2_, ...), custom_call_target="tpu_custom_call" | custom-call | flops 2147483648 | bytes 13631488 | tf_op jit(solution)/shard_map/pallas_call | solution.py:667
  266.7 2.9 pad_maximum_fusion
  270.7 3.2 fusion.1
  275.7 3.4 fusion
  282.3 5.0 %collective-permute-done.40 = bf16[256,1024]{1,0:T(8,128)(2,1)S(1)} collective-permute-done((bf16[256,1024]{1,0:T(8,128)(2,1)S(1)}, bf16[256,1024]{1,0:T(8,128)(2,1)S(1)}, u32[]{:S(2)}, u32[]{:S(2)}) %collective-permute-start.40) | collective-permute-done | bytes 524320 | tf_op jit(solution)/shard_map/ppermute | solution.py:25
  289.7 2.4 collective-permute-done.30
  292.3 2.2 collective-permute-start.31
  294.5 10.6 %collective-permute-done.41 = bf16[128,1024]{1,0:T(8,128)(2,1)S(1)} collective-permute-done((bf16[128,1024]{1,0:T(8,128)(2,1)S(1)}, bf16[128,1024]{1,0:T(8,128)(2,1)S(1)}, u32[]{:S(2)}, u32[]{:S(2)}) %collective-permute-start.41) | collective-permute-done | bytes 262176 | tf_op jit(solution)/shard_map/ppermute | solution.py:25
  306.5 2.1 collective-permute-start.51
  313.7 4.9 %collective-permute-done.43 = bf16[32,1024]{1,0:T(8,128)(2,1)S(1)} collective-permute-done((bf16[32,1024]{1,0:T(8,128)(2,1)S(1)}, bf16[32,1024]{1,0:T(8,128)(2,1)S(1)}, u32[]{:S(2)}, u32[]{:S(2)}) %collective-permute-start.43) | collective-permute-done | bytes 65568 | tf_op jit(solution)/shard_map/ppermute | solution.py:25
  318.6 2.9 collective-permute-start.44
  329.5 2.9 collective-permute-done.54
  332.6 2.5 collective-permute-done.60
  336.3 2.3 collective-permute-done.61
  340.2 2.7 collective-permute-start.71
  344.8 3.1 collective-permute-start.72
  348.2 4.3 %collective-permute-start.47 = (bf16[256,1024]{1,0:T(8,128)(2,1)S(1)}, bf16[256,1024]{1,0:T(8,128)(2,1)S(1)}, u32[]{:S(2)}, u32[]{:S(2)}) collective-permute-start(bf16[256,1024]{1,0:T(8,128)(2,1)S(1)} %pad_maximum_fusion.11), channel_id=1, source_target_pairs={{0,2},{1,3},{2,0},{3,1},{4,6},{5,7},{6,4},{7,5},{8,10},{9,11},{10,... | collective-permute-start | bytes 1572872 | tf_op jit(solution)/shard_map/ppermute | solution.py:25
  354.5 6.1 %collective-permute-done.36 = bf16[128,1024]{1,0:T(8,128)(2,1)S(1)} collective-permute-done((bf16[128,1024]{1,0:T(8,128)(2,1)S(1)}, bf16[128,1024]{1,0:T(8,128)(2,1)S(1)}, u32[]{:S(2)}, u32[]{:S(2)}) %collective-permute-start.36) | collective-permute-done | bytes 262176 | tf_op jit(solution)/shard_map/ppermute | solution.py:25
  360.9 3.5 collective-permute-done.64
  365.4 17.0 %collective-permute-start.48 = (bf16[512,1024]{1,0:T(8,128)(2,1)S(1)}, bf16[512,1024]{1,0:T(8,128)(2,1)S(1)}, u32[]{:S(2)}, u32[]{:S(2)}) collective-permute-start(bf16[512,1024]{1,0:T(8,128)(2,1)S(1)} %pad_maximum_fusion.4), channel_id=1, source_target_pairs={{0,1},{1,0},{2,3},{3,2},{4,5},{5,4},{6,7},{7,6},{8,9},{9,8},{10,11... | collective-permute-start | bytes 3145736 | tf_op jit(solution)/shard_map/ppermute | solution.py:25
  384.0 3.7 collective-permute-start.66
  388.1 3.5 collective-permute-start.75
  392.1 2.5 maximum_convert_fusion.1
  395.2 2.4 maximum_convert_fusion.2
  398.2 2.4 maximum_convert_fusion
  401.3 2.4 maximum_convert_fusion.3
  404.3 2.4 maximum_convert_fusion.4
  (305 shorter events, 86.5 us)
Async XLA Ops:
  32.0 25.5 %collective-permute-start.11 = (bf16[512,1024]{1,0:T(8,128)(2,1)S(1)}, bf16[512,1024]{1,0:T(8,128)(2,1)}, u32[]{:S(2)}, u32[]{:S(2)}) collective-permute-start(bf16[512,1024]{1,0:T(8,128)(2,1)S(1)} %copy-done.2), channel_id=1, source_target_pairs={{0,2},{1,3},{2,0},{3,1},{4,6},{5,7},{6,4},{7,5},{8,10},{9,11},{10,... | collective-permute-start | bytes 3145736 | tf_op jit(solution)/shard_map/ppermute | solution.py:25
  36.5 12.7 %collective-permute-start.5 = (bf16[4,128,128]{2,1,0:T(8,128)(2,1)S(1)}, bf16[4,128,128]{2,1,0:T(8,128)(2,1)S(1)}, u32[]{:S(2)}, u32[]{:S(2)}) collective-permute-start(bf16[4,128,128]{2,1,0:T(8,128)(2,1)S(1)} %get-tuple-element.132), channel_id=1, source_target_pairs={{0,1},{1,0},{2,3},{3,2},{4,5},{5,4},{6,7},{7,6},{8,9},{9,8},{10,11... | collective-permute-start | bytes 393224 | tf_op jit(solution)/shard_map/ppermute | solution.py:25
  49.1 21.9 %collective-permute-start.7 = (bf16[512,1024]{1,0:T(8,128)(2,1)S(1)}, bf16[512,1024]{1,0:T(8,128)(2,1)S(1)}, u32[]{:S(2)}, u32[]{:S(2)}) collective-permute-start(bf16[512,1024]{1,0:T(8,128)(2,1)S(1)} %copy-done.2), channel_id=1, source_target_pairs={{0,1},{1,0},{2,3},{3,2},{4,5},{5,4},{6,7},{7,6},{8,9},{9,8},{10,11... | collective-permute-start | bytes 3145736 | tf_op jit(solution)/shard_map/ppermute | solution.py:25
  55.5 13.2 %collective-permute-start.17 = (bf16[256,1024]{1,0:T(8,128)(2,1)}, bf16[256,1024]{1,0:T(8,128)(2,1)S(1)}, u32[]{:S(2)}, u32[]{:S(2)}) collective-permute-start(bf16[256,1024]{1,0:T(8,128)(2,1)} %get-tuple-element.84.n0.refs_7_), channel_id=1, source_target_pairs={{0,2},{1,3},{2,0},{3,1},{4,6},{5,7},{6,4},{7,5},{8,10},{9,11},{10,... | collective-permute-start | bytes 1572872 | tf_op jit(solution)/shard_map/ppermute | solution.py:25
  56.7 14.2 %collective-permute-start.15 = (bf16[256,1024]{1,0:T(8,128)(2,1)}, bf16[256,1024]{1,0:T(8,128)(2,1)}, u32[]{:S(2)}, u32[]{:S(2)}) collective-permute-start(bf16[256,1024]{1,0:T(8,128)(2,1)} %get-tuple-element.84.n0.refs_7_), channel_id=1, source_target_pairs={{0,1},{1,0},{2,3},{3,2},{4,5},{5,4},{6,7},{7,6},{8,9},{9,8},{10,11... | collective-permute-start | bytes 1572872 | tf_op jit(solution)/shard_map/ppermute | solution.py:25
  57.5 35.2 %collective-permute-start.12 = (bf16[512,1024]{1,0:T(8,128)(2,1)}, bf16[512,1024]{1,0:T(8,128)(2,1)S(1)}, u32[]{:S(2)}, u32[]{:S(2)}) collective-permute-start(bf16[512,1024]{1,0:T(8,128)(2,1)} %collective-permute-done.11.c0.refs_16_.refs_23_), channel_id=1, source_target_pairs={{0,1},{1,0},{2,3},{3,2},{4,5},{5,4},{6,7},{7,6},{8,9},{9,8},{10,11... | collective-permute-start | bytes 3145736 | tf_op jit(solution)/shard_map/ppermute | solution.py:25
  62.9 19.4 %collective-permute-start.9 = (bf16[256,1024]{1,0:T(8,128)(2,1)}, bf16[256,1024]{1,0:T(8,128)(2,1)}, u32[]{:S(2)}, u32[]{:S(2)}) collective-permute-start(bf16[256,1024]{1,0:T(8,128)(2,1)} %get-tuple-element.77.n0.refs_0_), channel_id=1, source_target_pairs={{0,2},{1,3},{2,0},{3,1},{4,6},{5,7},{6,4},{7,5},{8,10},{9,11},{10,... | collective-permute-start | bytes 1572872 | tf_op jit(solution)/shard_map/ppermute | solution.py:25
  68.7 13.7 %collective-permute-start.6 = (bf16[256,1024]{1,0:T(8,128)(2,1)}, bf16[256,1024]{1,0:T(8,128)(2,1)}, u32[]{:S(2)}, u32[]{:S(2)}) collective-permute-start(bf16[256,1024]{1,0:T(8,128)(2,1)} %get-tuple-element.77.n0.refs_0_), channel_id=1, source_target_pairs={{0,1},{1,0},{2,3},{3,2},{4,5},{5,4},{6,7},{7,6},{8,9},{9,8},{10,11... | collective-permute-start | bytes 1572872 | tf_op jit(solution)/shard_map/ppermute | solution.py:25
  70.9 21.7 %collective-permute-start.18 = (bf16[256,1024]{1,0:T(8,128)(2,1)S(1)}, bf16[256,1024]{1,0:T(8,128)(2,1)}, u32[]{:S(2)}, u32[]{:S(2)}) collective-permute-start(bf16[256,1024]{1,0:T(8,128)(2,1)S(1)} %collective-permute-done.17.n0.refs_21_), channel_id=1, source_target_pairs={{0,1},{1,0},{2,3},{3,2},{4,5},{5,4},{6,7},{7,6},{8,9},{9,8},{10,11... | collective-permute-start | bytes 1572872 | tf_op jit(solution)/shard_map/ppermute | solution.py:25
  81.8 70.8 %collective-permute-start.16 = (bf16[2,256,1024]{2,1,0:T(8,128)(2,1)}, bf16[2,256,1024]{2,1,0:T(8,128)(2,1)}, u32[]{:S(2)}, u32[]{:S(2)}) collective-permute-start(bf16[2,256,1024]{2,1,0:T(8,128)(2,1)} %get-tuple-element.86), channel_id=1, source_target_pairs={{0,1},{1,0},{2,3},{3,2},{4,5},{5,4},{6,7},{7,6},{8,9},{9,8},{10,11... | collective-permute-start | bytes 3145736 | tf_op jit(solution)/shard_map/ppermute | solution.py:25
  82.3 21.7 %collective-permute-start.10 = (bf16[256,1024]{1,0:T(8,128)(2,1)}, bf16[256,1024]{1,0:T(8,128)(2,1)S(1)}, u32[]{:S(2)}, u32[]{:S(2)}) collective-permute-start(bf16[256,1024]{1,0:T(8,128)(2,1)} %collective-permute-done.9.n0.refs_14_), channel_id=1, source_target_pairs={{0,1},{1,0},{2,3},{3,2},{4,5},{5,4},{6,7},{7,6},{8,9},{9,8},{10,11... | collective-permute-start | bytes 1572872 | tf_op jit(solution)/shard_map/ppermute | solution.py:25
  92.2 70.1 %collective-permute-start.8 = (bf16[2,256,1024]{2,1,0:T(8,128)(2,1)}, bf16[2,256,1024]{2,1,0:T(8,128)(2,1)}, u32[]{:S(2)}, u32[]{:S(2)}) collective-permute-start(bf16[2,256,1024]{2,1,0:T(8,128)(2,1)} %get-tuple-element.80), channel_id=1, source_target_pairs={{0,1},{1,0},{2,3},{3,2},{4,5},{5,4},{6,7},{7,6},{8,9},{9,8},{10,11... | collective-permute-start | bytes 3145736 | tf_op jit(solution)/shard_map/ppermute | solution.py:25
  103.9 28.6 %collective-permute-start.19 = (bf16[2,256,1024]{2,1,0:T(8,128)(2,1)}, bf16[2,256,1024]{2,1,0:T(8,128)(2,1)}, u32[]{:S(2)}, u32[]{:S(2)}) collective-permute-start(bf16[2,256,1024]{2,1,0:T(8,128)(2,1)} %get-tuple-element.88), channel_id=1, source_target_pairs={{0,1},{1,0},{2,3},{3,2},{4,5},{5,4},{6,7},{7,6},{8,9},{9,8},{10,11... | collective-permute-start | bytes 3145736 | tf_op jit(solution)/shard_map/ppermute | solution.py:25
  114.7 21.7 %collective-permute-start.13 = (bf16[2,256,1024]{2,1,0:T(8,128)(2,1)}, bf16[2,256,1024]{2,1,0:T(8,128)(2,1)S(1)}, u32[]{:S(2)}, u32[]{:S(2)}) collective-permute-start(bf16[2,256,1024]{2,1,0:T(8,128)(2,1)} %get-tuple-element.82), channel_id=1, source_target_pairs={{0,1},{1,0},{2,3},{3,2},{4,5},{5,4},{6,7},{7,6},{8,9},{9,8},{10,11... | collective-permute-start | bytes 3145736 | tf_op jit(solution)/shard_map/ppermute | solution.py:25
  131.9 18.0 %collective-permute-start.79 = (bf16[4,704,128]{2,1,0:T(8,128)(2,1)}, bf16[4,704,128]{2,1,0:T(8,128)(2,1)}, u32[]{:S(2)}, u32[]{:S(2)}) collective-permute-start(bf16[4,704,128]{2,1,0:T(8,128)(2,1)} %slice.137), channel_id=1, source_target_pairs={{0,8},{1,9},{2,10},{3,11},{4,12},{5,13},{6,14},{7,15},{8,0},{9,1},... | collective-permute-start | bytes 2162696 | tf_op jit(solution)/shard_map/ppermute | solution.py:25
  135.2 19.8 %collective-permute-start.22 = (bf16[256,1024]{1,0:T(8,128)(2,1)}, bf16[256,1024]{1,0:T(8,128)(2,1)}, u32[]{:S(2)}, u32[]{:S(2)}) collective-permute-start(bf16[256,1024]{1,0:T(8,128)(2,1)} %get-tuple-element.141), channel_id=1, source_target_pairs={{0,2},{1,3},{2,0},{3,1},{4,6},{5,7},{6,4},{7,5},{8,10},{9,11},{10,... | collective-permute-start | bytes 1572872 | tf_op jit(solution)/shard_map/ppermute | solution.py:25
  140.1 22.5 %collective-permute-start.21 = (bf16[256,1024]{1,0:T(8,128)(2,1)}, bf16[256,1024]{1,0:T(8,128)(2,1)S(1)}, u32[]{:S(2)}, u32[]{:S(2)}) collective-permute-start(bf16[256,1024]{1,0:T(8,128)(2,1)} %get-tuple-element.139), channel_id=1, source_target_pairs={{0,2},{1,3},{2,0},{3,1},{4,6},{5,7},{6,4},{7,5},{8,10},{9,11},{10,... | collective-permute-start | bytes 1572872 | tf_op jit(solution)/shard_map/ppermute | solution.py:25
  149.9 38.6 %collective-permute-start.76 = (bf16[4,2,704,128]{3,2,1,0:T(8,128)(2,1)}, bf16[4,2,704,128]{3,2,1,0:T(8,128)(2,1)}, u32[]{:S(2)}, u32[]{:S(2)}) collective-permute-start(bf16[4,2,704,128]{3,2,1,0:T(8,128)(2,1)} %slice.129), channel_id=1, source_target_pairs={{0,4},{1,5},{2,6},{3,7},{4,0},{5,1},{6,2},{7,3},{8,12},{9,13},{10,... | collective-permute-start | bytes 4325384 | tf_op jit(solution)/shard_map/ppermute | solution.py:25
  152.6 20.0 %collective-permute-start.80 = (bf16[2,704,128]{2,1,0:T(8,128)(2,1)S(1)}, bf16[2,704,128]{2,1,0:T(8,128)(2,1)S(1)}, u32[]{:S(2)}, u32[]{:S(2)}) collective-permute-start(bf16[2,704,128]{2,1,0:T(8,128)(2,1)S(1)} %slice.164), channel_id=1, source_target_pairs={{0,16},{1,17},{2,18},{3,19},{4,20},{5,21},{6,22},{7,23},{8,24},{9,... | collective-permute-start | bytes 1081352 | tf_op jit(solution)/shard_map/ppermute | solution.py:25
  155.0 90.7 %collective-permute-start.20 = (bf16[256,1024]{1,0:T(8,128)(2,1)}, bf16[256,1024]{1,0:T(8,128)(2,1)}, u32[]{:S(2)}, u32[]{:S(2)}) collective-permute-start(bf16[256,1024]{1,0:T(8,128)(2,1)} %get-tuple-element.142), channel_id=1, source_target_pairs={{0,2},{1,3},{2,0},{3,1},{4,6},{5,7},{6,4},{7,5},{8,10},{9,11},{10,... | collective-permute-start | bytes 1572872 | tf_op jit(solution)/shard_map/ppermute | solution.py:25
  162.3 85.2 %collective-permute-start.14 = (bf16[256,1024]{1,0:T(8,128)(2,1)}, bf16[256,1024]{1,0:T(8,128)(2,1)}, u32[]{:S(2)}, u32[]{:S(2)}) collective-permute-start(bf16[256,1024]{1,0:T(8,128)(2,1)} %get-tuple-element.140), channel_id=1, source_target_pairs={{0,2},{1,3},{2,0},{3,1},{4,6},{5,7},{6,4},{7,5},{8,10},{9,11},{10,... | collective-permute-start | bytes 1572872 | tf_op jit(solution)/shard_map/ppermute | solution.py:25
  172.7 13.5 %collective-permute-start.81 = (bf16[1,704,128]{2,1,0:T(8,128)(2,1)S(1)}, bf16[1,704,128]{2,1,0:T(8,128)(2,1)S(1)}, u32[]{:S(2)}, u32[]{:S(2)}) collective-permute-start(bf16[1,704,128]{2,1,0:T(8,128)(2,1)S(1)} %slice.166), channel_id=1, source_target_pairs={{0,4},{1,5},{2,6},{3,7},{4,0},{5,1},{6,2},{7,3},{8,12},{9,13},{10,... | collective-permute-start | bytes 540680 | tf_op jit(solution)/shard_map/ppermute | solution.py:25
  173.7 13.3 %collective-permute-start.24 = (bf16[4,128,128]{2,1,0:T(8,128)(2,1)S(1)}, bf16[4,128,128]{2,1,0:T(8,128)(2,1)S(1)}, u32[]{:S(2)}, u32[]{:S(2)}) collective-permute-start(bf16[4,128,128]{2,1,0:T(8,128)(2,1)S(1)} %fusion.73), channel_id=1, source_target_pairs={{0,2},{1,3},{2,0},{3,1},{4,6},{5,7},{6,4},{7,5},{8,10},{9,11},{10,... | collective-permute-start | bytes 393224 | tf_op jit(solution)/shard_map/ppermute | solution.py:25
  190.3 59.9 %collective-permute-start.77 = (bf16[2,2,704,128]{3,2,1,0:T(8,128)(2,1)S(1)}, bf16[2,2,704,128]{3,2,1,0:T(8,128)(2,1)S(1)}, u32[]{:S(2)}, u32[]{:S(2)}) collective-permute-start(bf16[2,2,704,128]{3,2,1,0:T(8,128)(2,1)S(1)} %slice.158), channel_id=1, source_target_pairs={{0,8},{1,9},{2,10},{3,11},{4,12},{5,13},{6,14},{7,15},{8,0},{9,1},... | collective-permute-start | bytes 2162696 | tf_op jit(solution)/shard_map/ppermute | solution.py:25
  191.8 17.0 %collective-permute-start.26 = (bf16[4,128,128]{2,1,0:T(8,128)(2,1)}, bf16[4,128,128]{2,1,0:T(8,128)(2,1)}, u32[]{:S(2)}, u32[]{:S(2)}) collective-permute-start(bf16[4,128,128]{2,1,0:T(8,128)(2,1)} %fusion.61), channel_id=1, source_target_pairs={{0,8},{1,9},{2,10},{3,11},{4,12},{5,13},{6,14},{7,15},{8,0},{9,1},... | collective-permute-start | bytes 393224 | tf_op jit(solution)/shard_map/ppermute | solution.py:25
  210.5 10.4 %collective-permute-start.27 = (bf16[4,128,128]{2,1,0:T(8,128)(2,1)}, bf16[4,128,128]{2,1,0:T(8,128)(2,1)S(1)}, u32[]{:S(2)}, u32[]{:S(2)}) collective-permute-start(bf16[4,128,128]{2,1,0:T(8,128)(2,1)} %fusion.50), channel_id=1, source_target_pairs={{0,16},{1,17},{2,18},{3,19},{4,20},{5,21},{6,22},{7,23},{8,24},{9,... | collective-permute-start | bytes 393224 | tf_op jit(solution)/shard_map/ppermute | solution.py:25
  222.1 7.1 %collective-permute-start.28 = (bf16[4,128,128]{2,1,0:T(8,128)(2,1)S(1)}, bf16[4,128,128]{2,1,0:T(8,128)(2,1)S(1)}, u32[]{:S(2)}, u32[]{:S(2)}) collective-permute-start(bf16[4,128,128]{2,1,0:T(8,128)(2,1)S(1)} %get-tuple-element.126), channel_id=1, source_target_pairs={{0,1},{1,0},{2,3},{3,2},{4,5},{5,4},{6,7},{7,6},{8,9},{9,8},{10,11... | collective-permute-start | bytes 393224 | tf_op jit(solution)/shard_map/ppermute | solution.py:25
  229.2 46.5 %collective-permute-start.29 = (bf16[3,512,1024]{2,1,0:T(8,128)(2,1)}, bf16[3,512,1024]{2,1,0:T(8,128)(2,1)}, u32[]{:S(2)}, u32[]{:S(2)}) collective-permute-start(bf16[3,512,1024]{2,1,0:T(8,128)(2,1)} %slice_bitcast_fusion), channel_id=1, source_target_pairs={{0,1},{1,0},{2,3},{3,2},{4,5},{5,4},{6,7},{7,6},{8,9},{9,8},{10,11... | collective-permute-start | bytes 9437192 | tf_op jit(solution)/shard_map/ppermute | solution.py:25
  245.2 25.5 %collective-permute-start.39 = (bf16[2,512,1024]{2,1,0:T(8,128)(2,1)}, bf16[2,512,1024]{2,1,0:T(8,128)(2,1)}, u32[]{:S(2)}, u32[]{:S(2)}) collective-permute-start(bf16[2,512,1024]{2,1,0:T(8,128)(2,1)} %slice_bitcast_fusion.2), channel_id=1, source_target_pairs={{0,1},{1,0},{2,3},{3,2},{4,5},{5,4},{6,7},{7,6},{8,9},{9,8},{10,11... | collective-permute-start | bytes 6291464 | tf_op jit(solution)/shard_map/ppermute | solution.py:25
  250.4 19.3 %collective-permute-start.78 = (bf16[1,2,704,128]{3,2,1,0:T(8,128)(2,1)S(1)}, bf16[1,2,704,128]{3,2,1,0:T(8,128)(2,1)S(1)}, u32[]{:S(2)}, u32[]{:S(2)}) collective-permute-start(bf16[1,2,704,128]{3,2,1,0:T(8,128)(2,1)S(1)} %slice.160), channel_id=1, source_target_pairs={{0,16},{1,17},{2,18},{3,19},{4,20},{5,21},{6,22},{7,23},{8,24},{9,... | collective-permute-start | bytes 1081352 | tf_op jit(solution)/shard_map/ppermute | solution.py:25
  274.1 13.2 %collective-permute-start.40 = (bf16[256,1024]{1,0:T(8,128)(2,1)S(1)}, bf16[256,1024]{1,0:T(8,128)(2,1)S(1)}, u32[]{:S(2)}, u32[]{:S(2)}) collective-permute-start(bf16[256,1024]{1,0:T(8,128)(2,1)S(1)} %dynamic-slice_bitcast_fusion.3), channel_id=1, source_target_pairs={{0,2},{1,3},{2,0},{3,1},{4,6},{5,7},{6,4},{7,5},{8,10},{9,11},{10,... | collective-permute-start | bytes 1572872 | tf_op jit(solution)/shard_map/ppermute | solution.py:25
  275.4 12.9 %collective-permute-start.49 = (bf16[256,1024]{1,0:T(8,128)(2,1)S(1)}, bf16[256,1024]{1,0:T(8,128)(2,1)S(1)}, u32[]{:S(2)}, u32[]{:S(2)}) collective-permute-start(bf16[256,1024]{1,0:T(8,128)(2,1)S(1)} %dynamic-slice_bitcast_fusion.2), channel_id=1, source_target_pairs={{0,4},{1,5},{2,6},{3,7},{4,0},{5,1},{6,2},{7,3},{8,12},{9,13},{10,... | collective-permute-start | bytes 1572872 | tf_op jit(solution)/shard_map/ppermute | solution.py:25
  279.5 12.6 %collective-permute-start.30 = (bf16[256,1024]{1,0:T(8,128)(2,1)S(1)}, bf16[256,1024]{1,0:T(8,128)(2,1)S(1)}, u32[]{:S(2)}, u32[]{:S(2)}) collective-permute-start(bf16[256,1024]{1,0:T(8,128)(2,1)S(1)} %dynamic-slice_bitcast_fusion.4), channel_id=1, source_target_pairs={{0,8},{1,9},{2,10},{3,11},{4,12},{5,13},{6,14},{7,15},{8,0},{9,1},... | collective-permute-start | bytes 1572872 | tf_op jit(solution)/shard_map/ppermute | solution.py:25
  280.7 28.0 %collective-permute-start.58 = (bf16[256,1024]{1,0:T(8,128)(2,1)S(1)}, bf16[256,1024]{1,0:T(8,128)(2,1)S(1)}, u32[]{:S(2)}, u32[]{:S(2)}) collective-permute-start(bf16[256,1024]{1,0:T(8,128)(2,1)S(1)} %dynamic-slice_bitcast_fusion.1), channel_id=1, source_target_pairs={{0,4},{1,5},{2,6},{3,7},{4,0},{5,1},{6,2},{7,3},{8,12},{9,13},{10,... | collective-permute-start | bytes 1572872 | tf_op jit(solution)/shard_map/ppermute | solution.py:25
  282.0 27.3 %collective-permute-start.67 = (bf16[256,1024]{1,0:T(8,128)(2,1)S(1)}, bf16[256,1024]{1,0:T(8,128)(2,1)S(1)}, u32[]{:S(2)}, u32[]{:S(2)}) collective-permute-start(bf16[256,1024]{1,0:T(8,128)(2,1)S(1)} %dynamic-slice_bitcast_fusion), channel_id=1, source_target_pairs={{0,2},{1,3},{2,0},{3,1},{4,6},{5,7},{6,4},{7,5},{8,10},{9,11},{10,... | collective-permute-start | bytes 1572872 | tf_op jit(solution)/shard_map/ppermute | solution.py:25
  287.6 17.6 %collective-permute-start.41 = (bf16[128,1024]{1,0:T(8,128)(2,1)S(1)}, bf16[128,1024]{1,0:T(8,128)(2,1)S(1)}, u32[]{:S(2)}, u32[]{:S(2)}) collective-permute-start(bf16[128,1024]{1,0:T(8,128)(2,1)S(1)} %dynamic-slice_bitcast_fusion.8), channel_id=1, source_target_pairs={{0,4},{1,5},{2,6},{3,7},{4,0},{5,1},{6,2},{7,3},{8,12},{9,13},{10,... | collective-permute-start | bytes 786440 | tf_op jit(solution)/shard_map/ppermute | solution.py:25
  288.5 17.9 %collective-permute-start.50 = (bf16[128,1024]{1,0:T(8,128)(2,1)S(1)}, bf16[128,1024]{1,0:T(8,128)(2,1)S(1)}, u32[]{:S(2)}, u32[]{:S(2)}) collective-permute-start(bf16[128,1024]{1,0:T(8,128)(2,1)S(1)} %dynamic-slice_bitcast_fusion.7), channel_id=1, source_target_pairs={{0,8},{1,9},{2,10},{3,11},{4,12},{5,13},{6,14},{7,15},{8,0},{9,1},... | collective-permute-start | bytes 786440 | tf_op jit(solution)/shard_map/ppermute | solution.py:25
  292.3 29.5 %collective-permute-start.31 = (bf16[128,1024]{1,0:T(8,128)(2,1)S(1)}, bf16[128,1024]{1,0:T(8,128)(2,1)S(1)}, u32[]{:S(2)}, u32[]{:S(2)}) collective-permute-start(bf16[128,1024]{1,0:T(8,128)(2,1)S(1)} %dynamic-slice_bitcast_fusion.9), channel_id=1, source_target_pairs={{0,16},{1,17},{2,18},{3,19},{4,20},{5,21},{6,22},{7,23},{8,24},{9,... | collective-permute-start | bytes 786440 | tf_op jit(solution)/shard_map/ppermute | solution.py:25
  308.9 16.9 %collective-permute-start.59 = (bf16[128,1024]{1,0:T(8,128)(2,1)S(1)}, bf16[128,1024]{1,0:T(8,128)(2,1)S(1)}, u32[]{:S(2)}, u32[]{:S(2)}) collective-permute-start(bf16[128,1024]{1,0:T(8,128)(2,1)S(1)} %dynamic-slice_bitcast_fusion.6), channel_id=1, source_target_pairs={{0,8},{1,9},{2,10},{3,11},{4,12},{5,13},{6,14},{7,15},{8,0},{9,1},... | collective-permute-start | bytes 786440 | tf_op jit(solution)/shard_map/ppermute | solution.py:25
  309.6 17.8 %collective-permute-start.68 = (bf16[128,1024]{1,0:T(8,128)(2,1)S(1)}, bf16[128,1024]{1,0:T(8,128)(2,1)S(1)}, u32[]{:S(2)}, u32[]{:S(2)}) collective-permute-start(bf16[128,1024]{1,0:T(8,128)(2,1)S(1)} %dynamic-slice_bitcast_fusion.5), channel_id=1, source_target_pairs={{0,4},{1,5},{2,6},{3,7},{4,0},{5,1},{6,2},{7,3},{8,12},{9,13},{10,... | collective-permute-start | bytes 786440 | tf_op jit(solution)/shard_map/ppermute | solution.py:25
  309.9 8.7 %collective-permute-start.43 = (bf16[32,1024]{1,0:T(8,128)(2,1)S(1)}, bf16[32,1024]{1,0:T(8,128)(2,1)S(1)}, u32[]{:S(2)}, u32[]{:S(2)}) collective-permute-start(bf16[32,1024]{1,0:T(8,128)(2,1)S(1)} %dynamic-slice_bitcast_fusion.18), channel_id=1, source_target_pairs={{0,16},{1,17},{2,18},{3,19},{4,20},{5,21},{6,22},{7,23},{8,24},{9,... | collective-permute-start | bytes 196616 | tf_op jit(solution)/shard_map/ppermute | solution.py:25
  313.3 8.2 %collective-permute-start.52 = (bf16[32,1024]{1,0:T(8,128)(2,1)S(1)}, bf16[32,1024]{1,0:T(8,128)(2,1)S(1)}, u32[]{:S(2)}, u32[]{:S(2)}) collective-permute-start(bf16[32,1024]{1,0:T(8,128)(2,1)S(1)} %dynamic-slice_bitcast_fusion.17), channel_id=1, source_target_pairs={{0,2},{1,3},{2,0},{3,1},{4,6},{5,7},{6,4},{7,5},{8,10},{9,11},{10,... | collective-permute-start | bytes 196616 | tf_op jit(solution)/shard_map/ppermute | solution.py:25
  324.7 7.7 %collective-permute-start.54 = (bf16[64,1024]{1,0:T(8,128)(2,1)S(1)}, bf16[64,1024]{1,0:T(8,128)(2,1)S(1)}, u32[]{:S(2)}, u32[]{:S(2)}) collective-permute-start(bf16[64,1024]{1,0:T(8,128)(2,1)S(1)} %pad_maximum_fusion.24), channel_id=1, source_target_pairs={{0,16},{1,17},{2,18},{3,19},{4,20},{5,21},{6,22},{7,23},{8,24},{9,... | collective-permute-start | bytes 393224 | tf_op jit(solution)/shard_map/ppermute | solution.py:25
  325.8 9.2 %collective-permute-start.60 = (bf16[64,1024]{1,0:T(8,128)(2,1)S(1)}, bf16[64,1024]{1,0:T(8,128)(2,1)S(1)}, u32[]{:S(2)}, u32[]{:S(2)}) collective-permute-start(bf16[64,1024]{1,0:T(8,128)(2,1)S(1)} %dynamic-slice_bitcast_fusion.11), channel_id=1, source_target_pairs={{0,16},{1,17},{2,18},{3,19},{4,20},{5,21},{6,22},{7,23},{8,24},{9,... | collective-permute-start | bytes 393224 | tf_op jit(solution)/shard_map/ppermute | solution.py:25
  327.4 8.4 %collective-permute-start.69 = (bf16[64,1024]{1,0:T(8,128)(2,1)S(1)}, bf16[64,1024]{1,0:T(8,128)(2,1)S(1)}, u32[]{:S(2)}, u32[]{:S(2)}) collective-permute-start(bf16[64,1024]{1,0:T(8,128)(2,1)S(1)} %dynamic-slice_bitcast_fusion.10), channel_id=1, source_target_pairs={{0,8},{1,9},{2,10},{3,11},{4,12},{5,13},{6,14},{7,15},{8,0},{9,1},... | collective-permute-start | bytes 393224 | tf_op jit(solution)/shard_map/ppermute | solution.py:25
  327.8 8.1 %collective-permute-start.33 = (bf16[32,1024]{1,0:T(8,128)(2,1)S(1)}, bf16[32,1024]{1,0:T(8,128)(2,1)S(1)}, u32[]{:S(2)}, u32[]{:S(2)}) collective-permute-start(bf16[32,1024]{1,0:T(8,128)(2,1)S(1)} %dynamic-slice_bitcast_fusion.19), channel_id=1, source_target_pairs={{0,4},{1,5},{2,6},{3,7},{4,0},{5,1},{6,2},{7,3},{8,12},{9,13},{10,... | collective-permute-start | bytes 196616 | tf_op jit(solution)/shard_map/ppermute | solution.py:25
  328.2 19.8 %collective-permute-start.46 = (bf16[128,1024]{1,0:T(8,128)(2,1)S(1)}, bf16[128,1024]{1,0:T(8,128)(2,1)S(1)}, u32[]{:S(2)}, u32[]{:S(2)}) collective-permute-start(bf16[128,1024]{1,0:T(8,128)(2,1)S(1)} %pad_maximum_fusion.18), channel_id=1, source_target_pairs={{0,4},{1,5},{2,6},{3,7},{4,0},{5,1},{6,2},{7,3},{8,12},{9,13},{10,... | collective-permute-start | bytes 786440 | tf_op jit(solution)/shard_map/ppermute | solution.py:25
  332.5 20.0 %collective-permute-start.55 = (bf16[128,1024]{1,0:T(8,128)(2,1)S(1)}, bf16[128,1024]{1,0:T(8,128)(2,1)S(1)}, u32[]{:S(2)}, u32[]{:S(2)}) collective-permute-start(bf16[128,1024]{1,0:T(8,128)(2,1)S(1)} %pad_maximum_fusion.19), channel_id=1, source_target_pairs={{0,8},{1,9},{2,10},{3,11},{4,12},{5,13},{6,14},{7,15},{8,0},{9,1},... | collective-permute-start | bytes 786440 | tf_op jit(solution)/shard_map/ppermute | solution.py:25
  336.0 7.0 %collective-permute-start.34 = (bf16[32,1024]{1,0:T(8,128)(2,1)S(1)}, bf16[32,1024]{1,0:T(8,128)(2,1)S(1)}, u32[]{:S(2)}, u32[]{:S(2)}) collective-permute-start(bf16[32,1024]{1,0:T(8,128)(2,1)S(1)} %fusion.69), channel_id=1, source_target_pairs={{0,4},{1,5},{2,6},{3,7},{4,0},{5,1},{6,2},{7,3},{8,12},{9,13},{10,... | collective-permute-start | bytes 196616 | tf_op jit(solution)/shard_map/ppermute | solution.py:25
  343.4 9.3 %collective-permute-start.63 = (bf16[64,1024]{1,0:T(8,128)(2,1)S(1)}, bf16[64,1024]{1,0:T(8,128)(2,1)S(1)}, u32[]{:S(2)}, u32[]{:S(2)}) collective-permute-start(bf16[64,1024]{1,0:T(8,128)(2,1)S(1)} %pad_maximum_fusion.25), channel_id=1, source_target_pairs={{0,16},{1,17},{2,18},{3,19},{4,20},{5,21},{6,22},{7,23},{8,24},{9,... | collective-permute-start | bytes 393224 | tf_op jit(solution)/shard_map/ppermute | solution.py:25
  344.8 8.1 %collective-permute-start.72 = (bf16[64,1024]{1,0:T(8,128)(2,1)S(1)}, bf16[64,1024]{1,0:T(8,128)(2,1)S(1)}, u32[]{:S(2)}, u32[]{:S(2)}) collective-permute-start(bf16[64,1024]{1,0:T(8,128)(2,1)S(1)} %pad_maximum_fusion.26), channel_id=1, source_target_pairs={{0,8},{1,9},{2,10},{3,11},{4,12},{5,13},{6,14},{7,15},{8,0},{9,1},... | collective-permute-start | bytes 393224 | tf_op jit(solution)/shard_map/ppermute | solution.py:25
  347.9 12.7 %collective-permute-start.36 = (bf16[128,1024]{1,0:T(8,128)(2,1)S(1)}, bf16[128,1024]{1,0:T(8,128)(2,1)S(1)}, u32[]{:S(2)}, u32[]{:S(2)}) collective-permute-start(bf16[128,1024]{1,0:T(8,128)(2,1)S(1)} %pad_maximum_fusion.17), channel_id=1, source_target_pairs={{0,16},{1,17},{2,18},{3,19},{4,20},{5,21},{6,22},{7,23},{8,24},{9,... | collective-permute-start | bytes 786440 | tf_op jit(solution)/shard_map/ppermute | solution.py:25
  348.2 16.9 %collective-permute-start.47 = (bf16[256,1024]{1,0:T(8,128)(2,1)S(1)}, bf16[256,1024]{1,0:T(8,128)(2,1)S(1)}, u32[]{:S(2)}, u32[]{:S(2)}) collective-permute-start(bf16[256,1024]{1,0:T(8,128)(2,1)S(1)} %pad_maximum_fusion.11), channel_id=1, source_target_pairs={{0,2},{1,3},{2,0},{3,1},{4,6},{5,7},{6,4},{7,5},{8,10},{9,11},{10,... | collective-permute-start | bytes 1572872 | tf_op jit(solution)/shard_map/ppermute | solution.py:25
  352.6 29.8 %collective-permute-start.56 = (bf16[256,1024]{1,0:T(8,128)(2,1)S(1)}, bf16[256,1024]{1,0:T(8,128)(2,1)S(1)}, u32[]{:S(2)}, u32[]{:S(2)}) collective-permute-start(bf16[256,1024]{1,0:T(8,128)(2,1)S(1)} %pad_maximum_fusion.12), channel_id=1, source_target_pairs={{0,4},{1,5},{2,6},{3,7},{4,0},{5,1},{6,2},{7,3},{8,12},{9,13},{10,... | collective-permute-start | bytes 1572872 | tf_op jit(solution)/shard_map/ppermute | solution.py:25
  352.8 11.5 %collective-permute-start.64 = (bf16[128,1024]{1,0:T(8,128)(2,1)S(1)}, bf16[128,1024]{1,0:T(8,128)(2,1)S(1)}, u32[]{:S(2)}, u32[]{:S(2)}) collective-permute-start(bf16[128,1024]{1,0:T(8,128)(2,1)S(1)} %pad_maximum_fusion.20), channel_id=1, source_target_pairs={{0,8},{1,9},{2,10},{3,11},{4,12},{5,13},{6,14},{7,15},{8,0},{9,1},... | collective-permute-start | bytes 786440 | tf_op jit(solution)/shard_map/ppermute | solution.py:25
  353.0 11.8 %collective-permute-start.73 = (bf16[128,1024]{1,0:T(8,128)(2,1)S(1)}, bf16[128,1024]{1,0:T(8,128)(2,1)S(1)}, u32[]{:S(2)}, u32[]{:S(2)}) collective-permute-start(bf16[128,1024]{1,0:T(8,128)(2,1)S(1)} %pad_maximum_fusion.21), channel_id=1, source_target_pairs={{0,4},{1,5},{2,6},{3,7},{4,0},{5,1},{6,2},{7,3},{8,12},{9,13},{10,... | collective-permute-start | bytes 786440 | tf_op jit(solution)/shard_map/ppermute | solution.py:25
  360.8 22.0 %collective-permute-start.37 = (bf16[256,1024]{1,0:T(8,128)(2,1)S(1)}, bf16[256,1024]{1,0:T(8,128)(2,1)S(1)}, u32[]{:S(2)}, u32[]{:S(2)}) collective-permute-start(bf16[256,1024]{1,0:T(8,128)(2,1)S(1)} %pad_maximum_fusion.10), channel_id=1, source_target_pairs={{0,8},{1,9},{2,10},{3,11},{4,12},{5,13},{6,14},{7,15},{8,0},{9,1},... | collective-permute-start | bytes 1572872 | tf_op jit(solution)/shard_map/ppermute | solution.py:25
  364.5 19.2 %collective-permute-start.65 = (bf16[256,1024]{1,0:T(8,128)(2,1)S(1)}, bf16[256,1024]{1,0:T(8,128)(2,1)S(1)}, u32[]{:S(2)}, u32[]{:S(2)}) collective-permute-start(bf16[256,1024]{1,0:T(8,128)(2,1)S(1)} %pad_maximum_fusion.13), channel_id=1, source_target_pairs={{0,4},{1,5},{2,6},{3,7},{4,0},{5,1},{6,2},{7,3},{8,12},{9,13},{10,... | collective-permute-start | bytes 1572872 | tf_op jit(solution)/shard_map/ppermute | solution.py:25
  365.0 22.8 %collective-permute-start.74 = (bf16[256,1024]{1,0:T(8,128)(2,1)S(1)}, bf16[256,1024]{1,0:T(8,128)(2,1)S(1)}, u32[]{:S(2)}, u32[]{:S(2)}) collective-permute-start(bf16[256,1024]{1,0:T(8,128)(2,1)S(1)} %pad_maximum_fusion.14), channel_id=1, source_target_pairs={{0,2},{1,3},{2,0},{3,1},{4,6},{5,7},{6,4},{7,5},{8,10},{9,11},{10,... | collective-permute-start | bytes 1572872 | tf_op jit(solution)/shard_map/ppermute | solution.py:25
  365.4 26.1 %collective-permute-start.48 = (bf16[512,1024]{1,0:T(8,128)(2,1)S(1)}, bf16[512,1024]{1,0:T(8,128)(2,1)S(1)}, u32[]{:S(2)}, u32[]{:S(2)}) collective-permute-start(bf16[512,1024]{1,0:T(8,128)(2,1)S(1)} %pad_maximum_fusion.4), channel_id=1, source_target_pairs={{0,1},{1,0},{2,3},{3,2},{4,5},{5,4},{6,7},{7,6},{8,9},{9,8},{10,11... | collective-permute-start | bytes 3145736 | tf_op jit(solution)/shard_map/ppermute | solution.py:25
  382.7 11.9 %collective-permute-start.57 = (bf16[512,1024]{1,0:T(8,128)(2,1)S(1)}, bf16[512,1024]{1,0:T(8,128)(2,1)S(1)}, u32[]{:S(2)}, u32[]{:S(2)}) collective-permute-start(bf16[512,1024]{1,0:T(8,128)(2,1)S(1)} %pad_maximum_fusion.5), channel_id=1, source_target_pairs={{0,1},{1,0},{2,3},{3,2},{4,5},{5,4},{6,7},{7,6},{8,9},{9,8},{10,11... | collective-permute-start | bytes 3145736 | tf_op jit(solution)/shard_map/ppermute | solution.py:25
  383.2 14.5 %collective-permute-start.38 = (bf16[512,1024]{1,0:T(8,128)(2,1)S(1)}, bf16[512,1024]{1,0:T(8,128)(2,1)S(1)}, u32[]{:S(2)}, u32[]{:S(2)}) collective-permute-start(bf16[512,1024]{1,0:T(8,128)(2,1)S(1)} %pad_maximum_fusion.3), channel_id=1, source_target_pairs={{0,1},{1,0},{2,3},{3,2},{4,5},{5,4},{6,7},{7,6},{8,9},{9,8},{10,11... | collective-permute-start | bytes 3145736 | tf_op jit(solution)/shard_map/ppermute | solution.py:25
  384.0 16.7 %collective-permute-start.66 = (bf16[512,1024]{1,0:T(8,128)(2,1)S(1)}, bf16[512,1024]{1,0:T(8,128)(2,1)S(1)}, u32[]{:S(2)}, u32[]{:S(2)}) collective-permute-start(bf16[512,1024]{1,0:T(8,128)(2,1)S(1)} %pad_maximum_fusion.6), channel_id=1, source_target_pairs={{0,1},{1,0},{2,3},{3,2},{4,5},{5,4},{6,7},{7,6},{8,9},{9,8},{10,11... | collective-permute-start | bytes 3145736 | tf_op jit(solution)/shard_map/ppermute | solution.py:25
  388.1 15.6 %collective-permute-start.75 = (bf16[512,1024]{1,0:T(8,128)(2,1)S(1)}, bf16[512,1024]{1,0:T(8,128)(2,1)S(1)}, u32[]{:S(2)}, u32[]{:S(2)}) collective-permute-start(bf16[512,1024]{1,0:T(8,128)(2,1)S(1)} %pad_maximum_fusion.7), channel_id=1, source_target_pairs={{0,1},{1,0},{2,3},{3,2},{4,5},{5,4},{6,7},{7,6},{8,9},{9,8},{10,11... | collective-permute-start | bytes 3145736 | tf_op jit(solution)/shard_map/ppermute | solution.py:25
  (41 other events, 250.0 us)

commit v3 on v2

--- a/solution.py
+++ b/solution.py
@@ -13,7 +13,7 @@
 EPS = 1e-06
 FLOAT = jnp.float32
 BHALF = jnp.bfloat16
-VMEM_BYTES = 60 * 1024 * 1024
+VMEM_BYTES = 24 * 1024 * 1024
 
 
 def bits_of(count):
@@ -187,7 +187,7 @@
 SMEM_SPEC = pl.BlockSpec(memory_space=pltpu.SMEM)
 
 
-def call(body, grid, in_specs, out_specs, out_shape, flops, moved, scratch=()):
+def call(body, grid, in_specs, out_specs, out_shape, flops, moved, scratch=(), vmem=VMEM_BYTES):
     return pl.pallas_call(
         body,
         grid=grid,
@@ -196,7 +196,7 @@
         out_shape=out_shape,
         scratch_shapes=scratch,
         cost_estimate=pl.CostEstimate(flops=flops, bytes_accessed=moved, transcendentals=0),
-        compiler_params=pltpu.CompilerParams(vmem_limit_bytes=VMEM_BYTES),
+        compiler_params=pltpu.CompilerParams(vmem_limit_bytes=vmem),
     )
 
 
@@ -477,6 +477,7 @@
             pltpu.VMEM((n, 2 * BLOCK, inner), BHALF),
             pltpu.SemaphoreType.DMA((n, 7)),
         ],
+        vmem=VMEM_BYTES if n <= 4 else 2 * VMEM_BYTES,
     )(place, *flat)
 
 

time: 412 us -> 384 us (0.932)
  Pallas kernels: 139 us -> 81.5 us
  waiting for transfers between devices: 87.7 us -> 121 us
  local copies, waits for them, and re-layouts: 18.1 us -> 33 us
  other arithmetic: 58.5 us -> 47.1 us
  starting transfers between devices: 102 us -> 93.2 us
    ppermute x82, waiting for transfers between devices: 87.7 us -> 121 us  [swap(): return lax.ppermute(value, axes, [(s, s ^ mask) for s in range(count)])]
    unnamed x46 -> x130, local copies, waits for them, and re-layouts: 4.59 us -> 25.6 us
    pallas_call x4, Pallas kernels: 39.9 us -> 24.9 us  [unit(): call(unit_body, (1,), [piece] * 2 + [cot] * 2 + [whole(down.shape)] * 3,...]
    pallas_call x2, Pallas kernels: 16.2 us -> 5.26 us  [tokens_side(): call(tokens_body, (1,), [row, own, row, row, row, own] + [whole] * 4, own...]
    ppermute x82, starting transfers between devices: 102 us -> 93.2 us  [swap(): return lax.ppermute(value, axes, [(s, s ^ mask) for s in range(count)])]
    pallas_call x2, Pallas kernels: 10.5 us -> 3.6 us  [join(): call(functools.partial(join_body, heads, block > 0), (1,), [SMEM_SPEC, ro...]
    pallas_call x2, Pallas kernels: 13.7 us -> 6.89 us  [grads(): pl.pallas_call(body, grid_spec=spec, out_shape=shape_of((2, n, half, cols...]
    pallas_call x2, Pallas kernels: 12.3 us -> 6.91 us  [turn(): call(functools.partial(turn_body, heads), (1,), [SMEM_SPEC, first, first,...]
  transfers between devices with their start and end apart: 82 -> 82, of which waited for: 26 -> 30; matrix products, arithmetic and copies ran while one was open for 15% -> 12% of each run, Pallas kernels for 32% -> 20%
where the time goes in v3:
time: 384 us; the launch traced here: 379 us
  waiting for transfers between devices  121 us (32%)
  starting transfers between devices  93.2 us (24%)
  Pallas kernels  81.5 us (21%)
  other arithmetic  47.1 us (12%)
  local copies, waits for them, and re-layouts  33 us (9%)
    ppermute x82, waiting for transfers between devices, swap(): return lax.ppermute(value, axes, [(s, s ^ mask) for s in range(count)])  121 us
    ppermute x82, starting transfers between devices, swap(): return lax.ppermute(value, axes, [(s, s ^ mask) for s in range(count)])  93.2 us
    unnamed x130, local copies, waits for them, and re-layouts  25.6 us
    pallas_call x4, Pallas kernels, unit(): call(unit_body, (1,), [piece] * 2 + [cot] * 2 + [whole(down.shape)] * 3,...  24.9 us
    pallas_call x1, Pallas kernels, unit_grads(): call(functools.partial(unit_grads_body, n, orders), (1,), [SMEM_SPEC] + [...  13.3 us
    convert_element_type x5, other arithmetic, reduced(): outs.append(double(piece, [1], place).astype(FLOAT))  12.2 us
  transfers between devices with their start and end apart: 82, of which 30 were waited for; matrix products, arithmetic and copies ran while one was open for 12% of the time, Pallas kernels for 20%

profile of v3, /device:TPU:1, one launch (start us, length us, event | category | flops | bytes accessed | tf_op | source)
XLA Modules:
  0.0 378.8 jit_solution(9054555664311272457)
XLA Ops:
  3.3 1.7 copy-done.6
  6.5 4.7 %shard_map.186 = (bf16[512,1024]{1,0:T(8,128)(2,1)S(1)}, f32[512,1024]{1,0:T(8,128)S(1)}, bf16[512,1024]{1,0:T(8,128)(2,1)S(1)}, bf16[512,1024]{1,0:T(8,128)(2,1...) custom-call(f32[8]{0:T(128)S(1)} %get-tuple-element.216.rate, bf16[512,1024]{1,0:T(8,128)(2,1)S(1)} %copy-done.3, ...), custom_call_target="tpu_custom_call" | custom-call | flops 2147483648 | bytes 10485760 | tf_op jit(solution)/shard_map/pallas_call | solution.py:242
  18.1 2.7 collective-permute-start.1
  20.8 3.7 collective-permute-done.1
  27.3 3.2 collective-permute-done.2
  32.5 3.0 collective-permute-done.3
  35.5 1.7 fusion.37
  37.2 2.2 collective-permute-start.4
  40.6 2.9 collective-permute-done.4
  44.7 3.9 %collective-permute-start.5 = (bf16[4,128,128]{2,1,0:T(8,128)(2,1)S(1)}, bf16[4,128,128]{2,1,0:T(8,128)(2,1)S(1)}, u32[]{:S(2)}, u32[]{:S(2)}) collective-permute-start(bf16[4,128,128]{2,1,0:T(8,128)(2,1)S(1)} %get-tuple-element.132), channel_id=1, source_target_pairs={{0,1},{1,0},{2,3},{3,2},{4,5},{5,4},{6,7},{7,6},{8,9},{9,8},{10,11... | collective-permute-start | bytes 393224 | tf_op jit(solution)/shard_map/ppermute | solution.py:25
  54.8 5.4 %shard_map.187 = (f32[512,1024]{1,0:T(8,128)S(1)}, bf16[512,1024]{1,0:T(8,128)(2,1)S(1)}, f32[512,1024]{1,0:T(8,128)S(1)}, f32[512,1024]{1,0:T(8,128)S(1)}) custom-call(f32[8]{0:T(128)S(1)} %get-tuple-element.216.rate, bf16[512,1024]{1,0:T(8,128)(2,1)S(1)} %copy-done.57, bf16[1024,1024]{1,0:T(8,128)(2,1)S(1)} %copy-done.10, ...), custom_call_target="tpu_custom_call" | custom-call | flops 2147483648 | bytes 14680064 | tf_op jit(solution)/shard_map/pallas_call | solution.py:292
  60.6 2.8 copy-done
  63.4 1.8 shard_map.191
  68.2 1.8 shard_map.188
  73.7 6.2 %collective-permute-done.17.n0.refs_21_ = bf16[256,1024]{1,0:T(8,128)(2,1)S(1)} collective-permute-done((bf16[256,1024]{1,0:T(8,128)(2,1)S(1)}, bf16[256,1024]{1,0:T(8,128)(2,1)S(1)}, u32[]{:S(2)}, u32[]{:S(2)}) %collective-permute-start.17) | collective-permute-done | bytes 524320 | tf_op jit(solution)/shard_map/ppermute | solution.py:25
  81.2 7.2 %shard_map.192 = (f32[2,256,1024]{2,1,0:T(8,128)S(1)}, bf16[2,256,1024]{2,1,0:T(8,128)(2,1)}, bf16[512,704]{1,0:T(8,128)(2,1)S(1)}, bf16[512,704]{1,0:T(8,128)(2,1)S(1)}, bf16[512,704]{1,0:T(8,128)(2,1)S(1)}) custom-call(bf16[256,1024]{1,0:T(8,128)(2,1)S(1)} %get-tuple-element.84.n0.refs_7_, bf16[256,1024]{1,0:T(8,128)(2,1)S(1)} %collective-permute-done.15.n1.refs_8_, ...), custom_call_target="tpu_custom_call" | custom-call | flops 4429185024 | bytes 9568256 | tf_op jit(solution)/shard_map/pallas_call | solution.py:380
  91.9 7.2 %shard_map.189 = (f32[2,256,1024]{2,1,0:T(8,128)S(1)}, bf16[2,256,1024]{2,1,0:T(8,128)(2,1)}, bf16[512,704]{1,0:T(8,128)(2,1)S(1)}, bf16[512,704]{1,0:T(8,128)(2,1)S(1)}, bf16[512,704]{1,0:T(8,128)(2,1)S(1)}) custom-call(bf16[256,1024]{1,0:T(8,128)(2,1)S(1)} %get-tuple-element.77.n0.refs_0_, bf16[256,1024]{1,0:T(8,128)(2,1)S(1)} %collective-permute-done.6.n1.refs_1_, ...), custom_call_target="tpu_custom_call" | custom-call | flops 4429185024 | bytes 9568256 | tf_op jit(solution)/shard_map/pallas_call | solution.py:380
  100.4 5.4 %shard_map.193 = (f32[2,256,1024]{2,1,0:T(8,128)S(1)}, bf16[2,256,1024]{2,1,0:T(8,128)(2,1)S(1)}, bf16[512,704]{1,0:T(8,128)(2,1)S(1)}, bf16[512,704]{1,0:T(8,128)(2,1)S(1)}, bf16[512,704]{1,0:T(8,128)(2,1)S(1)}) custom-call(bf16[256,1024]{1,0:T(8,128)(2,1)S(1)} %collective-permute-done.17.n0.refs_21_, ...), custom_call_target="tpu_custom_call" | custom-call | flops 4429185024 | bytes 9568256 | tf_op jit(solution)/shard_map/pallas_call | solution.py:380
  106.4 5.1 %shard_map.190 = (f32[2,256,1024]{2,1,0:T(8,128)S(1)}, bf16[2,256,1024]{2,1,0:T(8,128)(2,1)S(1)}, bf16[512,704]{1,0:T(8,128)(2,1)S(1)}, bf16[512,704]{1,0:T(8,128)(2,1)S(1)}, bf16[512,704]{1,0:T(8,128)(2,1)S(1)}) custom-call(bf16[256,1024]{1,0:T(8,128)(2,1)S(1)} %collective-permute-done.9.n0.refs_14_, ...), custom_call_target="tpu_custom_call" | custom-call | flops 4429185024 | bytes 9568256 | tf_op jit(solution)/shard_map/pallas_call | solution.py:380
  111.6 13.3 %shard_map.202 = (bf16[8,2,704,128]{3,2,1,0:T(8,128)(2,1)S(1)}, bf16[8,704,128]{2,1,0:T(8,128)(2,1)S(1)}) custom-call(s32[1]{0:T(128)} %bitcast.95.place, bf16[256,1024]{1,0:T(8,128)(2,1)S(1)} %get-tuple-element.77.n0.refs_0_, bf16[256,1024]{1,0:T(8,128)(2,1)S(1)} %collective-permute-done.6.n1.refs_1_, bf16[512,1024]{1,0:T(8,128)(2,1)} %refs_9_, ...), custom_call_target="tpu_custom_call" | custom-call | flops 8858370048 | bytes 21364736 | tf_op jit(solution)/shard_map/pallas_call | solution.py:464
  133.8 9.7 %collective-permute-done.79 = bf16[4,704,128]{2,1,0:T(8,128)(2,1)} collective-permute-done((bf16[4,704,128]{2,1,0:T(8,128)(2,1)}, bf16[4,704,128]{2,1,0:T(8,128)(2,1)}, u32[]{:S(2)}, u32[]{:S(2)}) %collective-permute-start.79) | collective-permute-done | bytes 720928 | tf_op jit(solution)/shard_map/ppermute | solution.py:25
  146.3 2.4 collective-permute-start.80
  150.0 3.4 shard_map.195
  153.8 3.5 shard_map.194
  157.4 2.2 collective-permute-start.23
  159.6 4.8 %collective-permute-done.80 = bf16[2,704,128]{2,1,0:T(8,128)(2,1)S(1)} collective-permute-done((bf16[2,704,128]{2,1,0:T(8,128)(2,1)S(1)}, bf16[2,704,128]{2,1,0:T(8,128)(2,1)S(1)}, u32[]{:S(2)}, u32[]{:S(2)}) %collective-permute-start.80) | collective-permute-done | bytes 360480 | tf_op jit(solution)/shard_map/ppermute | solution.py:25
  166.2 13.0 %collective-permute-done.81 = bf16[1,704,128]{2,1,0:T(8,128)(2,1)S(1)} collective-permute-done((bf16[1,704,128]{2,1,0:T(8,128)(2,1)S(1)}, bf16[1,704,128]{2,1,0:T(8,128)(2,1)S(1)}, u32[]{:S(2)}, u32[]{:S(2)}) %collective-permute-start.81) | collective-permute-done | bytes 180256 | tf_op jit(solution)/shard_map/ppermute | solution.py:25
  184.9 7.6 %shard_map.196 = (bf16[512,1024]{1,0:T(8,128)(2,1)S(1)}, f32[512,1024]{1,0:T(8,128)S(1)}, f32[512,1024]{1,0:T(8,128)S(1)}) custom-call(f32[8]{0:T(128)S(1)} %get-tuple-element.216.rate, f32[512,1024]{1,0:T(8,128)S(1)} %copy-done.40, bf16[512,1024]{1,0:T(8,128)(2,1)S(1)} %get-tuple-element.72.query, bf16[512,1024]{1,0:T(8,128)(2,1)S(1)} %copy-done.26, ...), custom_call_target="tpu_custom_call" | custom-call | flops 1610612736 | bytes 12582912 | tf_op jit(solution)/shard_map/pallas_call | solution.py:559
  192.5 8.6 %collective-permute-done.26 = bf16[4,128,128]{2,1,0:T(8,128)(2,1)S(1)} collective-permute-done((bf16[4,128,128]{2,1,0:T(8,128)(2,1)S(1)}, bf16[4,128,128]{2,1,0:T(8,128)(2,1)S(1)}, u32[]{:S(2)}, u32[]{:S(2)}) %collective-permute-start.26) | collective-permute-done | bytes 131104 | tf_op jit(solution)/shard_map/ppermute | solution.py:25
  201.3 3.1 collective-permute-start.27
  204.3 3.9 %shard_map.200 = bf16[2,3,512,1024]{3,2,1,0:T(8,128)(2,1)S(1)} custom-call(s32[1]{0:T(128)} %bitcast.30.core, bf16[512,1024]{1,0:T(8,128)(2,1)S(1)} %pad_maximum_fusion.2.refs_0_, bf16[512,1024]{1,0:T(8,128)(2,1)S(1)} %copy-done.58, bf16[256,1024]{1,0:T(8,128)(2,1)S(1)} %get-tuple-element.110.refs_2_, bf16[256,1024]{1,0:T(8,128)(2,1)S(1)} %get-tuple-element.111.refs_3_, ...), custom_call_target="tpu_custom_call" | custom-call | flops 3221225472 | bytes 12582912 | tf_op jit(solution)/shard_map/pallas_call | solution.py:646
  208.6 4.3 %collective-permute-start.28 = (bf16[4,128,128]{2,1,0:T(8,128)(2,1)S(1)}, bf16[4,128,128]{2,1,0:T(8,128)(2,1)S(1)}, u32[]{:S(2)}, u32[]{:S(2)}) collective-permute-start(bf16[4,128,128]{2,1,0:T(8,128)(2,1)S(1)} %get-tuple-element.126), channel_id=1, source_target_pairs={{0,1},{1,0},{2,3},{3,2},{4,5},{5,4},{6,7},{7,6},{8,9},{9,8},{10,11... | collective-permute-start | bytes 393224 | tf_op jit(solution)/shard_map/ppermute | solution.py:25
  214.8 2.8 shard_map.197
  217.6 3.0 shard_map.201
  222.1 1.7 fusion.8
  223.9 1.7 fusion.10
  229.7 2.6 shard_map.199
  232.4 2.6 shard_map.198
  236.6 10.4 %collective-permute-done.78 = bf16[1,2,704,128]{3,2,1,0:T(8,128)(2,1)S(1)} collective-permute-done((bf16[1,2,704,128]{3,2,1,0:T(8,128)(2,1)S(1)}, bf16[1,2,704,128]{3,2,1,0:T(8,128)(2,1)S(1)}, u32[]{:S(2)}, u32[]{:S(2)}) %collective-permute-start.78) | collective-permute-done | bytes 360480 | tf_op jit(solution)/shard_map/ppermute | solution.py:25
  254.7 7.3 %collective-permute-done.40 = bf16[256,1024]{1,0:T(8,128)(2,1)S(1)} collective-permute-done((bf16[256,1024]{1,0:T(8,128)(2,1)S(1)}, bf16[256,1024]{1,0:T(8,128)(2,1)S(1)}, u32[]{:S(2)}, u32[]{:S(2)}) %collective-permute-start.40) | collective-permute-done | bytes 524320 | tf_op jit(solution)/shard_map/ppermute | solution.py:25
  263.4 1.7 collective-permute-done.30
  265.3 2.0 collective-permute-start.31
  267.3 12.5 %collective-permute-done.41 = bf16[128,1024]{1,0:T(8,128)(2,1)S(1)} collective-permute-done((bf16[128,1024]{1,0:T(8,128)(2,1)S(1)}, bf16[128,1024]{1,0:T(8,128)(2,1)S(1)}, u32[]{:S(2)}, u32[]{:S(2)}) %collective-permute-start.41) | collective-permute-done | bytes 262176 | tf_op jit(solution)/shard_map/ppermute | solution.py:25
  280.2 3.2 collective-permute-start.51
  287.4 4.3 %collective-permute-done.43 = bf16[32,1024]{1,0:T(8,128)(2,1)S(1)} collective-permute-done((bf16[32,1024]{1,0:T(8,128)(2,1)S(1)}, bf16[32,1024]{1,0:T(8,128)(2,1)S(1)}, u32[]{:S(2)}, u32[]{:S(2)}) %collective-permute-start.43) | collective-permute-done | bytes 65568 | tf_op jit(solution)/shard_map/ppermute | solution.py:25
  291.7 2.9 collective-permute-start.44
  297.0 2.1 collective-permute-start.45
  303.7 3.2 collective-permute-done.54
  307.0 1.8 collective-permute-done.60
  310.3 2.0 collective-permute-done.61
  312.7 1.9 collective-permute-done.70
  314.6 2.7 collective-permute-start.71
  319.2 2.8 collective-permute-start.72
  323.0 2.2 collective-permute-done.63
  326.4 8.7 %collective-permute-done.36 = bf16[128,1024]{1,0:T(8,128)(2,1)S(1)} collective-permute-done((bf16[128,1024]{1,0:T(8,128)(2,1)S(1)}, bf16[128,1024]{1,0:T(8,128)(2,1)S(1)}, u32[]{:S(2)}, u32[]{:S(2)}) %collective-permute-start.36) | collective-permute-done | bytes 262176 | tf_op jit(solution)/shard_map/ppermute | solution.py:25
  335.4 2.6 collective-permute-done.64
  339.0 16.4 %collective-permute-start.48 = (bf16[512,1024]{1,0:T(8,128)(2,1)S(1)}, bf16[512,1024]{1,0:T(8,128)(2,1)S(1)}, u32[]{:S(2)}, u32[]{:S(2)}) collective-permute-start(bf16[512,1024]{1,0:T(8,128)(2,1)S(1)} %pad_maximum_fusion.4), channel_id=1, source_target_pairs={{0,1},{1,0},{2,3},{3,2},{4,5},{5,4},{6,7},{7,6},{8,9},{9,8},{10,11... | collective-permute-start | bytes 3145736 | tf_op jit(solution)/shard_map/ppermute | solution.py:25
  357.0 2.3 collective-permute-start.66
  359.6 3.5 collective-permute-start.75
  363.7 2.5 maximum_convert_fusion.1
  366.7 2.4 maximum_convert_fusion.2
  369.8 2.4 maximum_convert_fusion
  372.8 2.4 maximum_convert_fusion.3
  375.9 2.4 maximum_convert_fusion.4
  (388 shorter events, 100.4 us)
Async XLA Ops:
  39.3 28.6 %collective-permute-start.11 = (bf16[512,1024]{1,0:T(8,128)(2,1)}, bf16[512,1024]{1,0:T(8,128)(2,1)S(1)}, u32[]{:S(2)}, u32[]{:S(2)}) collective-permute-start(bf16[512,1024]{1,0:T(8,128)(2,1)} %refs_9_), channel_id=1, source_target_pairs={{0,2},{1,3},{2,0},{3,1},{4,6},{5,7},{6,4},{7,5},{8,10},{9,11},{10,... | collective-permute-start | bytes 3145736 | tf_op jit(solution)/shard_map/ppermute | solution.py:25
  44.7 15.7 %collective-permute-start.5 = (bf16[4,128,128]{2,1,0:T(8,128)(2,1)S(1)}, bf16[4,128,128]{2,1,0:T(8,128)(2,1)S(1)}, u32[]{:S(2)}, u32[]{:S(2)}) collective-permute-start(bf16[4,128,128]{2,1,0:T(8,128)(2,1)S(1)} %get-tuple-element.132), channel_id=1, source_target_pairs={{0,1},{1,0},{2,3},{3,2},{4,5},{5,4},{6,7},{7,6},{8,9},{9,8},{10,11... | collective-permute-start | bytes 393224 | tf_op jit(solution)/shard_map/ppermute | solution.py:25
  60.3 20.8 %collective-permute-start.7 = (bf16[512,1024]{1,0:T(8,128)(2,1)}, bf16[512,1024]{1,0:T(8,128)(2,1)S(1)}, u32[]{:S(2)}, u32[]{:S(2)}) collective-permute-start(bf16[512,1024]{1,0:T(8,128)(2,1)} %refs_9_), channel_id=1, source_target_pairs={{0,1},{1,0},{2,3},{3,2},{4,5},{5,4},{6,7},{7,6},{8,9},{9,8},{10,11... | collective-permute-start | bytes 3145736 | tf_op jit(solution)/shard_map/ppermute | solution.py:25
  66.3 13.6 %collective-permute-start.17 = (bf16[256,1024]{1,0:T(8,128)(2,1)S(1)}, bf16[256,1024]{1,0:T(8,128)(2,1)S(1)}, u32[]{:S(2)}, u32[]{:S(2)}) collective-permute-start(bf16[256,1024]{1,0:T(8,128)(2,1)S(1)} %get-tuple-element.84.n0.refs_7_), channel_id=1, source_target_pairs={{0,2},{1,3},{2,0},{3,1},{4,6},{5,7},{6,4},{7,5},{8,10},{9,11},{10,... | collective-permute-start | bytes 1572872 | tf_op jit(solution)/shard_map/ppermute | solution.py:25
  67.7 13.5 %collective-permute-start.15 = (bf16[256,1024]{1,0:T(8,128)(2,1)S(1)}, bf16[256,1024]{1,0:T(8,128)(2,1)S(1)}, u32[]{:S(2)}, u32[]{:S(2)}) collective-permute-start(bf16[256,1024]{1,0:T(8,128)(2,1)S(1)} %get-tuple-element.84.n0.refs_7_), channel_id=1, source_target_pairs={{0,1},{1,0},{2,3},{3,2},{4,5},{5,4},{6,7},{7,6},{8,9},{9,8},{10,11... | collective-permute-start | bytes 1572872 | tf_op jit(solution)/shard_map/ppermute | solution.py:25
  68.0 32.5 %collective-permute-start.12 = (bf16[512,1024]{1,0:T(8,128)(2,1)S(1)}, bf16[512,1024]{1,0:T(8,128)(2,1)S(1)}, u32[]{:S(2)}, u32[]{:S(2)}) collective-permute-start(bf16[512,1024]{1,0:T(8,128)(2,1)S(1)} %collective-permute-done.11.c0.refs_16_.refs_23_), channel_id=1, source_target_pairs={{0,1},{1,0},{2,3},{3,2},{4,5},{5,4},{6,7},{7,6},{8,9},{9,8},{10,11... | collective-permute-start | bytes 3145736 | tf_op jit(solution)/shard_map/ppermute | solution.py:25
  73.5 17.6 %collective-permute-start.9 = (bf16[256,1024]{1,0:T(8,128)(2,1)S(1)}, bf16[256,1024]{1,0:T(8,128)(2,1)S(1)}, u32[]{:S(2)}, u32[]{:S(2)}) collective-permute-start(bf16[256,1024]{1,0:T(8,128)(2,1)S(1)} %get-tuple-element.77.n0.refs_0_), channel_id=1, source_target_pairs={{0,2},{1,3},{2,0},{3,1},{4,6},{5,7},{6,4},{7,5},{8,10},{9,11},{10,... | collective-permute-start | bytes 1572872 | tf_op jit(solution)/shard_map/ppermute | solution.py:25
  79.9 12.1 %collective-permute-start.6 = (bf16[256,1024]{1,0:T(8,128)(2,1)S(1)}, bf16[256,1024]{1,0:T(8,128)(2,1)S(1)}, u32[]{:S(2)}, u32[]{:S(2)}) collective-permute-start(bf16[256,1024]{1,0:T(8,128)(2,1)S(1)} %get-tuple-element.77.n0.refs_0_), channel_id=1, source_target_pairs={{0,1},{1,0},{2,3},{3,2},{4,5},{5,4},{6,7},{7,6},{8,9},{9,8},{10,11... | collective-permute-start | bytes 1572872 | tf_op jit(solution)/shard_map/ppermute | solution.py:25
  81.1 19.3 %collective-permute-start.18 = (bf16[256,1024]{1,0:T(8,128)(2,1)S(1)}, bf16[256,1024]{1,0:T(8,128)(2,1)S(1)}, u32[]{:S(2)}, u32[]{:S(2)}) collective-permute-start(bf16[256,1024]{1,0:T(8,128)(2,1)S(1)} %collective-permute-done.17.n0.refs_21_), channel_id=1, source_target_pairs={{0,1},{1,0},{2,3},{3,2},{4,5},{5,4},{6,7},{7,6},{8,9},{9,8},{10,11... | collective-permute-start | bytes 1572872 | tf_op jit(solution)/shard_map/ppermute | solution.py:25
  89.7 56.6 %collective-permute-start.16 = (bf16[2,256,1024]{2,1,0:T(8,128)(2,1)}, bf16[2,256,1024]{2,1,0:T(8,128)(2,1)}, u32[]{:S(2)}, u32[]{:S(2)}) collective-permute-start(bf16[2,256,1024]{2,1,0:T(8,128)(2,1)} %get-tuple-element.86), channel_id=1, source_target_pairs={{0,1},{1,0},{2,3},{3,2},{4,5},{5,4},{6,7},{7,6},{8,9},{9,8},{10,11... | collective-permute-start | bytes 3145736 | tf_op jit(solution)/shard_map/ppermute | solution.py:25
  91.1 15.3 %collective-permute-start.10 = (bf16[256,1024]{1,0:T(8,128)(2,1)S(1)}, bf16[256,1024]{1,0:T(8,128)(2,1)S(1)}, u32[]{:S(2)}, u32[]{:S(2)}) collective-permute-start(bf16[256,1024]{1,0:T(8,128)(2,1)S(1)} %collective-permute-done.9.n0.refs_14_), channel_id=1, source_target_pairs={{0,1},{1,0},{2,3},{3,2},{4,5},{5,4},{6,7},{7,6},{8,9},{9,8},{10,11... | collective-permute-start | bytes 1572872 | tf_op jit(solution)/shard_map/ppermute | solution.py:25
  100.4 53.0 %collective-permute-start.8 = (bf16[2,256,1024]{2,1,0:T(8,128)(2,1)}, bf16[2,256,1024]{2,1,0:T(8,128)(2,1)}, u32[]{:S(2)}, u32[]{:S(2)}) collective-permute-start(bf16[2,256,1024]{2,1,0:T(8,128)(2,1)} %get-tuple-element.80), channel_id=1, source_target_pairs={{0,1},{1,0},{2,3},{3,2},{4,5},{5,4},{6,7},{7,6},{8,9},{9,8},{10,11... | collective-permute-start | bytes 3145736 | tf_op jit(solution)/shard_map/ppermute | solution.py:25
  105.8 20.8 %collective-permute-start.19 = (bf16[2,256,1024]{2,1,0:T(8,128)(2,1)S(1)}, bf16[2,256,1024]{2,1,0:T(8,128)(2,1)S(1)}, u32[]{:S(2)}, u32[]{:S(2)}) collective-permute-start(bf16[2,256,1024]{2,1,0:T(8,128)(2,1)S(1)} %get-tuple-element.88), channel_id=1, source_target_pairs={{0,1},{1,0},{2,3},{3,2},{4,5},{5,4},{6,7},{7,6},{8,9},{9,8},{10,11... | collective-permute-start | bytes 3145736 | tf_op jit(solution)/shard_map/ppermute | solution.py:25
  111.6 17.6 %collective-permute-start.13 = (bf16[2,256,1024]{2,1,0:T(8,128)(2,1)S(1)}, bf16[2,256,1024]{2,1,0:T(8,128)(2,1)S(1)}, u32[]{:S(2)}, u32[]{:S(2)}) collective-permute-start(bf16[2,256,1024]{2,1,0:T(8,128)(2,1)S(1)} %get-tuple-element.82), channel_id=1, source_target_pairs={{0,1},{1,0},{2,3},{3,2},{4,5},{5,4},{6,7},{7,6},{8,9},{9,8},{10,11... | collective-permute-start | bytes 3145736 | tf_op jit(solution)/shard_map/ppermute | solution.py:25
  126.0 17.6 %collective-permute-start.79 = (bf16[4,704,128]{2,1,0:T(8,128)(2,1)}, bf16[4,704,128]{2,1,0:T(8,128)(2,1)}, u32[]{:S(2)}, u32[]{:S(2)}) collective-permute-start(bf16[4,704,128]{2,1,0:T(8,128)(2,1)} %slice.137), channel_id=1, source_target_pairs={{0,8},{1,9},{2,10},{3,11},{4,12},{5,13},{6,14},{7,15},{8,0},{9,1},... | collective-permute-start | bytes 2162696 | tf_op jit(solution)/shard_map/ppermute | solution.py:25
  128.0 20.8 %collective-permute-start.22 = (bf16[256,1024]{1,0:T(8,128)(2,1)}, bf16[256,1024]{1,0:T(8,128)(2,1)}, u32[]{:S(2)}, u32[]{:S(2)}) collective-permute-start(bf16[256,1024]{1,0:T(8,128)(2,1)} %get-tuple-element.141), channel_id=1, source_target_pairs={{0,2},{1,3},{2,0},{3,1},{4,6},{5,7},{6,4},{7,5},{8,10},{9,11},{10,... | collective-permute-start | bytes 1572872 | tf_op jit(solution)/shard_map/ppermute | solution.py:25
  130.5 23.2 %collective-permute-start.21 = (bf16[256,1024]{1,0:T(8,128)(2,1)}, bf16[256,1024]{1,0:T(8,128)(2,1)}, u32[]{:S(2)}, u32[]{:S(2)}) collective-permute-start(bf16[256,1024]{1,0:T(8,128)(2,1)} %get-tuple-element.139), channel_id=1, source_target_pairs={{0,2},{1,3},{2,0},{3,1},{4,6},{5,7},{6,4},{7,5},{8,10},{9,11},{10,... | collective-permute-start | bytes 1572872 | tf_op jit(solution)/shard_map/ppermute | solution.py:25
  143.5 38.0 %collective-permute-start.76 = (bf16[4,2,704,128]{3,2,1,0:T(8,128)(2,1)S(1)}, bf16[4,2,704,128]{3,2,1,0:T(8,128)(2,1)S(1)}, u32[]{:S(2)}, u32[]{:S(2)}) collective-permute-start(bf16[4,2,704,128]{3,2,1,0:T(8,128)(2,1)S(1)} %slice.129), channel_id=1, source_target_pairs={{0,4},{1,5},{2,6},{3,7},{4,0},{5,1},{6,2},{7,3},{8,12},{9,13},{10,... | collective-permute-start | bytes 4325384 | tf_op jit(solution)/shard_map/ppermute | solution.py:25
  146.3 18.1 %collective-permute-start.80 = (bf16[2,704,128]{2,1,0:T(8,128)(2,1)S(1)}, bf16[2,704,128]{2,1,0:T(8,128)(2,1)S(1)}, u32[]{:S(2)}, u32[]{:S(2)}) collective-permute-start(bf16[2,704,128]{2,1,0:T(8,128)(2,1)S(1)} %slice.164), channel_id=1, source_target_pairs={{0,16},{1,17},{2,18},{3,19},{4,20},{5,21},{6,22},{7,23},{8,24},{9,... | collective-permute-start | bytes 1081352 | tf_op jit(solution)/shard_map/ppermute | solution.py:25
  148.7 73.4 %collective-permute-start.20 = (bf16[256,1024]{1,0:T(8,128)(2,1)}, bf16[256,1024]{1,0:T(8,128)(2,1)}, u32[]{:S(2)}, u32[]{:S(2)}) collective-permute-start(bf16[256,1024]{1,0:T(8,128)(2,1)} %get-tuple-element.142), channel_id=1, source_target_pairs={{0,2},{1,3},{2,0},{3,1},{4,6},{5,7},{6,4},{7,5},{8,10},{9,11},{10,... | collective-permute-start | bytes 1572872 | tf_op jit(solution)/shard_map/ppermute | solution.py:25
  153.4 70.4 %collective-permute-start.14 = (bf16[256,1024]{1,0:T(8,128)(2,1)}, bf16[256,1024]{1,0:T(8,128)(2,1)}, u32[]{:S(2)}, u32[]{:S(2)}) collective-permute-start(bf16[256,1024]{1,0:T(8,128)(2,1)} %get-tuple-element.140), channel_id=1, source_target_pairs={{0,2},{1,3},{2,0},{3,1},{4,6},{5,7},{6,4},{7,5},{8,10},{9,11},{10,... | collective-permute-start | bytes 1572872 | tf_op jit(solution)/shard_map/ppermute | solution.py:25
  157.4 7.3 %collective-permute-start.23 = (bf16[4,128,128]{2,1,0:T(8,128)(2,1)S(1)}, bf16[4,128,128]{2,1,0:T(8,128)(2,1)S(1)}, u32[]{:S(2)}, u32[]{:S(2)}) collective-permute-start(bf16[4,128,128]{2,1,0:T(8,128)(2,1)S(1)} %fusion.64), channel_id=1, source_target_pairs={{0,1},{1,0},{2,3},{3,2},{4,5},{5,4},{6,7},{7,6},{8,9},{9,8},{10,11... | collective-permute-start | bytes 393224 | tf_op jit(solution)/shard_map/ppermute | solution.py:25
  164.5 14.7 %collective-permute-start.81 = (bf16[1,704,128]{2,1,0:T(8,128)(2,1)S(1)}, bf16[1,704,128]{2,1,0:T(8,128)(2,1)S(1)}, u32[]{:S(2)}, u32[]{:S(2)}) collective-permute-start(bf16[1,704,128]{2,1,0:T(8,128)(2,1)S(1)} %slice.166), channel_id=1, source_target_pairs={{0,4},{1,5},{2,6},{3,7},{4,0},{5,1},{6,2},{7,3},{8,12},{9,13},{10,... | collective-permute-start | bytes 540680 | tf_op jit(solution)/shard_map/ppermute | solution.py:25
  164.9 15.1 %collective-permute-start.24 = (bf16[4,128,128]{2,1,0:T(8,128)(2,1)S(1)}, bf16[4,128,128]{2,1,0:T(8,128)(2,1)S(1)}, u32[]{:S(2)}, u32[]{:S(2)}) collective-permute-start(bf16[4,128,128]{2,1,0:T(8,128)(2,1)S(1)} %fusion.73), channel_id=1, source_target_pairs={{0,2},{1,3},{2,0},{3,1},{4,6},{5,7},{6,4},{7,5},{8,10},{9,11},{10,... | collective-permute-start | bytes 393224 | tf_op jit(solution)/shard_map/ppermute | solution.py:25
  182.9 43.8 %collective-permute-start.77 = (bf16[2,2,704,128]{3,2,1,0:T(8,128)(2,1)}, bf16[2,2,704,128]{3,2,1,0:T(8,128)(2,1)}, u32[]{:S(2)}, u32[]{:S(2)}) collective-permute-start(bf16[2,2,704,128]{3,2,1,0:T(8,128)(2,1)} %slice.158), channel_id=1, source_target_pairs={{0,8},{1,9},{2,10},{3,11},{4,12},{5,13},{6,14},{7,15},{8,0},{9,1},... | collective-permute-start | bytes 2162696 | tf_op jit(solution)/shard_map/ppermute | solution.py:25
  184.2 17.0 %collective-permute-start.26 = (bf16[4,128,128]{2,1,0:T(8,128)(2,1)S(1)}, bf16[4,128,128]{2,1,0:T(8,128)(2,1)S(1)}, u32[]{:S(2)}, u32[]{:S(2)}) collective-permute-start(bf16[4,128,128]{2,1,0:T(8,128)(2,1)S(1)} %fusion.61), channel_id=1, source_target_pairs={{0,8},{1,9},{2,10},{3,11},{4,12},{5,13},{6,14},{7,15},{8,0},{9,1},... | collective-permute-start | bytes 393224 | tf_op jit(solution)/shard_map/ppermute | solution.py:25
  201.3 7.0 %collective-permute-start.27 = (bf16[4,128,128]{2,1,0:T(8,128)(2,1)S(1)}, bf16[4,128,128]{2,1,0:T(8,128)(2,1)S(1)}, u32[]{:S(2)}, u32[]{:S(2)}) collective-permute-start(bf16[4,128,128]{2,1,0:T(8,128)(2,1)S(1)} %fusion.50), channel_id=1, source_target_pairs={{0,16},{1,17},{2,18},{3,19},{4,20},{5,21},{6,22},{7,23},{8,24},{9,... | collective-permute-start | bytes 393224 | tf_op jit(solution)/shard_map/ppermute | solution.py:25
  213.2 37.7 %collective-permute-start.29 = (bf16[3,512,1024]{2,1,0:T(8,128)(2,1)S(1)}, bf16[3,512,1024]{2,1,0:T(8,128)(2,1)S(1)}, u32[]{:S(2)}, u32[]{:S(2)}) collective-permute-start(bf16[3,512,1024]{2,1,0:T(8,128)(2,1)S(1)} %slice_bitcast_fusion), channel_id=1, source_target_pairs={{0,1},{1,0},{2,3},{3,2},{4,5},{5,4},{6,7},{7,6},{8,9},{9,8},{10,11... | collective-permute-start | bytes 9437192 | tf_op jit(solution)/shard_map/ppermute | solution.py:25
  222.1 25.9 %collective-permute-start.39 = (bf16[2,512,1024]{2,1,0:T(8,128)(2,1)}, bf16[2,512,1024]{2,1,0:T(8,128)(2,1)S(1)}, u32[]{:S(2)}, u32[]{:S(2)}) collective-permute-start(bf16[2,512,1024]{2,1,0:T(8,128)(2,1)} %slice_bitcast_fusion.2), channel_id=1, source_target_pairs={{0,1},{1,0},{2,3},{3,2},{4,5},{5,4},{6,7},{7,6},{8,9},{9,8},{10,11... | collective-permute-start | bytes 6291464 | tf_op jit(solution)/shard_map/ppermute | solution.py:25
  228.3 18.7 %collective-permute-start.78 = (bf16[1,2,704,128]{3,2,1,0:T(8,128)(2,1)S(1)}, bf16[1,2,704,128]{3,2,1,0:T(8,128)(2,1)S(1)}, u32[]{:S(2)}, u32[]{:S(2)}) collective-permute-start(bf16[1,2,704,128]{3,2,1,0:T(8,128)(2,1)S(1)} %slice.160), channel_id=1, source_target_pairs={{0,16},{1,17},{2,18},{3,19},{4,20},{5,21},{6,22},{7,23},{8,24},{9,... | collective-permute-start | bytes 1081352 | tf_op jit(solution)/shard_map/ppermute | solution.py:25
  249.2 12.7 %collective-permute-start.40 = (bf16[256,1024]{1,0:T(8,128)(2,1)S(1)}, bf16[256,1024]{1,0:T(8,128)(2,1)S(1)}, u32[]{:S(2)}, u32[]{:S(2)}) collective-permute-start(bf16[256,1024]{1,0:T(8,128)(2,1)S(1)} %dynamic-slice_bitcast_fusion.3), channel_id=1, source_target_pairs={{0,2},{1,3},{2,0},{3,1},{4,6},{5,7},{6,4},{7,5},{8,10},{9,11},{10,... | collective-permute-start | bytes 1572872 | tf_op jit(solution)/shard_map/ppermute | solution.py:25
  250.6 12.4 %collective-permute-start.49 = (bf16[256,1024]{1,0:T(8,128)(2,1)S(1)}, bf16[256,1024]{1,0:T(8,128)(2,1)S(1)}, u32[]{:S(2)}, u32[]{:S(2)}) collective-permute-start(bf16[256,1024]{1,0:T(8,128)(2,1)S(1)} %dynamic-slice_bitcast_fusion.2), channel_id=1, source_target_pairs={{0,4},{1,5},{2,6},{3,7},{4,0},{5,1},{6,2},{7,3},{8,12},{9,13},{10,... | collective-permute-start | bytes 1572872 | tf_op jit(solution)/shard_map/ppermute | solution.py:25
  252.9 12.2 %collective-permute-start.30 = (bf16[256,1024]{1,0:T(8,128)(2,1)S(1)}, bf16[256,1024]{1,0:T(8,128)(2,1)S(1)}, u32[]{:S(2)}, u32[]{:S(2)}) collective-permute-start(bf16[256,1024]{1,0:T(8,128)(2,1)S(1)} %dynamic-slice_bitcast_fusion.4), channel_id=1, source_target_pairs={{0,8},{1,9},{2,10},{3,11},{4,12},{5,13},{6,14},{7,15},{8,0},{9,1},... | collective-permute-start | bytes 1572872 | tf_op jit(solution)/shard_map/ppermute | solution.py:25
  253.0 30.3 %collective-permute-start.58 = (bf16[256,1024]{1,0:T(8,128)(2,1)S(1)}, bf16[256,1024]{1,0:T(8,128)(2,1)S(1)}, u32[]{:S(2)}, u32[]{:S(2)}) collective-permute-start(bf16[256,1024]{1,0:T(8,128)(2,1)S(1)} %dynamic-slice_bitcast_fusion.1), channel_id=1, source_target_pairs={{0,4},{1,5},{2,6},{3,7},{4,0},{5,1},{6,2},{7,3},{8,12},{9,13},{10,... | collective-permute-start | bytes 1572872 | tf_op jit(solution)/shard_map/ppermute | solution.py:25
  254.3 29.3 %collective-permute-start.67 = (bf16[256,1024]{1,0:T(8,128)(2,1)S(1)}, bf16[256,1024]{1,0:T(8,128)(2,1)S(1)}, u32[]{:S(2)}, u32[]{:S(2)}) collective-permute-start(bf16[256,1024]{1,0:T(8,128)(2,1)S(1)} %dynamic-slice_bitcast_fusion), channel_id=1, source_target_pairs={{0,2},{1,3},{2,0},{3,1},{4,6},{5,7},{6,4},{7,5},{8,10},{9,11},{10,... | collective-permute-start | bytes 1572872 | tf_op jit(solution)/shard_map/ppermute | solution.py:25
  262.2 17.6 %collective-permute-start.41 = (bf16[128,1024]{1,0:T(8,128)(2,1)S(1)}, bf16[128,1024]{1,0:T(8,128)(2,1)S(1)}, u32[]{:S(2)}, u32[]{:S(2)}) collective-permute-start(bf16[128,1024]{1,0:T(8,128)(2,1)S(1)} %dynamic-slice_bitcast_fusion.8), channel_id=1, source_target_pairs={{0,4},{1,5},{2,6},{3,7},{4,0},{5,1},{6,2},{7,3},{8,12},{9,13},{10,... | collective-permute-start | bytes 786440 | tf_op jit(solution)/shard_map/ppermute | solution.py:25
  263.2 16.8 %collective-permute-start.50 = (bf16[128,1024]{1,0:T(8,128)(2,1)S(1)}, bf16[128,1024]{1,0:T(8,128)(2,1)S(1)}, u32[]{:S(2)}, u32[]{:S(2)}) collective-permute-start(bf16[128,1024]{1,0:T(8,128)(2,1)S(1)} %dynamic-slice_bitcast_fusion.7), channel_id=1, source_target_pairs={{0,8},{1,9},{2,10},{3,11},{4,12},{5,13},{6,14},{7,15},{8,0},{9,1},... | collective-permute-start | bytes 786440 | tf_op jit(solution)/shard_map/ppermute | solution.py:25
  265.3 29.7 %collective-permute-start.31 = (bf16[128,1024]{1,0:T(8,128)(2,1)S(1)}, bf16[128,1024]{1,0:T(8,128)(2,1)S(1)}, u32[]{:S(2)}, u32[]{:S(2)}) collective-permute-start(bf16[128,1024]{1,0:T(8,128)(2,1)S(1)} %dynamic-slice_bitcast_fusion.9), channel_id=1, source_target_pairs={{0,16},{1,17},{2,18},{3,19},{4,20},{5,21},{6,22},{7,23},{8,24},{9,... | collective-permute-start | bytes 786440 | tf_op jit(solution)/shard_map/ppermute | solution.py:25
  283.6 16.6 %collective-permute-start.59 = (bf16[128,1024]{1,0:T(8,128)(2,1)S(1)}, bf16[128,1024]{1,0:T(8,128)(2,1)S(1)}, u32[]{:S(2)}, u32[]{:S(2)}) collective-permute-start(bf16[128,1024]{1,0:T(8,128)(2,1)S(1)} %dynamic-slice_bitcast_fusion.6), channel_id=1, source_target_pairs={{0,8},{1,9},{2,10},{3,11},{4,12},{5,13},{6,14},{7,15},{8,0},{9,1},... | collective-permute-start | bytes 786440 | tf_op jit(solution)/shard_map/ppermute | solution.py:25
  283.9 17.8 %collective-permute-start.68 = (bf16[128,1024]{1,0:T(8,128)(2,1)S(1)}, bf16[128,1024]{1,0:T(8,128)(2,1)S(1)}, u32[]{:S(2)}, u32[]{:S(2)}) collective-permute-start(bf16[128,1024]{1,0:T(8,128)(2,1)S(1)} %dynamic-slice_bitcast_fusion.5), channel_id=1, source_target_pairs={{0,4},{1,5},{2,6},{3,7},{4,0},{5,1},{6,2},{7,3},{8,12},{9,13},{10,... | collective-permute-start | bytes 786440 | tf_op jit(solution)/shard_map/ppermute | solution.py:25
  284.3 7.4 %collective-permute-start.43 = (bf16[32,1024]{1,0:T(8,128)(2,1)S(1)}, bf16[32,1024]{1,0:T(8,128)(2,1)S(1)}, u32[]{:S(2)}, u32[]{:S(2)}) collective-permute-start(bf16[32,1024]{1,0:T(8,128)(2,1)S(1)} %dynamic-slice_bitcast_fusion.18), channel_id=1, source_target_pairs={{0,16},{1,17},{2,18},{3,19},{4,20},{5,21},{6,22},{7,23},{8,24},{9,... | collective-permute-start | bytes 196616 | tf_op jit(solution)/shard_map/ppermute | solution.py:25
  287.1 7.5 %collective-permute-start.52 = (bf16[32,1024]{1,0:T(8,128)(2,1)S(1)}, bf16[32,1024]{1,0:T(8,128)(2,1)S(1)}, u32[]{:S(2)}, u32[]{:S(2)}) collective-permute-start(bf16[32,1024]{1,0:T(8,128)(2,1)S(1)} %dynamic-slice_bitcast_fusion.17), channel_id=1, source_target_pairs={{0,2},{1,3},{2,0},{3,1},{4,6},{5,7},{6,4},{7,5},{8,10},{9,11},{10,... | collective-permute-start | bytes 196616 | tf_op jit(solution)/shard_map/ppermute | solution.py:25
  299.1 7.7 %collective-permute-start.54 = (bf16[64,1024]{1,0:T(8,128)(2,1)S(1)}, bf16[64,1024]{1,0:T(8,128)(2,1)S(1)}, u32[]{:S(2)}, u32[]{:S(2)}) collective-permute-start(bf16[64,1024]{1,0:T(8,128)(2,1)S(1)} %pad_maximum_fusion.24), channel_id=1, source_target_pairs={{0,16},{1,17},{2,18},{3,19},{4,20},{5,21},{6,22},{7,23},{8,24},{9,... | collective-permute-start | bytes 393224 | tf_op jit(solution)/shard_map/ppermute | solution.py:25
  300.3 8.5 %collective-permute-start.60 = (bf16[64,1024]{1,0:T(8,128)(2,1)S(1)}, bf16[64,1024]{1,0:T(8,128)(2,1)S(1)}, u32[]{:S(2)}, u32[]{:S(2)}) collective-permute-start(bf16[64,1024]{1,0:T(8,128)(2,1)S(1)} %dynamic-slice_bitcast_fusion.11), channel_id=1, source_target_pairs={{0,16},{1,17},{2,18},{3,19},{4,20},{5,21},{6,22},{7,23},{8,24},{9,... | collective-permute-start | bytes 393224 | tf_op jit(solution)/shard_map/ppermute | solution.py:25
  301.8 8.0 %collective-permute-start.69 = (bf16[64,1024]{1,0:T(8,128)(2,1)S(1)}, bf16[64,1024]{1,0:T(8,128)(2,1)S(1)}, u32[]{:S(2)}, u32[]{:S(2)}) collective-permute-start(bf16[64,1024]{1,0:T(8,128)(2,1)S(1)} %dynamic-slice_bitcast_fusion.10), channel_id=1, source_target_pairs={{0,8},{1,9},{2,10},{3,11},{4,12},{5,13},{6,14},{7,15},{8,0},{9,1},... | collective-permute-start | bytes 393224 | tf_op jit(solution)/shard_map/ppermute | solution.py:25
  302.0 8.0 %collective-permute-start.33 = (bf16[32,1024]{1,0:T(8,128)(2,1)S(1)}, bf16[32,1024]{1,0:T(8,128)(2,1)S(1)}, u32[]{:S(2)}, u32[]{:S(2)}) collective-permute-start(bf16[32,1024]{1,0:T(8,128)(2,1)S(1)} %dynamic-slice_bitcast_fusion.19), channel_id=1, source_target_pairs={{0,4},{1,5},{2,6},{3,7},{4,0},{5,1},{6,2},{7,3},{8,12},{9,13},{10,... | collective-permute-start | bytes 196616 | tf_op jit(solution)/shard_map/ppermute | solution.py:25
  302.4 20.1 %collective-permute-start.46 = (bf16[128,1024]{1,0:T(8,128)(2,1)S(1)}, bf16[128,1024]{1,0:T(8,128)(2,1)S(1)}, u32[]{:S(2)}, u32[]{:S(2)}) collective-permute-start(bf16[128,1024]{1,0:T(8,128)(2,1)S(1)} %pad_maximum_fusion.18), channel_id=1, source_target_pairs={{0,4},{1,5},{2,6},{3,7},{4,0},{5,1},{6,2},{7,3},{8,12},{9,13},{10,... | collective-permute-start | bytes 786440 | tf_op jit(solution)/shard_map/ppermute | solution.py:25
  306.9 15.8 %collective-permute-start.55 = (bf16[128,1024]{1,0:T(8,128)(2,1)S(1)}, bf16[128,1024]{1,0:T(8,128)(2,1)S(1)}, u32[]{:S(2)}, u32[]{:S(2)}) collective-permute-start(bf16[128,1024]{1,0:T(8,128)(2,1)S(1)} %pad_maximum_fusion.19), channel_id=1, source_target_pairs={{0,8},{1,9},{2,10},{3,11},{4,12},{5,13},{6,14},{7,15},{8,0},{9,1},... | collective-permute-start | bytes 786440 | tf_op jit(solution)/shard_map/ppermute | solution.py:25
  310.0 7.3 %collective-permute-start.34 = (bf16[32,1024]{1,0:T(8,128)(2,1)S(1)}, bf16[32,1024]{1,0:T(8,128)(2,1)S(1)}, u32[]{:S(2)}, u32[]{:S(2)}) collective-permute-start(bf16[32,1024]{1,0:T(8,128)(2,1)S(1)} %fusion.69), channel_id=1, source_target_pairs={{0,4},{1,5},{2,6},{3,7},{4,0},{5,1},{6,2},{7,3},{8,12},{9,13},{10,... | collective-permute-start | bytes 196616 | tf_op jit(solution)/shard_map/ppermute | solution.py:25
  317.8 7.4 %collective-permute-start.63 = (bf16[64,1024]{1,0:T(8,128)(2,1)S(1)}, bf16[64,1024]{1,0:T(8,128)(2,1)S(1)}, u32[]{:S(2)}, u32[]{:S(2)}) collective-permute-start(bf16[64,1024]{1,0:T(8,128)(2,1)S(1)} %pad_maximum_fusion.25), channel_id=1, source_target_pairs={{0,16},{1,17},{2,18},{3,19},{4,20},{5,21},{6,22},{7,23},{8,24},{9,... | collective-permute-start | bytes 393224 | tf_op jit(solution)/shard_map/ppermute | solution.py:25
  319.2 7.1 %collective-permute-start.72 = (bf16[64,1024]{1,0:T(8,128)(2,1)S(1)}, bf16[64,1024]{1,0:T(8,128)(2,1)S(1)}, u32[]{:S(2)}, u32[]{:S(2)}) collective-permute-start(bf16[64,1024]{1,0:T(8,128)(2,1)S(1)} %pad_maximum_fusion.26), channel_id=1, source_target_pairs={{0,8},{1,9},{2,10},{3,11},{4,12},{5,13},{6,14},{7,15},{8,0},{9,1},... | collective-permute-start | bytes 393224 | tf_op jit(solution)/shard_map/ppermute | solution.py:25
  322.0 13.1 %collective-permute-start.36 = (bf16[128,1024]{1,0:T(8,128)(2,1)S(1)}, bf16[128,1024]{1,0:T(8,128)(2,1)S(1)}, u32[]{:S(2)}, u32[]{:S(2)}) collective-permute-start(bf16[128,1024]{1,0:T(8,128)(2,1)S(1)} %pad_maximum_fusion.17), channel_id=1, source_target_pairs={{0,16},{1,17},{2,18},{3,19},{4,20},{5,21},{6,22},{7,23},{8,24},{9,... | collective-permute-start | bytes 786440 | tf_op jit(solution)/shard_map/ppermute | solution.py:25
  322.6 16.1 %collective-permute-start.47 = (bf16[256,1024]{1,0:T(8,128)(2,1)S(1)}, bf16[256,1024]{1,0:T(8,128)(2,1)S(1)}, u32[]{:S(2)}, u32[]{:S(2)}) collective-permute-start(bf16[256,1024]{1,0:T(8,128)(2,1)S(1)} %pad_maximum_fusion.11), channel_id=1, source_target_pairs={{0,2},{1,3},{2,0},{3,1},{4,6},{5,7},{6,4},{7,5},{8,10},{9,11},{10,... | collective-permute-start | bytes 1572872 | tf_op jit(solution)/shard_map/ppermute | solution.py:25
  322.9 32.5 %collective-permute-start.56 = (bf16[256,1024]{1,0:T(8,128)(2,1)S(1)}, bf16[256,1024]{1,0:T(8,128)(2,1)S(1)}, u32[]{:S(2)}, u32[]{:S(2)}) collective-permute-start(bf16[256,1024]{1,0:T(8,128)(2,1)S(1)} %pad_maximum_fusion.12), channel_id=1, source_target_pairs={{0,4},{1,5},{2,6},{3,7},{4,0},{5,1},{6,2},{7,3},{8,12},{9,13},{10,... | collective-permute-start | bytes 1572872 | tf_op jit(solution)/shard_map/ppermute | solution.py:25
  325.3 12.6 %collective-permute-start.64 = (bf16[128,1024]{1,0:T(8,128)(2,1)S(1)}, bf16[128,1024]{1,0:T(8,128)(2,1)S(1)}, u32[]{:S(2)}, u32[]{:S(2)}) collective-permute-start(bf16[128,1024]{1,0:T(8,128)(2,1)S(1)} %pad_maximum_fusion.20), channel_id=1, source_target_pairs={{0,8},{1,9},{2,10},{3,11},{4,12},{5,13},{6,14},{7,15},{8,0},{9,1},... | collective-permute-start | bytes 786440 | tf_op jit(solution)/shard_map/ppermute | solution.py:25
  326.3 11.9 %collective-permute-start.73 = (bf16[128,1024]{1,0:T(8,128)(2,1)S(1)}, bf16[128,1024]{1,0:T(8,128)(2,1)S(1)}, u32[]{:S(2)}, u32[]{:S(2)}) collective-permute-start(bf16[128,1024]{1,0:T(8,128)(2,1)S(1)} %pad_maximum_fusion.21), channel_id=1, source_target_pairs={{0,4},{1,5},{2,6},{3,7},{4,0},{5,1},{6,2},{7,3},{8,12},{9,13},{10,... | collective-permute-start | bytes 786440 | tf_op jit(solution)/shard_map/ppermute | solution.py:25
  335.3 20.5 %collective-permute-start.37 = (bf16[256,1024]{1,0:T(8,128)(2,1)S(1)}, bf16[256,1024]{1,0:T(8,128)(2,1)S(1)}, u32[]{:S(2)}, u32[]{:S(2)}) collective-permute-start(bf16[256,1024]{1,0:T(8,128)(2,1)S(1)} %pad_maximum_fusion.10), channel_id=1, source_target_pairs={{0,8},{1,9},{2,10},{3,11},{4,12},{5,13},{6,14},{7,15},{8,0},{9,1},... | collective-permute-start | bytes 1572872 | tf_op jit(solution)/shard_map/ppermute | solution.py:25
  338.1 18.6 %collective-permute-start.65 = (bf16[256,1024]{1,0:T(8,128)(2,1)S(1)}, bf16[256,1024]{1,0:T(8,128)(2,1)S(1)}, u32[]{:S(2)}, u32[]{:S(2)}) collective-permute-start(bf16[256,1024]{1,0:T(8,128)(2,1)S(1)} %pad_maximum_fusion.13), channel_id=1, source_target_pairs={{0,4},{1,5},{2,6},{3,7},{4,0},{5,1},{6,2},{7,3},{8,12},{9,13},{10,... | collective-permute-start | bytes 1572872 | tf_op jit(solution)/shard_map/ppermute | solution.py:25
  338.4 20.9 %collective-permute-start.74 = (bf16[256,1024]{1,0:T(8,128)(2,1)S(1)}, bf16[256,1024]{1,0:T(8,128)(2,1)S(1)}, u32[]{:S(2)}, u32[]{:S(2)}) collective-permute-start(bf16[256,1024]{1,0:T(8,128)(2,1)S(1)} %pad_maximum_fusion.14), channel_id=1, source_target_pairs={{0,2},{1,3},{2,0},{3,1},{4,6},{5,7},{6,4},{7,5},{8,10},{9,11},{10,... | collective-permute-start | bytes 1572872 | tf_op jit(solution)/shard_map/ppermute | solution.py:25
  339.0 24.1 %collective-permute-start.48 = (bf16[512,1024]{1,0:T(8,128)(2,1)S(1)}, bf16[512,1024]{1,0:T(8,128)(2,1)S(1)}, u32[]{:S(2)}, u32[]{:S(2)}) collective-permute-start(bf16[512,1024]{1,0:T(8,128)(2,1)S(1)} %pad_maximum_fusion.4), channel_id=1, source_target_pairs={{0,1},{1,0},{2,3},{3,2},{4,5},{5,4},{6,7},{7,6},{8,9},{9,8},{10,11... | collective-permute-start | bytes 3145736 | tf_op jit(solution)/shard_map/ppermute | solution.py:25
  355.7 10.4 %collective-permute-start.57 = (bf16[512,1024]{1,0:T(8,128)(2,1)S(1)}, bf16[512,1024]{1,0:T(8,128)(2,1)S(1)}, u32[]{:S(2)}, u32[]{:S(2)}) collective-permute-start(bf16[512,1024]{1,0:T(8,128)(2,1)S(1)} %pad_maximum_fusion.5), channel_id=1, source_target_pairs={{0,1},{1,0},{2,3},{3,2},{4,5},{5,4},{6,7},{7,6},{8,9},{9,8},{10,11... | collective-permute-start | bytes 3145736 | tf_op jit(solution)/shard_map/ppermute | solution.py:25
  356.2 13.0 %collective-permute-start.38 = (bf16[512,1024]{1,0:T(8,128)(2,1)S(1)}, bf16[512,1024]{1,0:T(8,128)(2,1)S(1)}, u32[]{:S(2)}, u32[]{:S(2)}) collective-permute-start(bf16[512,1024]{1,0:T(8,128)(2,1)S(1)} %pad_maximum_fusion.3), channel_id=1, source_target_pairs={{0,1},{1,0},{2,3},{3,2},{4,5},{5,4},{6,7},{7,6},{8,9},{9,8},{10,11... | collective-permute-start | bytes 3145736 | tf_op jit(solution)/shard_map/ppermute | solution.py:25
  357.0 15.2 %collective-permute-start.66 = (bf16[512,1024]{1,0:T(8,128)(2,1)S(1)}, bf16[512,1024]{1,0:T(8,128)(2,1)S(1)}, u32[]{:S(2)}, u32[]{:S(2)}) collective-permute-start(bf16[512,1024]{1,0:T(8,128)(2,1)S(1)} %pad_maximum_fusion.6), channel_id=1, source_target_pairs={{0,1},{1,0},{2,3},{3,2},{4,5},{5,4},{6,7},{7,6},{8,9},{9,8},{10,11... | collective-permute-start | bytes 3145736 | tf_op jit(solution)/shard_map/ppermute | solution.py:25
  359.6 15.7 %collective-permute-start.75 = (bf16[512,1024]{1,0:T(8,128)(2,1)S(1)}, bf16[512,1024]{1,0:T(8,128)(2,1)S(1)}, u32[]{:S(2)}, u32[]{:S(2)}) collective-permute-start(bf16[512,1024]{1,0:T(8,128)(2,1)S(1)} %pad_maximum_fusion.7), channel_id=1, source_target_pairs={{0,1},{1,0},{2,3},{3,2},{4,5},{5,4},{6,7},{7,6},{8,9},{9,8},{10,11... | collective-permute-start | bytes 3145736 | tf_op jit(solution)/shard_map/ppermute | solution.py:25
  (83 other events, 514.1 us)

commit v4 on v3

--- a/solution.py
+++ b/solution.py
@@ -716,7 +716,7 @@
     far = ring[1:]
 
     normed, pre_key, keys, values, contrib, local = kv(
-        rate, tokens, key_weight, value_weight, cosine, sine, 2
+        rate, tokens, key_weight, value_weight, cosine, sine, 1
     )
     state, mark = decayed_scan(local, rate, float(count), span, place, False)
     pre_query, query, gate, intra = qu(
@@ -783,6 +783,25 @@
     query_back, key_part, value_part = query_side(
         rate, pre_query, query, keys, values, cosine, sine, backs, [j[4] for j in joined], 2
     )
+    rest = bits_of(devices)[1:]
+    lines = [
+        [m for m in rest if m < members],
+        [m for m in rest if members <= m < members * across],
+        [m for m in rest if m >= members * across],
+    ]
+
+    def order_of(k):
+        return [m for i in range(3) for m in lines[(i + k) % 3]]
+
+    def chip_sums(part):
+        kept = (part[0].astype(FLOAT) + swap(part[1], 1).astype(FLOAT)).astype(BHALF)
+        return [kept[k] for k in range(kept.shape[0])]
+
+    def rest_of(piece, k, done):
+        order = order_of(k)
+        piece = double(halve(piece, order[done:], place), list(reversed(order)), place)
+        return double(piece, [1], place).astype(FLOAT)
+
     gated = jnp.concatenate([j[1] for j in joined], axis=0)
     early = grads(
         core,
@@ -794,16 +813,20 @@
             (1, [2 * blocks]),
         ],
     )
+    moved = [halve(piece, order_of(k)[:1], place) for k, piece in enumerate(chip_sums(early))]
     key_back, value_back = key_side(
         rate, pre_key, keys, values, key_part, value_part, cosine, sine, outer,
-        [t[4] for t in turned], 2,
+        [t[4] for t in turned], 1,
     )
     late = grads(core, [normed], [key_back, value_back], [(0, [0]), (0, [1])])
     weights = (query_weight, key_weight, value_weight, modulate_weight)
+    late_sums = chip_sums(late)
+    late_moved = [halve(p, order_of(k)[:1], place) for k, p in enumerate(late_sums)]
+    late_key = after(key_back, *late_sums)
     tokens_grad = jnp.concatenate(
         [
             tokens_side(
-                b, tokens, turned[b][0], query_back, key_back, value_back, turned[b][2], weights
+                b, tokens, turned[b][0], query_back, late_key, value_back, turned[b][2], weights
             )
             for b in range(blocks)
         ],
@@ -825,24 +848,8 @@
     down_grad = fold(down_part, masks[1]).astype(FLOAT)
     gate_grad, linear_grad = pair_grad[0].T, pair_grad[1].T
 
-    rest = bits_of(devices)[1:]
-    lines = [
-        [m for m in rest if m < members],
-        [m for m in rest if members <= m < members * across],
-        [m for m in rest if m >= members * across],
-    ]
-
-    def reduced(part):
-        kept = (part[0].astype(FLOAT) + swap(part[1], 1).astype(FLOAT)).astype(BHALF)
-        outs = []
-        for k in range(kept.shape[0]):
-            order = [m for i in range(3) for m in lines[(i + k) % 3]]
-            piece = double(halve(kept[k], order, place), list(reversed(order)), place)
-            outs.append(double(piece, [1], place).astype(FLOAT))
-        return outs
-
-    output_grad, modulate_grad, query_grad = reduced(early)
-    key_grad, value_grad = reduced(late)
+    output_grad, modulate_grad, query_grad = [rest_of(p, k, 1) for k, p in enumerate(moved)]
+    key_grad, value_grad = [rest_of(p, k, 1) for k, p in enumerate(late_moved)]
     return (
         mixed,
         tokens_grad,

time: 384 us -> 384 us (level)
  no operation moved by 1% of the time
where the time goes in v4:
time: 384 us; the launch traced here: 377 us
  waiting for transfers between devices  121 us (32%)
  starting transfers between devices  92.9 us (24%)
  Pallas kernels  80 us (21%)
  other arithmetic  47.1 us (12%)
  local copies, waits for them, and re-layouts  33 us (9%)
    ppermute x82, waiting for transfers between devices, swap(): return lax.ppermute(value, axes, [(s, s ^ mask) for s in range(count)])  121 us
    ppermute x82, starting transfers between devices, swap(): return lax.ppermute(value, axes, [(s, s ^ mask) for s in range(count)])  92.9 us
    unnamed x130, local copies, waits for them, and re-layouts  25.6 us
    pallas_call x4, Pallas kernels, unit(): call(unit_body, (1,), [piece] * 2 + [cot] * 2 + [whole(down.shape)] * 3,...  24.9 us
    pallas_call x1, Pallas kernels, unit_grads(): call(functools.partial(unit_grads_body, n, orders), (1,), [SMEM_SPEC] + [...  13.3 us
    convert_element_type x5, other arithmetic, rest_of(): return double(piece, [1], place).astype(FLOAT)  12.2 us
  transfers between devices with their start and end apart: 82, of which 30 were waited for; matrix products, arithmetic and copies ran while one was open for 12% of the time, Pallas kernels for 20%

profile of v4, /device:TPU:1, one launch (start us, length us, event | category | flops | bytes accessed | tf_op | source)
XLA Modules:
  0.0 377.2 jit_solution(11740169103335400263)
XLA Ops:
  3.3 1.7 copy-done.6
  6.5 3.6 shard_map.186
  17.0 2.7 collective-permute-start.1
  19.7 3.7 collective-permute-done.1
  26.2 3.2 collective-permute-done.2
  31.4 3.0 collective-permute-done.3
  34.4 1.7 fusion.37
  36.1 2.2 collective-permute-start.4
  39.5 2.9 collective-permute-done.4
  43.6 3.9 %collective-permute-start.5 = (bf16[4,128,128]{2,1,0:T(8,128)(2,1)S(1)}, bf16[4,128,128]{2,1,0:T(8,128)(2,1)S(1)}, u32[]{:S(2)}, u32[]{:S(2)}) collective-permute-start(bf16[4,128,128]{2,1,0:T(8,128)(2,1)S(1)} %get-tuple-element.132), channel_id=1, source_target_pairs={{0,1},{1,0},{2,3},{3,2},{4,5},{5,4},{6,7},{7,6},{8,9},{9,8},{10,11... | collective-permute-start | bytes 393224 | tf_op jit(solution)/shard_map/ppermute | solution.py:25
  53.8 5.5 %shard_map.187 = (f32[512,1024]{1,0:T(8,128)S(1)}, bf16[512,1024]{1,0:T(8,128)(2,1)S(1)}, f32[512,1024]{1,0:T(8,128)S(1)}, f32[512,1024]{1,0:T(8,128)S(1)}) custom-call(f32[8]{0:T(128)S(1)} %get-tuple-element.216.rate, bf16[512,1024]{1,0:T(8,128)(2,1)S(1)} %copy-done.57, bf16[1024,1024]{1,0:T(8,128)(2,1)S(1)} %copy-done.10, ...), custom_call_target="tpu_custom_call" | custom-call | flops 2147483648 | bytes 14680064 | tf_op jit(solution)/shard_map/pallas_call | solution.py:292
  59.6 2.8 copy-done
  62.4 1.8 shard_map.191
  67.1 1.8 shard_map.188
  72.6 6.2 %collective-permute-done.17.n0.refs_21_ = bf16[256,1024]{1,0:T(8,128)(2,1)S(1)} collective-permute-done((bf16[256,1024]{1,0:T(8,128)(2,1)S(1)}, bf16[256,1024]{1,0:T(8,128)(2,1)S(1)}, u32[]{:S(2)}, u32[]{:S(2)}) %collective-permute-start.17) | collective-permute-done | bytes 524320 | tf_op jit(solution)/shard_map/ppermute | solution.py:25
  80.1 7.2 %shard_map.192 = (f32[2,256,1024]{2,1,0:T(8,128)S(1)}, bf16[2,256,1024]{2,1,0:T(8,128)(2,1)}, bf16[512,704]{1,0:T(8,128)(2,1)S(1)}, bf16[512,704]{1,0:T(8,128)(2,1)S(1)}, bf16[512,704]{1,0:T(8,128)(2,1)S(1)}) custom-call(bf16[256,1024]{1,0:T(8,128)(2,1)S(1)} %get-tuple-element.84.n0.refs_7_, bf16[256,1024]{1,0:T(8,128)(2,1)S(1)} %collective-permute-done.15.n1.refs_8_, ...), custom_call_target="tpu_custom_call" | custom-call | flops 4429185024 | bytes 9568256 | tf_op jit(solution)/shard_map/pallas_call | solution.py:380
  90.9 7.2 %shard_map.189 = (f32[2,256,1024]{2,1,0:T(8,128)S(1)}, bf16[2,256,1024]{2,1,0:T(8,128)(2,1)}, bf16[512,704]{1,0:T(8,128)(2,1)S(1)}, bf16[512,704]{1,0:T(8,128)(2,1)S(1)}, bf16[512,704]{1,0:T(8,128)(2,1)S(1)}) custom-call(bf16[256,1024]{1,0:T(8,128)(2,1)S(1)} %get-tuple-element.77.n0.refs_0_, bf16[256,1024]{1,0:T(8,128)(2,1)S(1)} %collective-permute-done.6.n1.refs_1_, ...), custom_call_target="tpu_custom_call" | custom-call | flops 4429185024 | bytes 9568256 | tf_op jit(solution)/shard_map/pallas_call | solution.py:380
  99.4 5.4 %shard_map.193 = (f32[2,256,1024]{2,1,0:T(8,128)S(1)}, bf16[2,256,1024]{2,1,0:T(8,128)(2,1)S(1)}, bf16[512,704]{1,0:T(8,128)(2,1)S(1)}, bf16[512,704]{1,0:T(8,128)(2,1)S(1)}, bf16[512,704]{1,0:T(8,128)(2,1)S(1)}) custom-call(bf16[256,1024]{1,0:T(8,128)(2,1)S(1)} %collective-permute-done.17.n0.refs_21_, ...), custom_call_target="tpu_custom_call" | custom-call | flops 4429185024 | bytes 9568256 | tf_op jit(solution)/shard_map/pallas_call | solution.py:380
  105.3 5.1 %shard_map.190 = (f32[2,256,1024]{2,1,0:T(8,128)S(1)}, bf16[2,256,1024]{2,1,0:T(8,128)(2,1)S(1)}, bf16[512,704]{1,0:T(8,128)(2,1)S(1)}, bf16[512,704]{1,0:T(8,128)(2,1)S(1)}, bf16[512,704]{1,0:T(8,128)(2,1)S(1)}) custom-call(bf16[256,1024]{1,0:T(8,128)(2,1)S(1)} %collective-permute-done.9.n0.refs_14_, ...), custom_call_target="tpu_custom_call" | custom-call | flops 4429185024 | bytes 9568256 | tf_op jit(solution)/shard_map/pallas_call | solution.py:380
  110.6 13.3 %shard_map.202 = (bf16[8,2,704,128]{3,2,1,0:T(8,128)(2,1)S(1)}, bf16[8,704,128]{2,1,0:T(8,128)(2,1)S(1)}) custom-call(s32[1]{0:T(128)} %bitcast.95.place, bf16[256,1024]{1,0:T(8,128)(2,1)S(1)} %get-tuple-element.77.n0.refs_0_, bf16[256,1024]{1,0:T(8,128)(2,1)S(1)} %collective-permute-done.6.n1.refs_1_, bf16[512,1024]{1,0:T(8,128)(2,1)} %refs_9_, ...), custom_call_target="tpu_custom_call" | custom-call | flops 8858370048 | bytes 21364736 | tf_op jit(solution)/shard_map/pallas_call | solution.py:464
  132.8 9.7 %collective-permute-done.79 = bf16[4,704,128]{2,1,0:T(8,128)(2,1)} collective-permute-done((bf16[4,704,128]{2,1,0:T(8,128)(2,1)}, bf16[4,704,128]{2,1,0:T(8,128)(2,1)}, u32[]{:S(2)}, u32[]{:S(2)}) %collective-permute-start.79) | collective-permute-done | bytes 720928 | tf_op jit(solution)/shard_map/ppermute | solution.py:25
  145.2 2.4 collective-permute-start.80
  148.9 3.4 shard_map.195
  152.7 3.5 shard_map.194
  156.4 2.2 collective-permute-start.23
  158.6 4.7 %collective-permute-done.80 = bf16[2,704,128]{2,1,0:T(8,128)(2,1)S(1)} collective-permute-done((bf16[2,704,128]{2,1,0:T(8,128)(2,1)S(1)}, bf16[2,704,128]{2,1,0:T(8,128)(2,1)S(1)}, u32[]{:S(2)}, u32[]{:S(2)}) %collective-permute-start.80) | collective-permute-done | bytes 360480 | tf_op jit(solution)/shard_map/ppermute | solution.py:25
  165.1 13.0 %collective-permute-done.81 = bf16[1,704,128]{2,1,0:T(8,128)(2,1)S(1)} collective-permute-done((bf16[1,704,128]{2,1,0:T(8,128)(2,1)S(1)}, bf16[1,704,128]{2,1,0:T(8,128)(2,1)S(1)}, u32[]{:S(2)}, u32[]{:S(2)}) %collective-permute-start.81) | collective-permute-done | bytes 180256 | tf_op jit(solution)/shard_map/ppermute | solution.py:25
  183.8 7.6 %shard_map.196 = (bf16[512,1024]{1,0:T(8,128)(2,1)S(1)}, f32[512,1024]{1,0:T(8,128)S(1)}, f32[512,1024]{1,0:T(8,128)S(1)}) custom-call(f32[8]{0:T(128)S(1)} %get-tuple-element.216.rate, f32[512,1024]{1,0:T(8,128)S(1)} %copy-done.40, bf16[512,1024]{1,0:T(8,128)(2,1)S(1)} %get-tuple-element.72.query, bf16[512,1024]{1,0:T(8,128)(2,1)S(1)} %copy-done.26, ...), custom_call_target="tpu_custom_call" | custom-call | flops 1610612736 | bytes 12582912 | tf_op jit(solution)/shard_map/pallas_call | solution.py:559
  191.4 8.6 %collective-permute-done.26 = bf16[4,128,128]{2,1,0:T(8,128)(2,1)S(1)} collective-permute-done((bf16[4,128,128]{2,1,0:T(8,128)(2,1)S(1)}, bf16[4,128,128]{2,1,0:T(8,128)(2,1)S(1)}, u32[]{:S(2)}, u32[]{:S(2)}) %collective-permute-start.26) | collective-permute-done | bytes 131104 | tf_op jit(solution)/shard_map/ppermute | solution.py:25
  200.2 3.1 collective-permute-start.27
  203.3 3.9 %shard_map.200 = bf16[2,3,512,1024]{3,2,1,0:T(8,128)(2,1)S(1)} custom-call(s32[1]{0:T(128)} %bitcast.30.core, bf16[512,1024]{1,0:T(8,128)(2,1)S(1)} %pad_maximum_fusion.2.refs_0_, bf16[512,1024]{1,0:T(8,128)(2,1)S(1)} %copy-done.58, bf16[256,1024]{1,0:T(8,128)(2,1)S(1)} %get-tuple-element.110.refs_2_, bf16[256,1024]{1,0:T(8,128)(2,1)S(1)} %get-tuple-element.111.refs_3_, ...), custom_call_target="tpu_custom_call" | custom-call | flops 3221225472 | bytes 12582912 | tf_op jit(solution)/shard_map/pallas_call | solution.py:646
  207.5 4.3 %collective-permute-start.28 = (bf16[4,128,128]{2,1,0:T(8,128)(2,1)S(1)}, bf16[4,128,128]{2,1,0:T(8,128)(2,1)S(1)}, u32[]{:S(2)}, u32[]{:S(2)}) collective-permute-start(bf16[4,128,128]{2,1,0:T(8,128)(2,1)S(1)} %get-tuple-element.126), channel_id=1, source_target_pairs={{0,1},{1,0},{2,3},{3,2},{4,5},{5,4},{6,7},{7,6},{8,9},{9,8},{10,11... | collective-permute-start | bytes 393224 | tf_op jit(solution)/shard_map/ppermute | solution.py:25
  213.7 2.4 shard_map.197
  216.2 3.0 shard_map.201
  220.7 1.7 fusion.8
  222.4 1.7 fusion.10
  228.3 2.6 shard_map.199
  230.9 2.6 shard_map.198
  235.1 10.5 %collective-permute-done.78 = bf16[1,2,704,128]{3,2,1,0:T(8,128)(2,1)S(1)} collective-permute-done((bf16[1,2,704,128]{3,2,1,0:T(8,128)(2,1)S(1)}, bf16[1,2,704,128]{3,2,1,0:T(8,128)(2,1)S(1)}, u32[]{:S(2)}, u32[]{:S(2)}) %collective-permute-start.78) | collective-permute-done | bytes 360480 | tf_op jit(solution)/shard_map/ppermute | solution.py:25
  253.2 7.3 %collective-permute-done.40 = bf16[256,1024]{1,0:T(8,128)(2,1)S(1)} collective-permute-done((bf16[256,1024]{1,0:T(8,128)(2,1)S(1)}, bf16[256,1024]{1,0:T(8,128)(2,1)S(1)}, u32[]{:S(2)}, u32[]{:S(2)}) %collective-permute-start.40) | collective-permute-done | bytes 524320 | tf_op jit(solution)/shard_map/ppermute | solution.py:25
  261.9 1.7 collective-permute-done.30
  263.8 2.0 collective-permute-start.31
  265.8 12.6 %collective-permute-done.41 = bf16[128,1024]{1,0:T(8,128)(2,1)S(1)} collective-permute-done((bf16[128,1024]{1,0:T(8,128)(2,1)S(1)}, bf16[128,1024]{1,0:T(8,128)(2,1)S(1)}, u32[]{:S(2)}, u32[]{:S(2)}) %collective-permute-start.41) | collective-permute-done | bytes 262176 | tf_op jit(solution)/shard_map/ppermute | solution.py:25
  278.7 3.2 collective-permute-start.51
  285.9 4.3 %collective-permute-done.43 = bf16[32,1024]{1,0:T(8,128)(2,1)S(1)} collective-permute-done((bf16[32,1024]{1,0:T(8,128)(2,1)S(1)}, bf16[32,1024]{1,0:T(8,128)(2,1)S(1)}, u32[]{:S(2)}, u32[]{:S(2)}) %collective-permute-start.43) | collective-permute-done | bytes 65568 | tf_op jit(solution)/shard_map/ppermute | solution.py:25
  290.3 2.9 collective-permute-start.44
  295.5 2.1 collective-permute-start.45
  302.2 3.2 collective-permute-done.54
  305.5 1.8 collective-permute-done.60
  308.8 2.0 collective-permute-done.61
  311.2 1.9 collective-permute-done.70
  313.2 2.7 collective-permute-start.71
  317.7 2.8 collective-permute-start.72
  321.5 2.3 collective-permute-done.63
  325.0 8.7 %collective-permute-done.36 = bf16[128,1024]{1,0:T(8,128)(2,1)S(1)} collective-permute-done((bf16[128,1024]{1,0:T(8,128)(2,1)S(1)}, bf16[128,1024]{1,0:T(8,128)(2,1)S(1)}, u32[]{:S(2)}, u32[]{:S(2)}) %collective-permute-start.36) | collective-permute-done | bytes 262176 | tf_op jit(solution)/shard_map/ppermute | solution.py:25
  333.9 2.5 collective-permute-done.64
  337.7 16.3 %collective-permute-start.48 = (bf16[512,1024]{1,0:T(8,128)(2,1)S(1)}, bf16[512,1024]{1,0:T(8,128)(2,1)S(1)}, u32[]{:S(2)}, u32[]{:S(2)}) collective-permute-start(bf16[512,1024]{1,0:T(8,128)(2,1)S(1)} %pad_maximum_fusion.4), channel_id=1, source_target_pairs={{0,1},{1,0},{2,3},{3,2},{4,5},{5,4},{6,7},{7,6},{8,9},{9,8},{10,11... | collective-permute-start | bytes 3145736 | tf_op jit(solution)/shard_map/ppermute | solution.py:25
  355.6 2.1 collective-permute-start.66
  358.1 3.5 collective-permute-start.75
  362.1 2.5 maximum_convert_fusion.1
  365.2 2.4 maximum_convert_fusion.2
  368.2 2.4 maximum_convert_fusion
  371.3 2.4 maximum_convert_fusion.3
  374.3 2.4 maximum_convert_fusion.4
  (388 shorter events, 100.4 us)
Async XLA Ops:
  38.3 28.6 %collective-permute-start.11 = (bf16[512,1024]{1,0:T(8,128)(2,1)}, bf16[512,1024]{1,0:T(8,128)(2,1)S(1)}, u32[]{:S(2)}, u32[]{:S(2)}) collective-permute-start(bf16[512,1024]{1,0:T(8,128)(2,1)} %refs_9_), channel_id=1, source_target_pairs={{0,2},{1,3},{2,0},{3,1},{4,6},{5,7},{6,4},{7,5},{8,10},{9,11},{10,... | collective-permute-start | bytes 3145736 | tf_op jit(solution)/shard_map/ppermute | solution.py:25
  43.6 15.7 %collective-permute-start.5 = (bf16[4,128,128]{2,1,0:T(8,128)(2,1)S(1)}, bf16[4,128,128]{2,1,0:T(8,128)(2,1)S(1)}, u32[]{:S(2)}, u32[]{:S(2)}) collective-permute-start(bf16[4,128,128]{2,1,0:T(8,128)(2,1)S(1)} %get-tuple-element.132), channel_id=1, source_target_pairs={{0,1},{1,0},{2,3},{3,2},{4,5},{5,4},{6,7},{7,6},{8,9},{9,8},{10,11... | collective-permute-start | bytes 393224 | tf_op jit(solution)/shard_map/ppermute | solution.py:25
  59.3 20.8 %collective-permute-start.7 = (bf16[512,1024]{1,0:T(8,128)(2,1)}, bf16[512,1024]{1,0:T(8,128)(2,1)S(1)}, u32[]{:S(2)}, u32[]{:S(2)}) collective-permute-start(bf16[512,1024]{1,0:T(8,128)(2,1)} %refs_9_), channel_id=1, source_target_pairs={{0,1},{1,0},{2,3},{3,2},{4,5},{5,4},{6,7},{7,6},{8,9},{9,8},{10,11... | collective-permute-start | bytes 3145736 | tf_op jit(solution)/shard_map/ppermute | solution.py:25
  65.2 13.6 %collective-permute-start.17 = (bf16[256,1024]{1,0:T(8,128)(2,1)S(1)}, bf16[256,1024]{1,0:T(8,128)(2,1)S(1)}, u32[]{:S(2)}, u32[]{:S(2)}) collective-permute-start(bf16[256,1024]{1,0:T(8,128)(2,1)S(1)} %get-tuple-element.84.n0.refs_7_), channel_id=1, source_target_pairs={{0,2},{1,3},{2,0},{3,1},{4,6},{5,7},{6,4},{7,5},{8,10},{9,11},{10,... | collective-permute-start | bytes 1572872 | tf_op jit(solution)/shard_map/ppermute | solution.py:25
  66.6 13.4 %collective-permute-start.15 = (bf16[256,1024]{1,0:T(8,128)(2,1)S(1)}, bf16[256,1024]{1,0:T(8,128)(2,1)S(1)}, u32[]{:S(2)}, u32[]{:S(2)}) collective-permute-start(bf16[256,1024]{1,0:T(8,128)(2,1)S(1)} %get-tuple-element.84.n0.refs_7_), channel_id=1, source_target_pairs={{0,1},{1,0},{2,3},{3,2},{4,5},{5,4},{6,7},{7,6},{8,9},{9,8},{10,11... | collective-permute-start | bytes 1572872 | tf_op jit(solution)/shard_map/ppermute | solution.py:25
  66.9 32.5 %collective-permute-start.12 = (bf16[512,1024]{1,0:T(8,128)(2,1)S(1)}, bf16[512,1024]{1,0:T(8,128)(2,1)S(1)}, u32[]{:S(2)}, u32[]{:S(2)}) collective-permute-start(bf16[512,1024]{1,0:T(8,128)(2,1)S(1)} %collective-permute-done.11.c0.refs_16_.refs_23_), channel_id=1, source_target_pairs={{0,1},{1,0},{2,3},{3,2},{4,5},{5,4},{6,7},{7,6},{8,9},{9,8},{10,11... | collective-permute-start | bytes 3145736 | tf_op jit(solution)/shard_map/ppermute | solution.py:25
  72.4 17.6 %collective-permute-start.9 = (bf16[256,1024]{1,0:T(8,128)(2,1)S(1)}, bf16[256,1024]{1,0:T(8,128)(2,1)S(1)}, u32[]{:S(2)}, u32[]{:S(2)}) collective-permute-start(bf16[256,1024]{1,0:T(8,128)(2,1)S(1)} %get-tuple-element.77.n0.refs_0_), channel_id=1, source_target_pairs={{0,2},{1,3},{2,0},{3,1},{4,6},{5,7},{6,4},{7,5},{8,10},{9,11},{10,... | collective-permute-start | bytes 1572872 | tf_op jit(solution)/shard_map/ppermute | solution.py:25
  78.8 12.0 %collective-permute-start.6 = (bf16[256,1024]{1,0:T(8,128)(2,1)S(1)}, bf16[256,1024]{1,0:T(8,128)(2,1)S(1)}, u32[]{:S(2)}, u32[]{:S(2)}) collective-permute-start(bf16[256,1024]{1,0:T(8,128)(2,1)S(1)} %get-tuple-element.77.n0.refs_0_), channel_id=1, source_target_pairs={{0,1},{1,0},{2,3},{3,2},{4,5},{5,4},{6,7},{7,6},{8,9},{9,8},{10,11... | collective-permute-start | bytes 1572872 | tf_op jit(solution)/shard_map/ppermute | solution.py:25
  80.0 19.4 %collective-permute-start.18 = (bf16[256,1024]{1,0:T(8,128)(2,1)S(1)}, bf16[256,1024]{1,0:T(8,128)(2,1)S(1)}, u32[]{:S(2)}, u32[]{:S(2)}) collective-permute-start(bf16[256,1024]{1,0:T(8,128)(2,1)S(1)} %collective-permute-done.17.n0.refs_21_), channel_id=1, source_target_pairs={{0,1},{1,0},{2,3},{3,2},{4,5},{5,4},{6,7},{7,6},{8,9},{9,8},{10,11... | collective-permute-start | bytes 1572872 | tf_op jit(solution)/shard_map/ppermute | solution.py:25
  88.6 56.6 %collective-permute-start.16 = (bf16[2,256,1024]{2,1,0:T(8,128)(2,1)}, bf16[2,256,1024]{2,1,0:T(8,128)(2,1)}, u32[]{:S(2)}, u32[]{:S(2)}) collective-permute-start(bf16[2,256,1024]{2,1,0:T(8,128)(2,1)} %get-tuple-element.86), channel_id=1, source_target_pairs={{0,1},{1,0},{2,3},{3,2},{4,5},{5,4},{6,7},{7,6},{8,9},{9,8},{10,11... | collective-permute-start | bytes 3145736 | tf_op jit(solution)/shard_map/ppermute | solution.py:25
  90.1 15.3 %collective-permute-start.10 = (bf16[256,1024]{1,0:T(8,128)(2,1)S(1)}, bf16[256,1024]{1,0:T(8,128)(2,1)S(1)}, u32[]{:S(2)}, u32[]{:S(2)}) collective-permute-start(bf16[256,1024]{1,0:T(8,128)(2,1)S(1)} %collective-permute-done.9.n0.refs_14_), channel_id=1, source_target_pairs={{0,1},{1,0},{2,3},{3,2},{4,5},{5,4},{6,7},{7,6},{8,9},{9,8},{10,11... | collective-permute-start | bytes 1572872 | tf_op jit(solution)/shard_map/ppermute | solution.py:25
  99.4 53.0 %collective-permute-start.8 = (bf16[2,256,1024]{2,1,0:T(8,128)(2,1)}, bf16[2,256,1024]{2,1,0:T(8,128)(2,1)}, u32[]{:S(2)}, u32[]{:S(2)}) collective-permute-start(bf16[2,256,1024]{2,1,0:T(8,128)(2,1)} %get-tuple-element.80), channel_id=1, source_target_pairs={{0,1},{1,0},{2,3},{3,2},{4,5},{5,4},{6,7},{7,6},{8,9},{9,8},{10,11... | collective-permute-start | bytes 3145736 | tf_op jit(solution)/shard_map/ppermute | solution.py:25
  104.8 20.8 %collective-permute-start.19 = (bf16[2,256,1024]{2,1,0:T(8,128)(2,1)S(1)}, bf16[2,256,1024]{2,1,0:T(8,128)(2,1)S(1)}, u32[]{:S(2)}, u32[]{:S(2)}) collective-permute-start(bf16[2,256,1024]{2,1,0:T(8,128)(2,1)S(1)} %get-tuple-element.88), channel_id=1, source_target_pairs={{0,1},{1,0},{2,3},{3,2},{4,5},{5,4},{6,7},{7,6},{8,9},{9,8},{10,11... | collective-permute-start | bytes 3145736 | tf_op jit(solution)/shard_map/ppermute | solution.py:25
  110.5 17.6 %collective-permute-start.13 = (bf16[2,256,1024]{2,1,0:T(8,128)(2,1)S(1)}, bf16[2,256,1024]{2,1,0:T(8,128)(2,1)S(1)}, u32[]{:S(2)}, u32[]{:S(2)}) collective-permute-start(bf16[2,256,1024]{2,1,0:T(8,128)(2,1)S(1)} %get-tuple-element.82), channel_id=1, source_target_pairs={{0,1},{1,0},{2,3},{3,2},{4,5},{5,4},{6,7},{7,6},{8,9},{9,8},{10,11... | collective-permute-start | bytes 3145736 | tf_op jit(solution)/shard_map/ppermute | solution.py:25
  124.9 17.6 %collective-permute-start.79 = (bf16[4,704,128]{2,1,0:T(8,128)(2,1)}, bf16[4,704,128]{2,1,0:T(8,128)(2,1)}, u32[]{:S(2)}, u32[]{:S(2)}) collective-permute-start(bf16[4,704,128]{2,1,0:T(8,128)(2,1)} %slice.137), channel_id=1, source_target_pairs={{0,8},{1,9},{2,10},{3,11},{4,12},{5,13},{6,14},{7,15},{8,0},{9,1},... | collective-permute-start | bytes 2162696 | tf_op jit(solution)/shard_map/ppermute | solution.py:25
  126.9 20.8 %collective-permute-start.22 = (bf16[256,1024]{1,0:T(8,128)(2,1)}, bf16[256,1024]{1,0:T(8,128)(2,1)}, u32[]{:S(2)}, u32[]{:S(2)}) collective-permute-start(bf16[256,1024]{1,0:T(8,128)(2,1)} %get-tuple-element.141), channel_id=1, source_target_pairs={{0,2},{1,3},{2,0},{3,1},{4,6},{5,7},{6,4},{7,5},{8,10},{9,11},{10,... | collective-permute-start | bytes 1572872 | tf_op jit(solution)/shard_map/ppermute | solution.py:25
  129.4 23.2 %collective-permute-start.21 = (bf16[256,1024]{1,0:T(8,128)(2,1)}, bf16[256,1024]{1,0:T(8,128)(2,1)}, u32[]{:S(2)}, u32[]{:S(2)}) collective-permute-start(bf16[256,1024]{1,0:T(8,128)(2,1)} %get-tuple-element.139), channel_id=1, source_target_pairs={{0,2},{1,3},{2,0},{3,1},{4,6},{5,7},{6,4},{7,5},{8,10},{9,11},{10,... | collective-permute-start | bytes 1572872 | tf_op jit(solution)/shard_map/ppermute | solution.py:25
  142.5 38.0 %collective-permute-start.76 = (bf16[4,2,704,128]{3,2,1,0:T(8,128)(2,1)S(1)}, bf16[4,2,704,128]{3,2,1,0:T(8,128)(2,1)S(1)}, u32[]{:S(2)}, u32[]{:S(2)}) collective-permute-start(bf16[4,2,704,128]{3,2,1,0:T(8,128)(2,1)S(1)} %slice.129), channel_id=1, source_target_pairs={{0,4},{1,5},{2,6},{3,7},{4,0},{5,1},{6,2},{7,3},{8,12},{9,13},{10,... | collective-permute-start | bytes 4325384 | tf_op jit(solution)/shard_map/ppermute | solution.py:25
  145.2 18.1 %collective-permute-start.80 = (bf16[2,704,128]{2,1,0:T(8,128)(2,1)S(1)}, bf16[2,704,128]{2,1,0:T(8,128)(2,1)S(1)}, u32[]{:S(2)}, u32[]{:S(2)}) collective-permute-start(bf16[2,704,128]{2,1,0:T(8,128)(2,1)S(1)} %slice.164), channel_id=1, source_target_pairs={{0,16},{1,17},{2,18},{3,19},{4,20},{5,21},{6,22},{7,23},{8,24},{9,... | collective-permute-start | bytes 1081352 | tf_op jit(solution)/shard_map/ppermute | solution.py:25
  147.6 73.0 %collective-permute-start.20 = (bf16[256,1024]{1,0:T(8,128)(2,1)}, bf16[256,1024]{1,0:T(8,128)(2,1)}, u32[]{:S(2)}, u32[]{:S(2)}) collective-permute-start(bf16[256,1024]{1,0:T(8,128)(2,1)} %get-tuple-element.142), channel_id=1, source_target_pairs={{0,2},{1,3},{2,0},{3,1},{4,6},{5,7},{6,4},{7,5},{8,10},{9,11},{10,... | collective-permute-start | bytes 1572872 | tf_op jit(solution)/shard_map/ppermute | solution.py:25
  152.4 70.0 %collective-permute-start.14 = (bf16[256,1024]{1,0:T(8,128)(2,1)}, bf16[256,1024]{1,0:T(8,128)(2,1)}, u32[]{:S(2)}, u32[]{:S(2)}) collective-permute-start(bf16[256,1024]{1,0:T(8,128)(2,1)} %get-tuple-element.140), channel_id=1, source_target_pairs={{0,2},{1,3},{2,0},{3,1},{4,6},{5,7},{6,4},{7,5},{8,10},{9,11},{10,... | collective-permute-start | bytes 1572872 | tf_op jit(solution)/shard_map/ppermute | solution.py:25
  156.4 7.3 %collective-permute-start.23 = (bf16[4,128,128]{2,1,0:T(8,128)(2,1)S(1)}, bf16[4,128,128]{2,1,0:T(8,128)(2,1)S(1)}, u32[]{:S(2)}, u32[]{:S(2)}) collective-permute-start(bf16[4,128,128]{2,1,0:T(8,128)(2,1)S(1)} %fusion.64), channel_id=1, source_target_pairs={{0,1},{1,0},{2,3},{3,2},{4,5},{5,4},{6,7},{7,6},{8,9},{9,8},{10,11... | collective-permute-start | bytes 393224 | tf_op jit(solution)/shard_map/ppermute | solution.py:25
  163.4 14.7 %collective-permute-start.81 = (bf16[1,704,128]{2,1,0:T(8,128)(2,1)S(1)}, bf16[1,704,128]{2,1,0:T(8,128)(2,1)S(1)}, u32[]{:S(2)}, u32[]{:S(2)}) collective-permute-start(bf16[1,704,128]{2,1,0:T(8,128)(2,1)S(1)} %slice.166), channel_id=1, source_target_pairs={{0,4},{1,5},{2,6},{3,7},{4,0},{5,1},{6,2},{7,3},{8,12},{9,13},{10,... | collective-permute-start | bytes 540680 | tf_op jit(solution)/shard_map/ppermute | solution.py:25
  163.8 15.1 %collective-permute-start.24 = (bf16[4,128,128]{2,1,0:T(8,128)(2,1)S(1)}, bf16[4,128,128]{2,1,0:T(8,128)(2,1)S(1)}, u32[]{:S(2)}, u32[]{:S(2)}) collective-permute-start(bf16[4,128,128]{2,1,0:T(8,128)(2,1)S(1)} %fusion.73), channel_id=1, source_target_pairs={{0,2},{1,3},{2,0},{3,1},{4,6},{5,7},{6,4},{7,5},{8,10},{9,11},{10,... | collective-permute-start | bytes 393224 | tf_op jit(solution)/shard_map/ppermute | solution.py:25
  181.8 43.4 %collective-permute-start.77 = (bf16[2,2,704,128]{3,2,1,0:T(8,128)(2,1)}, bf16[2,2,704,128]{3,2,1,0:T(8,128)(2,1)}, u32[]{:S(2)}, u32[]{:S(2)}) collective-permute-start(bf16[2,2,704,128]{3,2,1,0:T(8,128)(2,1)} %slice.158), channel_id=1, source_target_pairs={{0,8},{1,9},{2,10},{3,11},{4,12},{5,13},{6,14},{7,15},{8,0},{9,1},... | collective-permute-start | bytes 2162696 | tf_op jit(solution)/shard_map/ppermute | solution.py:25
  183.1 16.9 %collective-permute-start.26 = (bf16[4,128,128]{2,1,0:T(8,128)(2,1)S(1)}, bf16[4,128,128]{2,1,0:T(8,128)(2,1)S(1)}, u32[]{:S(2)}, u32[]{:S(2)}) collective-permute-start(bf16[4,128,128]{2,1,0:T(8,128)(2,1)S(1)} %fusion.61), channel_id=1, source_target_pairs={{0,8},{1,9},{2,10},{3,11},{4,12},{5,13},{6,14},{7,15},{8,0},{9,1},... | collective-permute-start | bytes 393224 | tf_op jit(solution)/shard_map/ppermute | solution.py:25
  200.2 7.0 %collective-permute-start.27 = (bf16[4,128,128]{2,1,0:T(8,128)(2,1)S(1)}, bf16[4,128,128]{2,1,0:T(8,128)(2,1)S(1)}, u32[]{:S(2)}, u32[]{:S(2)}) collective-permute-start(bf16[4,128,128]{2,1,0:T(8,128)(2,1)S(1)} %fusion.50), channel_id=1, source_target_pairs={{0,16},{1,17},{2,18},{3,19},{4,20},{5,21},{6,22},{7,23},{8,24},{9,... | collective-permute-start | bytes 393224 | tf_op jit(solution)/shard_map/ppermute | solution.py:25
  212.1 37.3 %collective-permute-start.29 = (bf16[3,512,1024]{2,1,0:T(8,128)(2,1)S(1)}, bf16[3,512,1024]{2,1,0:T(8,128)(2,1)S(1)}, u32[]{:S(2)}, u32[]{:S(2)}) collective-permute-start(bf16[3,512,1024]{2,1,0:T(8,128)(2,1)S(1)} %slice_bitcast_fusion), channel_id=1, source_target_pairs={{0,1},{1,0},{2,3},{3,2},{4,5},{5,4},{6,7},{7,6},{8,9},{9,8},{10,11... | collective-permute-start | bytes 9437192 | tf_op jit(solution)/shard_map/ppermute | solution.py:25
  220.6 25.9 %collective-permute-start.39 = (bf16[2,512,1024]{2,1,0:T(8,128)(2,1)}, bf16[2,512,1024]{2,1,0:T(8,128)(2,1)S(1)}, u32[]{:S(2)}, u32[]{:S(2)}) collective-permute-start(bf16[2,512,1024]{2,1,0:T(8,128)(2,1)} %slice_bitcast_fusion.2), channel_id=1, source_target_pairs={{0,1},{1,0},{2,3},{3,2},{4,5},{5,4},{6,7},{7,6},{8,9},{9,8},{10,11... | collective-permute-start | bytes 6291464 | tf_op jit(solution)/shard_map/ppermute | solution.py:25
  226.8 18.8 %collective-permute-start.78 = (bf16[1,2,704,128]{3,2,1,0:T(8,128)(2,1)S(1)}, bf16[1,2,704,128]{3,2,1,0:T(8,128)(2,1)S(1)}, u32[]{:S(2)}, u32[]{:S(2)}) collective-permute-start(bf16[1,2,704,128]{3,2,1,0:T(8,128)(2,1)S(1)} %slice.160), channel_id=1, source_target_pairs={{0,16},{1,17},{2,18},{3,19},{4,20},{5,21},{6,22},{7,23},{8,24},{9,... | collective-permute-start | bytes 1081352 | tf_op jit(solution)/shard_map/ppermute | solution.py:25
  247.8 12.8 %collective-permute-start.40 = (bf16[256,1024]{1,0:T(8,128)(2,1)S(1)}, bf16[256,1024]{1,0:T(8,128)(2,1)S(1)}, u32[]{:S(2)}, u32[]{:S(2)}) collective-permute-start(bf16[256,1024]{1,0:T(8,128)(2,1)S(1)} %dynamic-slice_bitcast_fusion.3), channel_id=1, source_target_pairs={{0,2},{1,3},{2,0},{3,1},{4,6},{5,7},{6,4},{7,5},{8,10},{9,11},{10,... | collective-permute-start | bytes 1572872 | tf_op jit(solution)/shard_map/ppermute | solution.py:25
  249.1 12.4 %collective-permute-start.49 = (bf16[256,1024]{1,0:T(8,128)(2,1)S(1)}, bf16[256,1024]{1,0:T(8,128)(2,1)S(1)}, u32[]{:S(2)}, u32[]{:S(2)}) collective-permute-start(bf16[256,1024]{1,0:T(8,128)(2,1)S(1)} %dynamic-slice_bitcast_fusion.2), channel_id=1, source_target_pairs={{0,4},{1,5},{2,6},{3,7},{4,0},{5,1},{6,2},{7,3},{8,12},{9,13},{10,... | collective-permute-start | bytes 1572872 | tf_op jit(solution)/shard_map/ppermute | solution.py:25
  251.4 12.2 %collective-permute-start.30 = (bf16[256,1024]{1,0:T(8,128)(2,1)S(1)}, bf16[256,1024]{1,0:T(8,128)(2,1)S(1)}, u32[]{:S(2)}, u32[]{:S(2)}) collective-permute-start(bf16[256,1024]{1,0:T(8,128)(2,1)S(1)} %dynamic-slice_bitcast_fusion.4), channel_id=1, source_target_pairs={{0,8},{1,9},{2,10},{3,11},{4,12},{5,13},{6,14},{7,15},{8,0},{9,1},... | collective-permute-start | bytes 1572872 | tf_op jit(solution)/shard_map/ppermute | solution.py:25
  251.5 30.3 %collective-permute-start.58 = (bf16[256,1024]{1,0:T(8,128)(2,1)S(1)}, bf16[256,1024]{1,0:T(8,128)(2,1)S(1)}, u32[]{:S(2)}, u32[]{:S(2)}) collective-permute-start(bf16[256,1024]{1,0:T(8,128)(2,1)S(1)} %dynamic-slice_bitcast_fusion.1), channel_id=1, source_target_pairs={{0,4},{1,5},{2,6},{3,7},{4,0},{5,1},{6,2},{7,3},{8,12},{9,13},{10,... | collective-permute-start | bytes 1572872 | tf_op jit(solution)/shard_map/ppermute | solution.py:25
  252.9 29.3 %collective-permute-start.67 = (bf16[256,1024]{1,0:T(8,128)(2,1)S(1)}, bf16[256,1024]{1,0:T(8,128)(2,1)S(1)}, u32[]{:S(2)}, u32[]{:S(2)}) collective-permute-start(bf16[256,1024]{1,0:T(8,128)(2,1)S(1)} %dynamic-slice_bitcast_fusion), channel_id=1, source_target_pairs={{0,2},{1,3},{2,0},{3,1},{4,6},{5,7},{6,4},{7,5},{8,10},{9,11},{10,... | collective-permute-start | bytes 1572872 | tf_op jit(solution)/shard_map/ppermute | solution.py:25
  260.8 17.6 %collective-permute-start.41 = (bf16[128,1024]{1,0:T(8,128)(2,1)S(1)}, bf16[128,1024]{1,0:T(8,128)(2,1)S(1)}, u32[]{:S(2)}, u32[]{:S(2)}) collective-permute-start(bf16[128,1024]{1,0:T(8,128)(2,1)S(1)} %dynamic-slice_bitcast_fusion.8), channel_id=1, source_target_pairs={{0,4},{1,5},{2,6},{3,7},{4,0},{5,1},{6,2},{7,3},{8,12},{9,13},{10,... | collective-permute-start | bytes 786440 | tf_op jit(solution)/shard_map/ppermute | solution.py:25
  261.8 16.8 %collective-permute-start.50 = (bf16[128,1024]{1,0:T(8,128)(2,1)S(1)}, bf16[128,1024]{1,0:T(8,128)(2,1)S(1)}, u32[]{:S(2)}, u32[]{:S(2)}) collective-permute-start(bf16[128,1024]{1,0:T(8,128)(2,1)S(1)} %dynamic-slice_bitcast_fusion.7), channel_id=1, source_target_pairs={{0,8},{1,9},{2,10},{3,11},{4,12},{5,13},{6,14},{7,15},{8,0},{9,1},... | collective-permute-start | bytes 786440 | tf_op jit(solution)/shard_map/ppermute | solution.py:25
  263.8 29.7 %collective-permute-start.31 = (bf16[128,1024]{1,0:T(8,128)(2,1)S(1)}, bf16[128,1024]{1,0:T(8,128)(2,1)S(1)}, u32[]{:S(2)}, u32[]{:S(2)}) collective-permute-start(bf16[128,1024]{1,0:T(8,128)(2,1)S(1)} %dynamic-slice_bitcast_fusion.9), channel_id=1, source_target_pairs={{0,16},{1,17},{2,18},{3,19},{4,20},{5,21},{6,22},{7,23},{8,24},{9,... | collective-permute-start | bytes 786440 | tf_op jit(solution)/shard_map/ppermute | solution.py:25
  282.1 16.6 %collective-permute-start.59 = (bf16[128,1024]{1,0:T(8,128)(2,1)S(1)}, bf16[128,1024]{1,0:T(8,128)(2,1)S(1)}, u32[]{:S(2)}, u32[]{:S(2)}) collective-permute-start(bf16[128,1024]{1,0:T(8,128)(2,1)S(1)} %dynamic-slice_bitcast_fusion.6), channel_id=1, source_target_pairs={{0,8},{1,9},{2,10},{3,11},{4,12},{5,13},{6,14},{7,15},{8,0},{9,1},... | collective-permute-start | bytes 786440 | tf_op jit(solution)/shard_map/ppermute | solution.py:25
  282.5 17.8 %collective-permute-start.68 = (bf16[128,1024]{1,0:T(8,128)(2,1)S(1)}, bf16[128,1024]{1,0:T(8,128)(2,1)S(1)}, u32[]{:S(2)}, u32[]{:S(2)}) collective-permute-start(bf16[128,1024]{1,0:T(8,128)(2,1)S(1)} %dynamic-slice_bitcast_fusion.5), channel_id=1, source_target_pairs={{0,4},{1,5},{2,6},{3,7},{4,0},{5,1},{6,2},{7,3},{8,12},{9,13},{10,... | collective-permute-start | bytes 786440 | tf_op jit(solution)/shard_map/ppermute | solution.py:25
  282.8 7.4 %collective-permute-start.43 = (bf16[32,1024]{1,0:T(8,128)(2,1)S(1)}, bf16[32,1024]{1,0:T(8,128)(2,1)S(1)}, u32[]{:S(2)}, u32[]{:S(2)}) collective-permute-start(bf16[32,1024]{1,0:T(8,128)(2,1)S(1)} %dynamic-slice_bitcast_fusion.18), channel_id=1, source_target_pairs={{0,16},{1,17},{2,18},{3,19},{4,20},{5,21},{6,22},{7,23},{8,24},{9,... | collective-permute-start | bytes 196616 | tf_op jit(solution)/shard_map/ppermute | solution.py:25
  285.6 7.5 %collective-permute-start.52 = (bf16[32,1024]{1,0:T(8,128)(2,1)S(1)}, bf16[32,1024]{1,0:T(8,128)(2,1)S(1)}, u32[]{:S(2)}, u32[]{:S(2)}) collective-permute-start(bf16[32,1024]{1,0:T(8,128)(2,1)S(1)} %dynamic-slice_bitcast_fusion.17), channel_id=1, source_target_pairs={{0,2},{1,3},{2,0},{3,1},{4,6},{5,7},{6,4},{7,5},{8,10},{9,11},{10,... | collective-permute-start | bytes 196616 | tf_op jit(solution)/shard_map/ppermute | solution.py:25
  297.7 7.7 %collective-permute-start.54 = (bf16[64,1024]{1,0:T(8,128)(2,1)S(1)}, bf16[64,1024]{1,0:T(8,128)(2,1)S(1)}, u32[]{:S(2)}, u32[]{:S(2)}) collective-permute-start(bf16[64,1024]{1,0:T(8,128)(2,1)S(1)} %pad_maximum_fusion.24), channel_id=1, source_target_pairs={{0,16},{1,17},{2,18},{3,19},{4,20},{5,21},{6,22},{7,23},{8,24},{9,... | collective-permute-start | bytes 393224 | tf_op jit(solution)/shard_map/ppermute | solution.py:25
  298.9 8.5 %collective-permute-start.60 = (bf16[64,1024]{1,0:T(8,128)(2,1)S(1)}, bf16[64,1024]{1,0:T(8,128)(2,1)S(1)}, u32[]{:S(2)}, u32[]{:S(2)}) collective-permute-start(bf16[64,1024]{1,0:T(8,128)(2,1)S(1)} %dynamic-slice_bitcast_fusion.11), channel_id=1, source_target_pairs={{0,16},{1,17},{2,18},{3,19},{4,20},{5,21},{6,22},{7,23},{8,24},{9,... | collective-permute-start | bytes 393224 | tf_op jit(solution)/shard_map/ppermute | solution.py:25
  300.4 8.0 %collective-permute-start.69 = (bf16[64,1024]{1,0:T(8,128)(2,1)S(1)}, bf16[64,1024]{1,0:T(8,128)(2,1)S(1)}, u32[]{:S(2)}, u32[]{:S(2)}) collective-permute-start(bf16[64,1024]{1,0:T(8,128)(2,1)S(1)} %dynamic-slice_bitcast_fusion.10), channel_id=1, source_target_pairs={{0,8},{1,9},{2,10},{3,11},{4,12},{5,13},{6,14},{7,15},{8,0},{9,1},... | collective-permute-start | bytes 393224 | tf_op jit(solution)/shard_map/ppermute | solution.py:25
  300.5 8.0 %collective-permute-start.33 = (bf16[32,1024]{1,0:T(8,128)(2,1)S(1)}, bf16[32,1024]{1,0:T(8,128)(2,1)S(1)}, u32[]{:S(2)}, u32[]{:S(2)}) collective-permute-start(bf16[32,1024]{1,0:T(8,128)(2,1)S(1)} %dynamic-slice_bitcast_fusion.19), channel_id=1, source_target_pairs={{0,4},{1,5},{2,6},{3,7},{4,0},{5,1},{6,2},{7,3},{8,12},{9,13},{10,... | collective-permute-start | bytes 196616 | tf_op jit(solution)/shard_map/ppermute | solution.py:25
  300.9 20.1 %collective-permute-start.46 = (bf16[128,1024]{1,0:T(8,128)(2,1)S(1)}, bf16[128,1024]{1,0:T(8,128)(2,1)S(1)}, u32[]{:S(2)}, u32[]{:S(2)}) collective-permute-start(bf16[128,1024]{1,0:T(8,128)(2,1)S(1)} %pad_maximum_fusion.18), channel_id=1, source_target_pairs={{0,4},{1,5},{2,6},{3,7},{4,0},{5,1},{6,2},{7,3},{8,12},{9,13},{10,... | collective-permute-start | bytes 786440 | tf_op jit(solution)/shard_map/ppermute | solution.py:25
  305.4 15.8 %collective-permute-start.55 = (bf16[128,1024]{1,0:T(8,128)(2,1)S(1)}, bf16[128,1024]{1,0:T(8,128)(2,1)S(1)}, u32[]{:S(2)}, u32[]{:S(2)}) collective-permute-start(bf16[128,1024]{1,0:T(8,128)(2,1)S(1)} %pad_maximum_fusion.19), channel_id=1, source_target_pairs={{0,8},{1,9},{2,10},{3,11},{4,12},{5,13},{6,14},{7,15},{8,0},{9,1},... | collective-permute-start | bytes 786440 | tf_op jit(solution)/shard_map/ppermute | solution.py:25
  308.6 7.3 %collective-permute-start.34 = (bf16[32,1024]{1,0:T(8,128)(2,1)S(1)}, bf16[32,1024]{1,0:T(8,128)(2,1)S(1)}, u32[]{:S(2)}, u32[]{:S(2)}) collective-permute-start(bf16[32,1024]{1,0:T(8,128)(2,1)S(1)} %fusion.69), channel_id=1, source_target_pairs={{0,4},{1,5},{2,6},{3,7},{4,0},{5,1},{6,2},{7,3},{8,12},{9,13},{10,... | collective-permute-start | bytes 196616 | tf_op jit(solution)/shard_map/ppermute | solution.py:25
  316.3 7.5 %collective-permute-start.63 = (bf16[64,1024]{1,0:T(8,128)(2,1)S(1)}, bf16[64,1024]{1,0:T(8,128)(2,1)S(1)}, u32[]{:S(2)}, u32[]{:S(2)}) collective-permute-start(bf16[64,1024]{1,0:T(8,128)(2,1)S(1)} %pad_maximum_fusion.25), channel_id=1, source_target_pairs={{0,16},{1,17},{2,18},{3,19},{4,20},{5,21},{6,22},{7,23},{8,24},{9,... | collective-permute-start | bytes 393224 | tf_op jit(solution)/shard_map/ppermute | solution.py:25
  317.7 7.1 %collective-permute-start.72 = (bf16[64,1024]{1,0:T(8,128)(2,1)S(1)}, bf16[64,1024]{1,0:T(8,128)(2,1)S(1)}, u32[]{:S(2)}, u32[]{:S(2)}) collective-permute-start(bf16[64,1024]{1,0:T(8,128)(2,1)S(1)} %pad_maximum_fusion.26), channel_id=1, source_target_pairs={{0,8},{1,9},{2,10},{3,11},{4,12},{5,13},{6,14},{7,15},{8,0},{9,1},... | collective-permute-start | bytes 393224 | tf_op jit(solution)/shard_map/ppermute | solution.py:25
  320.6 13.1 %collective-permute-start.36 = (bf16[128,1024]{1,0:T(8,128)(2,1)S(1)}, bf16[128,1024]{1,0:T(8,128)(2,1)S(1)}, u32[]{:S(2)}, u32[]{:S(2)}) collective-permute-start(bf16[128,1024]{1,0:T(8,128)(2,1)S(1)} %pad_maximum_fusion.17), channel_id=1, source_target_pairs={{0,16},{1,17},{2,18},{3,19},{4,20},{5,21},{6,22},{7,23},{8,24},{9,... | collective-permute-start | bytes 786440 | tf_op jit(solution)/shard_map/ppermute | solution.py:25
  321.2 16.2 %collective-permute-start.47 = (bf16[256,1024]{1,0:T(8,128)(2,1)S(1)}, bf16[256,1024]{1,0:T(8,128)(2,1)S(1)}, u32[]{:S(2)}, u32[]{:S(2)}) collective-permute-start(bf16[256,1024]{1,0:T(8,128)(2,1)S(1)} %pad_maximum_fusion.11), channel_id=1, source_target_pairs={{0,2},{1,3},{2,0},{3,1},{4,6},{5,7},{6,4},{7,5},{8,10},{9,11},{10,... | collective-permute-start | bytes 1572872 | tf_op jit(solution)/shard_map/ppermute | solution.py:25
  321.4 32.6 %collective-permute-start.56 = (bf16[256,1024]{1,0:T(8,128)(2,1)S(1)}, bf16[256,1024]{1,0:T(8,128)(2,1)S(1)}, u32[]{:S(2)}, u32[]{:S(2)}) collective-permute-start(bf16[256,1024]{1,0:T(8,128)(2,1)S(1)} %pad_maximum_fusion.12), channel_id=1, source_target_pairs={{0,4},{1,5},{2,6},{3,7},{4,0},{5,1},{6,2},{7,3},{8,12},{9,13},{10,... | collective-permute-start | bytes 1572872 | tf_op jit(solution)/shard_map/ppermute | solution.py:25
  323.8 12.6 %collective-permute-start.64 = (bf16[128,1024]{1,0:T(8,128)(2,1)S(1)}, bf16[128,1024]{1,0:T(8,128)(2,1)S(1)}, u32[]{:S(2)}, u32[]{:S(2)}) collective-permute-start(bf16[128,1024]{1,0:T(8,128)(2,1)S(1)} %pad_maximum_fusion.20), channel_id=1, source_target_pairs={{0,8},{1,9},{2,10},{3,11},{4,12},{5,13},{6,14},{7,15},{8,0},{9,1},... | collective-permute-start | bytes 786440 | tf_op jit(solution)/shard_map/ppermute | solution.py:25
  324.9 11.8 %collective-permute-start.73 = (bf16[128,1024]{1,0:T(8,128)(2,1)S(1)}, bf16[128,1024]{1,0:T(8,128)(2,1)S(1)}, u32[]{:S(2)}, u32[]{:S(2)}) collective-permute-start(bf16[128,1024]{1,0:T(8,128)(2,1)S(1)} %pad_maximum_fusion.21), channel_id=1, source_target_pairs={{0,4},{1,5},{2,6},{3,7},{4,0},{5,1},{6,2},{7,3},{8,12},{9,13},{10,... | collective-permute-start | bytes 786440 | tf_op jit(solution)/shard_map/ppermute | solution.py:25
  333.8 20.5 %collective-permute-start.37 = (bf16[256,1024]{1,0:T(8,128)(2,1)S(1)}, bf16[256,1024]{1,0:T(8,128)(2,1)S(1)}, u32[]{:S(2)}, u32[]{:S(2)}) collective-permute-start(bf16[256,1024]{1,0:T(8,128)(2,1)S(1)} %pad_maximum_fusion.10), channel_id=1, source_target_pairs={{0,8},{1,9},{2,10},{3,11},{4,12},{5,13},{6,14},{7,15},{8,0},{9,1},... | collective-permute-start | bytes 1572872 | tf_op jit(solution)/shard_map/ppermute | solution.py:25
  336.6 18.7 %collective-permute-start.65 = (bf16[256,1024]{1,0:T(8,128)(2,1)S(1)}, bf16[256,1024]{1,0:T(8,128)(2,1)S(1)}, u32[]{:S(2)}, u32[]{:S(2)}) collective-permute-start(bf16[256,1024]{1,0:T(8,128)(2,1)S(1)} %pad_maximum_fusion.13), channel_id=1, source_target_pairs={{0,4},{1,5},{2,6},{3,7},{4,0},{5,1},{6,2},{7,3},{8,12},{9,13},{10,... | collective-permute-start | bytes 1572872 | tf_op jit(solution)/shard_map/ppermute | solution.py:25
  336.9 20.9 %collective-permute-start.74 = (bf16[256,1024]{1,0:T(8,128)(2,1)S(1)}, bf16[256,1024]{1,0:T(8,128)(2,1)S(1)}, u32[]{:S(2)}, u32[]{:S(2)}) collective-permute-start(bf16[256,1024]{1,0:T(8,128)(2,1)S(1)} %pad_maximum_fusion.14), channel_id=1, source_target_pairs={{0,2},{1,3},{2,0},{3,1},{4,6},{5,7},{6,4},{7,5},{8,10},{9,11},{10,... | collective-permute-start | bytes 1572872 | tf_op jit(solution)/shard_map/ppermute | solution.py:25
  337.7 23.9 %collective-permute-start.48 = (bf16[512,1024]{1,0:T(8,128)(2,1)S(1)}, bf16[512,1024]{1,0:T(8,128)(2,1)S(1)}, u32[]{:S(2)}, u32[]{:S(2)}) collective-permute-start(bf16[512,1024]{1,0:T(8,128)(2,1)S(1)} %pad_maximum_fusion.4), channel_id=1, source_target_pairs={{0,1},{1,0},{2,3},{3,2},{4,5},{5,4},{6,7},{7,6},{8,9},{9,8},{10,11... | collective-permute-start | bytes 3145736 | tf_op jit(solution)/shard_map/ppermute | solution.py:25
  354.3 10.3 %collective-permute-start.57 = (bf16[512,1024]{1,0:T(8,128)(2,1)S(1)}, bf16[512,1024]{1,0:T(8,128)(2,1)S(1)}, u32[]{:S(2)}, u32[]{:S(2)}) collective-permute-start(bf16[512,1024]{1,0:T(8,128)(2,1)S(1)} %pad_maximum_fusion.5), channel_id=1, source_target_pairs={{0,1},{1,0},{2,3},{3,2},{4,5},{5,4},{6,7},{7,6},{8,9},{9,8},{10,11... | collective-permute-start | bytes 3145736 | tf_op jit(solution)/shard_map/ppermute | solution.py:25
  354.7 12.9 %collective-permute-start.38 = (bf16[512,1024]{1,0:T(8,128)(2,1)S(1)}, bf16[512,1024]{1,0:T(8,128)(2,1)S(1)}, u32[]{:S(2)}, u32[]{:S(2)}) collective-permute-start(bf16[512,1024]{1,0:T(8,128)(2,1)S(1)} %pad_maximum_fusion.3), channel_id=1, source_target_pairs={{0,1},{1,0},{2,3},{3,2},{4,5},{5,4},{6,7},{7,6},{8,9},{9,8},{10,11... | collective-permute-start | bytes 3145736 | tf_op jit(solution)/shard_map/ppermute | solution.py:25
  355.6 15.1 %collective-permute-start.66 = (bf16[512,1024]{1,0:T(8,128)(2,1)S(1)}, bf16[512,1024]{1,0:T(8,128)(2,1)S(1)}, u32[]{:S(2)}, u32[]{:S(2)}) collective-permute-start(bf16[512,1024]{1,0:T(8,128)(2,1)S(1)} %pad_maximum_fusion.6), channel_id=1, source_target_pairs={{0,1},{1,0},{2,3},{3,2},{4,5},{5,4},{6,7},{7,6},{8,9},{9,8},{10,11... | collective-permute-start | bytes 3145736 | tf_op jit(solution)/shard_map/ppermute | solution.py:25
  358.1 15.7 %collective-permute-start.75 = (bf16[512,1024]{1,0:T(8,128)(2,1)S(1)}, bf16[512,1024]{1,0:T(8,128)(2,1)S(1)}, u32[]{:S(2)}, u32[]{:S(2)}) collective-permute-start(bf16[512,1024]{1,0:T(8,128)(2,1)S(1)} %pad_maximum_fusion.7), channel_id=1, source_target_pairs={{0,1},{1,0},{2,3},{3,2},{4,5},{5,4},{6,7},{7,6},{8,9},{9,8},{10,11... | collective-permute-start | bytes 3145736 | tf_op jit(solution)/shard_map/ppermute | solution.py:25
  (83 other events, 512.8 us)

commit v5 on v4

--- a/solution.py
+++ b/solution.py
@@ -616,8 +616,9 @@
 
 def grads_body(lefts, pairs, core, *refs):
     left = refs[:lefts]
-    right = refs[lefts:-1]
-    out = refs[-1]
+    right = refs[lefts:-2]
+    keep, ship = refs[-2:]
+    step = pl.program_id(0)
     for k, (l, rs) in enumerate(pairs):
         acc = None
         start = 0
@@ -627,7 +628,14 @@
             term = dot_tn(left[l][start : start + rows], r[...])
             start += rows
             acc = term if acc is None else acc + term
-        out[0, k] = acc.astype(BHALF)
+
+        @pl.when(step == 0)
+        def _(acc=acc, k=k):
+            keep[k] = acc.astype(BHALF)
+
+        @pl.when(step == 1)
+        def _(acc=acc, k=k):
+            ship[k] = acc.astype(BHALF)
 
 
 def grads(core, lefts, rights, pairs):
@@ -639,14 +647,14 @@
         grid=(2,),
         in_specs=[pl.BlockSpec((tokens, half), lambda i, c: (0, i ^ c[0]))] * len(lefts)
         + [pl.BlockSpec(r.shape, lambda i, c: (0, 0)) for r in rights],
-        out_specs=pl.BlockSpec((1, len(pairs), half, cols), lambda i, c: (i, 0, 0, 0)),
+        out_specs=[pl.BlockSpec((len(pairs), half, cols), lambda i, c: (0, 0, 0))] * 2,
     )
     n = len(pairs)
     body = functools.partial(grads_body, len(lefts), pairs)
     return pl.pallas_call(
         body,
         grid_spec=spec,
-        out_shape=shape_of((2, n, half, cols), BHALF),
+        out_shape=[shape_of((n, half, cols), BHALF)] * 2,
         cost_estimate=pl.CostEstimate(
             flops=2 * n * tokens * width * cols, bytes_accessed=4 * n * width * cols, transcendentals=0
         ),

time: 384 us -> 394 us (1.026)
  waiting for transfers between devices: 121 us -> 125 us
    unnamed x130 -> x136, local copies, waits for them, and re-layouts: 25.6 us -> 31.3 us
  transfers between devices with their start and end apart: 82 -> 82, of which waited for: 30 -> 31; matrix products, arithmetic and copies ran while one was open for 12% -> 10% of each run, Pallas kernels for 20% -> 20%
where the time goes in v5:
time: 394 us; the launch traced here: 387 us
  waiting for transfers between devices  125 us (32%)
  starting transfers between devices  94.5 us (24%)
  Pallas kernels  82.1 us (21%)
  other arithmetic  45.8 us (12%)
  local copies, waits for them, and re-layouts  36.9 us (9%)
    ppermute x82, waiting for transfers between devices, swap(): return lax.ppermute(value, axes, [(s, s ^ mask) for s in range(count)])  125 us
    ppermute x82, starting transfers between devices, swap(): return lax.ppermute(value, axes, [(s, s ^ mask) for s in range(count)])  94.5 us
    unnamed x136, local copies, waits for them, and re-layouts  31.3 us
    pallas_call x4, Pallas kernels, unit(): call(unit_body, (1,), [piece] * 2 + [cot] * 2 + [whole(down.shape)] * 3,...  24.9 us
    pallas_call x1, Pallas kernels, unit_grads(): call(functools.partial(unit_grads_body, n, orders), (1,), [SMEM_SPEC] + [...  13.3 us
    convert_element_type x5, other arithmetic, rest_of(): return double(piece, [1], place).astype(FLOAT)  12.2 us
    pallas_call x2, Pallas kernels, grads(): pl.pallas_call(body, grid_spec=spec, out_shape=[shape_of((n, half, cols),...  9.06 us
  transfers between devices with their start and end apart: 82, of which 31 were waited for; matrix products, arithmetic and copies ran while one was open for 10% of the time, Pallas kernels for 20%

profile of v5, /device:TPU:1, one launch (start us, length us, event | category | flops | bytes accessed | tf_op | source)
XLA Modules:
  0.0 387.1 jit_solution(1502466599306747015)
XLA Ops:
  6.6 3.6 shard_map.186
  18.9 2.7 collective-permute-start.1
  21.6 3.7 collective-permute-done.1
  25.3 1.8 fusion.80
  28.4 3.2 collective-permute-done.2
  33.6 3.0 collective-permute-done.3
  36.5 1.7 fusion.35
  38.2 2.2 collective-permute-start.4
  41.6 2.9 collective-permute-done.4
  45.8 3.9 %collective-permute-start.5 = (bf16[4,128,128]{2,1,0:T(8,128)(2,1)S(1)}, bf16[4,128,128]{2,1,0:T(8,128)(2,1)S(1)}, u32[]{:S(2)}, u32[]{:S(2)}) collective-permute-start(bf16[4,128,128]{2,1,0:T(8,128)(2,1)S(1)} %get-tuple-element.140), channel_id=1, source_target_pairs={{0,1},{1,0},{2,3},{3,2},{4,5},{5,4},{6,7},{7,6},{8,9},{9,8},{10,11... | collective-permute-start | bytes 393224 | tf_op jit(solution)/shard_map/ppermute | solution.py:25
  55.9 5.4 %shard_map.187 = (f32[512,1024]{1,0:T(8,128)S(1)}, bf16[512,1024]{1,0:T(8,128)(2,1)S(1)}, f32[512,1024]{1,0:T(8,128)S(1)}, f32[512,1024]{1,0:T(8,128)S(1)}) custom-call(f32[8]{0:T(128)S(1)} %get-tuple-element.224.rate, bf16[512,1024]{1,0:T(8,128)(2,1)S(1)} %copy-done.59, bf16[1024,1024]{1,0:T(8,128)(2,1)S(1)} %copy-done.10, ...), custom_call_target="tpu_custom_call" | custom-call | flops 2147483648 | bytes 14680064 | tf_op jit(solution)/shard_map/pallas_call | solution.py:292
  62.9 2.1 copy-done
  65.0 1.8 shard_map.191
  72.2 1.8 shard_map.188
  77.6 6.2 %collective-permute-done.17.n0.refs_21_ = bf16[256,1024]{1,0:T(8,128)(2,1)S(1)} collective-permute-done((bf16[256,1024]{1,0:T(8,128)(2,1)S(1)}, bf16[256,1024]{1,0:T(8,128)(2,1)S(1)}, u32[]{:S(2)}, u32[]{:S(2)}) %collective-permute-start.17) | collective-permute-done | bytes 524320 | tf_op jit(solution)/shard_map/ppermute | solution.py:25
  85.1 7.2 %shard_map.192 = (f32[2,256,1024]{2,1,0:T(8,128)S(1)}, bf16[2,256,1024]{2,1,0:T(8,128)(2,1)}, bf16[512,704]{1,0:T(8,128)(2,1)S(1)}, bf16[512,704]{1,0:T(8,128)(2,1)S(1)}, bf16[512,704]{1,0:T(8,128)(2,1)S(1)}) custom-call(bf16[256,1024]{1,0:T(8,128)(2,1)S(1)} %get-tuple-element.88.n0.refs_7_, bf16[256,1024]{1,0:T(8,128)(2,1)S(1)} %collective-permute-done.15.n1.refs_8_, ...), custom_call_target="tpu_custom_call" | custom-call | flops 4429185024 | bytes 9568256 | tf_op jit(solution)/shard_map/pallas_call | solution.py:380
  95.9 7.2 %shard_map.189 = (f32[2,256,1024]{2,1,0:T(8,128)S(1)}, bf16[2,256,1024]{2,1,0:T(8,128)(2,1)}, bf16[512,704]{1,0:T(8,128)(2,1)S(1)}, bf16[512,704]{1,0:T(8,128)(2,1)S(1)}, bf16[512,704]{1,0:T(8,128)(2,1)S(1)}) custom-call(bf16[256,1024]{1,0:T(8,128)(2,1)S(1)} %get-tuple-element.81.n0.refs_0_, bf16[256,1024]{1,0:T(8,128)(2,1)S(1)} %collective-permute-done.6.n1.refs_1_, ...), custom_call_target="tpu_custom_call" | custom-call | flops 4429185024 | bytes 9568256 | tf_op jit(solution)/shard_map/pallas_call | solution.py:380
  104.4 5.4 %shard_map.193 = (f32[2,256,1024]{2,1,0:T(8,128)S(1)}, bf16[2,256,1024]{2,1,0:T(8,128)(2,1)S(1)}, bf16[512,704]{1,0:T(8,128)(2,1)S(1)}, bf16[512,704]{1,0:T(8,128)(2,1)S(1)}, bf16[512,704]{1,0:T(8,128)(2,1)S(1)}) custom-call(bf16[256,1024]{1,0:T(8,128)(2,1)S(1)} %collective-permute-done.17.n0.refs_21_, ...), custom_call_target="tpu_custom_call" | custom-call | flops 4429185024 | bytes 9568256 | tf_op jit(solution)/shard_map/pallas_call | solution.py:380
  110.4 5.1 %shard_map.190 = (f32[2,256,1024]{2,1,0:T(8,128)S(1)}, bf16[2,256,1024]{2,1,0:T(8,128)(2,1)S(1)}, bf16[512,704]{1,0:T(8,128)(2,1)S(1)}, bf16[512,704]{1,0:T(8,128)(2,1)S(1)}, bf16[512,704]{1,0:T(8,128)(2,1)S(1)}) custom-call(bf16[256,1024]{1,0:T(8,128)(2,1)S(1)} %collective-permute-done.9.n0.refs_14_, ...), custom_call_target="tpu_custom_call" | custom-call | flops 4429185024 | bytes 9568256 | tf_op jit(solution)/shard_map/pallas_call | solution.py:380
  115.6 13.3 %shard_map.202 = (bf16[8,2,704,128]{3,2,1,0:T(8,128)(2,1)S(1)}, bf16[8,704,128]{2,1,0:T(8,128)(2,1)S(1)}) custom-call(s32[1]{0:T(128)} %bitcast.91.place, bf16[256,1024]{1,0:T(8,128)(2,1)S(1)} %get-tuple-element.81.n0.refs_0_, bf16[256,1024]{1,0:T(8,128)(2,1)S(1)} %collective-permute-done.6.n1.refs_1_, bf16[512,1024]{1,0:T(8,128)(2,1)} %refs_9_, ...), custom_call_target="tpu_custom_call" | custom-call | flops 8858370048 | bytes 21364736 | tf_op jit(solution)/shard_map/pallas_call | solution.py:464
  136.4 11.2 %collective-permute-done.79 = bf16[4,704,128]{2,1,0:T(8,128)(2,1)} collective-permute-done((bf16[4,704,128]{2,1,0:T(8,128)(2,1)}, bf16[4,704,128]{2,1,0:T(8,128)(2,1)}, u32[]{:S(2)}, u32[]{:S(2)}) %collective-permute-start.79) | collective-permute-done | bytes 720928 | tf_op jit(solution)/shard_map/ppermute | solution.py:25
  150.5 2.4 collective-permute-start.80
  154.1 3.4 shard_map.195
  157.6 3.5 shard_map.194
  165.9 2.6 collective-permute-done.80
  169.0 21.0 %collective-permute-done.24 = bf16[4,128,128]{2,1,0:T(8,128)(2,1)S(1)} collective-permute-done((bf16[4,128,128]{2,1,0:T(8,128)(2,1)S(1)}, bf16[4,128,128]{2,1,0:T(8,128)(2,1)S(1)}, u32[]{:S(2)}, u32[]{:S(2)}) %collective-permute-start.24) | collective-permute-done | bytes 131104 | tf_op jit(solution)/shard_map/ppermute | solution.py:25
  191.2 2.8 collective-permute-done.25
  198.1 1.7 collective-permute-start.27
  199.9 7.6 %shard_map.196 = (bf16[512,1024]{1,0:T(8,128)(2,1)S(1)}, f32[512,1024]{1,0:T(8,128)S(1)}, f32[512,1024]{1,0:T(8,128)S(1)}) custom-call(f32[8]{0:T(128)S(1)} %get-tuple-element.224.rate, f32[512,1024]{1,0:T(8,128)S(1)} %copy-done.41, bf16[512,1024]{1,0:T(8,128)(2,1)S(1)} %get-tuple-element.76.query, bf16[512,1024]{1,0:T(8,128)(2,1)S(1)} %copy-done.26, ...), custom_call_target="tpu_custom_call" | custom-call | flops 1610612736 | bytes 12582912 | tf_op jit(solution)/shard_map/pallas_call | solution.py:559
  207.6 6.6 %collective-permute-done.27 = bf16[4,128,128]{2,1,0:T(8,128)(2,1)S(1)} collective-permute-done((bf16[4,128,128]{2,1,0:T(8,128)(2,1)S(1)}, bf16[4,128,128]{2,1,0:T(8,128)(2,1)S(1)}, u32[]{:S(2)}, u32[]{:S(2)}) %collective-permute-start.27) | collective-permute-done | bytes 131104 | tf_op jit(solution)/shard_map/ppermute | solution.py:25
  214.5 3.7 collective-permute-start.28
  218.2 5.3 %shard_map.200 = (bf16[3,512,1024]{2,1,0:T(8,128)(2,1)S(1)}, bf16[3,512,1024]{2,1,0:T(8,128)(2,1)S(1)}) custom-call(s32[1]{0:T(128)} %bitcast.30.core, bf16[512,1024]{1,0:T(8,128)(2,1)S(1)} %pad_maximum_fusion.2.refs_0_, bf16[512,1024]{1,0:T(8,128)(2,1)S(1)} %copy-done.60, bf16[256,1024]{1,0:T(8,128)(2,1)S(1)} %get-tuple-element.114.refs_2_, ...), custom_call_target="tpu_custom_call" | custom-call | flops 3221225472 | bytes 12582912 | tf_op jit(solution)/shard_map/pallas_call | solution.py:654
  225.1 2.4 shard_map.197
  227.5 3.8 shard_map.201
  233.1 1.7 fusion.8
  236.1 3.2 collective-permute-start.78
  239.3 2.6 shard_map.199
  242.0 2.6 shard_map.198
  246.2 9.2 %collective-permute-done.78 = bf16[1,2,704,128]{3,2,1,0:T(8,128)(2,1)S(1)} collective-permute-done((bf16[1,2,704,128]{3,2,1,0:T(8,128)(2,1)S(1)}, bf16[1,2,704,128]{3,2,1,0:T(8,128)(2,1)S(1)}, u32[]{:S(2)}, u32[]{:S(2)}) %collective-permute-start.78) | collective-permute-done | bytes 360480 | tf_op jit(solution)/shard_map/ppermute | solution.py:25
  263.1 7.1 %collective-permute-done.40 = bf16[256,1024]{1,0:T(8,128)(2,1)S(1)} collective-permute-done((bf16[256,1024]{1,0:T(8,128)(2,1)S(1)}, bf16[256,1024]{1,0:T(8,128)(2,1)S(1)}, u32[]{:S(2)}, u32[]{:S(2)}) %collective-permute-start.40) | collective-permute-done | bytes 524320 | tf_op jit(solution)/shard_map/ppermute | solution.py:25
  271.5 1.7 collective-permute-done.30
  273.5 1.7 collective-permute-start.31
  275.2 12.8 %collective-permute-done.41 = bf16[128,1024]{1,0:T(8,128)(2,1)S(1)} collective-permute-done((bf16[128,1024]{1,0:T(8,128)(2,1)S(1)}, bf16[128,1024]{1,0:T(8,128)(2,1)S(1)}, u32[]{:S(2)}, u32[]{:S(2)}) %collective-permute-start.41) | collective-permute-done | bytes 262176 | tf_op jit(solution)/shard_map/ppermute | solution.py:25
  288.3 1.9 collective-permute-start.51
  294.0 6.2 %collective-permute-done.43 = bf16[32,1024]{1,0:T(8,128)(2,1)S(1)} collective-permute-done((bf16[32,1024]{1,0:T(8,128)(2,1)S(1)}, bf16[32,1024]{1,0:T(8,128)(2,1)S(1)}, u32[]{:S(2)}, u32[]{:S(2)}) %collective-permute-start.43) | collective-permute-done | bytes 65568 | tf_op jit(solution)/shard_map/ppermute | solution.py:25
  300.3 2.9 collective-permute-start.44
  305.4 1.8 collective-permute-start.45
  307.8 2.1 collective-permute-start.60
  311.8 3.1 collective-permute-done.54
  315.1 3.9 %collective-permute-done.60 = bf16[64,1024]{1,0:T(8,128)(2,1)S(1)} collective-permute-done((bf16[64,1024]{1,0:T(8,128)(2,1)S(1)}, bf16[64,1024]{1,0:T(8,128)(2,1)S(1)}, u32[]{:S(2)}, u32[]{:S(2)}) %collective-permute-start.60) | collective-permute-done | bytes 131104 | tf_op jit(solution)/shard_map/ppermute | solution.py:25
  319.7 2.9 collective-permute-done.61
  326.2 1.7 collective-permute-start.63
  330.8 2.2 collective-permute-start.47
  333.2 1.7 collective-permute-start.56
  335.3 6.3 %collective-permute-done.36 = bf16[128,1024]{1,0:T(8,128)(2,1)S(1)} collective-permute-done((bf16[128,1024]{1,0:T(8,128)(2,1)S(1)}, bf16[128,1024]{1,0:T(8,128)(2,1)S(1)}, u32[]{:S(2)}, u32[]{:S(2)}) %collective-permute-start.36) | collective-permute-done | bytes 262176 | tf_op jit(solution)/shard_map/ppermute | solution.py:25
  341.8 2.4 collective-permute-done.64
  345.5 17.5 %collective-permute-start.48 = (bf16[512,1024]{1,0:T(8,128)(2,1)S(1)}, bf16[512,1024]{1,0:T(8,128)(2,1)S(1)}, u32[]{:S(2)}, u32[]{:S(2)}) collective-permute-start(bf16[512,1024]{1,0:T(8,128)(2,1)S(1)} %pad_maximum_fusion.4), channel_id=1, source_target_pairs={{0,1},{1,0},{2,3},{3,2},{4,5},{5,4},{6,7},{7,6},{8,9},{9,8},{10,11... | collective-permute-start | bytes 3145736 | tf_op jit(solution)/shard_map/ppermute | solution.py:25
  364.6 3.0 collective-permute-start.66
  367.9 3.5 collective-permute-start.75
  372.0 2.5 maximum_convert_fusion.1
  375.0 2.4 maximum_convert_fusion.2
  378.1 2.4 maximum_convert_fusion
  381.1 2.4 maximum_convert_fusion.3
  384.2 2.4 maximum_convert_fusion.4
  (392 shorter events, 104.0 us)
Async XLA Ops:
  18.9 6.4 %collective-permute-start.1 = (bf16[4,128,128]{2,1,0:T(8,128)(2,1)S(1)}, bf16[4,128,128]{2,1,0:T(8,128)(2,1)S(1)}, u32[]{:S(2)}, u32[]{:S(2)}) collective-permute-start(bf16[4,128,128]{2,1,0:T(8,128)(2,1)S(1)} %fusion.72), channel_id=1, source_target_pairs={{0,2},{1,3},{2,0},{3,1},{4,6},{5,7},{6,4},{7,5},{8,10},{9,11},{10,... | collective-permute-start | bytes 393224 | tf_op jit(solution)/shard_map/ppermute | solution.py:25
  40.4 31.5 %collective-permute-start.11 = (bf16[512,1024]{1,0:T(8,128)(2,1)}, bf16[512,1024]{1,0:T(8,128)(2,1)S(1)}, u32[]{:S(2)}, u32[]{:S(2)}) collective-permute-start(bf16[512,1024]{1,0:T(8,128)(2,1)} %refs_9_), channel_id=1, source_target_pairs={{0,2},{1,3},{2,0},{3,1},{4,6},{5,7},{6,4},{7,5},{8,10},{9,11},{10,... | collective-permute-start | bytes 3145736 | tf_op jit(solution)/shard_map/ppermute | solution.py:25
  45.8 17.0 %collective-permute-start.5 = (bf16[4,128,128]{2,1,0:T(8,128)(2,1)S(1)}, bf16[4,128,128]{2,1,0:T(8,128)(2,1)S(1)}, u32[]{:S(2)}, u32[]{:S(2)}) collective-permute-start(bf16[4,128,128]{2,1,0:T(8,128)(2,1)S(1)} %get-tuple-element.140), channel_id=1, source_target_pairs={{0,1},{1,0},{2,3},{3,2},{4,5},{5,4},{6,7},{7,6},{8,9},{9,8},{10,11... | collective-permute-start | bytes 393224 | tf_op jit(solution)/shard_map/ppermute | solution.py:25
  62.7 22.4 %collective-permute-start.7 = (bf16[512,1024]{1,0:T(8,128)(2,1)}, bf16[512,1024]{1,0:T(8,128)(2,1)S(1)}, u32[]{:S(2)}, u32[]{:S(2)}) collective-permute-start(bf16[512,1024]{1,0:T(8,128)(2,1)} %refs_9_), channel_id=1, source_target_pairs={{0,1},{1,0},{2,3},{3,2},{4,5},{5,4},{6,7},{7,6},{8,9},{9,8},{10,11... | collective-permute-start | bytes 3145736 | tf_op jit(solution)/shard_map/ppermute | solution.py:25
  70.3 13.5 %collective-permute-start.17 = (bf16[256,1024]{1,0:T(8,128)(2,1)S(1)}, bf16[256,1024]{1,0:T(8,128)(2,1)S(1)}, u32[]{:S(2)}, u32[]{:S(2)}) collective-permute-start(bf16[256,1024]{1,0:T(8,128)(2,1)S(1)} %get-tuple-element.88.n0.refs_7_), channel_id=1, source_target_pairs={{0,2},{1,3},{2,0},{3,1},{4,6},{5,7},{6,4},{7,5},{8,10},{9,11},{10,... | collective-permute-start | bytes 1572872 | tf_op jit(solution)/shard_map/ppermute | solution.py:25
  71.7 13.4 %collective-permute-start.15 = (bf16[256,1024]{1,0:T(8,128)(2,1)S(1)}, bf16[256,1024]{1,0:T(8,128)(2,1)S(1)}, u32[]{:S(2)}, u32[]{:S(2)}) collective-permute-start(bf16[256,1024]{1,0:T(8,128)(2,1)S(1)} %get-tuple-element.88.n0.refs_7_), channel_id=1, source_target_pairs={{0,1},{1,0},{2,3},{3,2},{4,5},{5,4},{6,7},{7,6},{8,9},{9,8},{10,11... | collective-permute-start | bytes 1572872 | tf_op jit(solution)/shard_map/ppermute | solution.py:25
  72.0 32.5 %collective-permute-start.12 = (bf16[512,1024]{1,0:T(8,128)(2,1)S(1)}, bf16[512,1024]{1,0:T(8,128)(2,1)S(1)}, u32[]{:S(2)}, u32[]{:S(2)}) collective-permute-start(bf16[512,1024]{1,0:T(8,128)(2,1)S(1)} %collective-permute-done.11.c0.refs_16_.refs_23_), channel_id=1, source_target_pairs={{0,1},{1,0},{2,3},{3,2},{4,5},{5,4},{6,7},{7,6},{8,9},{9,8},{10,11... | collective-permute-start | bytes 3145736 | tf_op jit(solution)/shard_map/ppermute | solution.py:25
  77.5 17.6 %collective-permute-start.9 = (bf16[256,1024]{1,0:T(8,128)(2,1)S(1)}, bf16[256,1024]{1,0:T(8,128)(2,1)S(1)}, u32[]{:S(2)}, u32[]{:S(2)}) collective-permute-start(bf16[256,1024]{1,0:T(8,128)(2,1)S(1)} %get-tuple-element.81.n0.refs_0_), channel_id=1, source_target_pairs={{0,2},{1,3},{2,0},{3,1},{4,6},{5,7},{6,4},{7,5},{8,10},{9,11},{10,... | collective-permute-start | bytes 1572872 | tf_op jit(solution)/shard_map/ppermute | solution.py:25
  83.9 12.1 %collective-permute-start.6 = (bf16[256,1024]{1,0:T(8,128)(2,1)S(1)}, bf16[256,1024]{1,0:T(8,128)(2,1)S(1)}, u32[]{:S(2)}, u32[]{:S(2)}) collective-permute-start(bf16[256,1024]{1,0:T(8,128)(2,1)S(1)} %get-tuple-element.81.n0.refs_0_), channel_id=1, source_target_pairs={{0,1},{1,0},{2,3},{3,2},{4,5},{5,4},{6,7},{7,6},{8,9},{9,8},{10,11... | collective-permute-start | bytes 1572872 | tf_op jit(solution)/shard_map/ppermute | solution.py:25
  85.1 19.3 %collective-permute-start.18 = (bf16[256,1024]{1,0:T(8,128)(2,1)S(1)}, bf16[256,1024]{1,0:T(8,128)(2,1)S(1)}, u32[]{:S(2)}, u32[]{:S(2)}) collective-permute-start(bf16[256,1024]{1,0:T(8,128)(2,1)S(1)} %collective-permute-done.17.n0.refs_21_), channel_id=1, source_target_pairs={{0,1},{1,0},{2,3},{3,2},{4,5},{5,4},{6,7},{7,6},{8,9},{9,8},{10,11... | collective-permute-start | bytes 1572872 | tf_op jit(solution)/shard_map/ppermute | solution.py:25
  93.6 56.8 %collective-permute-start.16 = (bf16[2,256,1024]{2,1,0:T(8,128)(2,1)}, bf16[2,256,1024]{2,1,0:T(8,128)(2,1)}, u32[]{:S(2)}, u32[]{:S(2)}) collective-permute-start(bf16[2,256,1024]{2,1,0:T(8,128)(2,1)} %get-tuple-element.90), channel_id=1, source_target_pairs={{0,1},{1,0},{2,3},{3,2},{4,5},{5,4},{6,7},{7,6},{8,9},{9,8},{10,11... | collective-permute-start | bytes 3145736 | tf_op jit(solution)/shard_map/ppermute | solution.py:25
  95.1 15.3 %collective-permute-start.10 = (bf16[256,1024]{1,0:T(8,128)(2,1)S(1)}, bf16[256,1024]{1,0:T(8,128)(2,1)S(1)}, u32[]{:S(2)}, u32[]{:S(2)}) collective-permute-start(bf16[256,1024]{1,0:T(8,128)(2,1)S(1)} %collective-permute-done.9.n0.refs_14_), channel_id=1, source_target_pairs={{0,1},{1,0},{2,3},{3,2},{4,5},{5,4},{6,7},{7,6},{8,9},{9,8},{10,11... | collective-permute-start | bytes 1572872 | tf_op jit(solution)/shard_map/ppermute | solution.py:25
  104.4 53.2 %collective-permute-start.8 = (bf16[2,256,1024]{2,1,0:T(8,128)(2,1)}, bf16[2,256,1024]{2,1,0:T(8,128)(2,1)}, u32[]{:S(2)}, u32[]{:S(2)}) collective-permute-start(bf16[2,256,1024]{2,1,0:T(8,128)(2,1)} %get-tuple-element.84), channel_id=1, source_target_pairs={{0,1},{1,0},{2,3},{3,2},{4,5},{5,4},{6,7},{7,6},{8,9},{9,8},{10,11... | collective-permute-start | bytes 3145736 | tf_op jit(solution)/shard_map/ppermute | solution.py:25
  109.8 20.8 %collective-permute-start.19 = (bf16[2,256,1024]{2,1,0:T(8,128)(2,1)S(1)}, bf16[2,256,1024]{2,1,0:T(8,128)(2,1)S(1)}, u32[]{:S(2)}, u32[]{:S(2)}) collective-permute-start(bf16[2,256,1024]{2,1,0:T(8,128)(2,1)S(1)} %get-tuple-element.92), channel_id=1, source_target_pairs={{0,1},{1,0},{2,3},{3,2},{4,5},{5,4},{6,7},{7,6},{8,9},{9,8},{10,11... | collective-permute-start | bytes 3145736 | tf_op jit(solution)/shard_map/ppermute | solution.py:25
  115.5 17.6 %collective-permute-start.13 = (bf16[2,256,1024]{2,1,0:T(8,128)(2,1)S(1)}, bf16[2,256,1024]{2,1,0:T(8,128)(2,1)S(1)}, u32[]{:S(2)}, u32[]{:S(2)}) collective-permute-start(bf16[2,256,1024]{2,1,0:T(8,128)(2,1)S(1)} %get-tuple-element.86), channel_id=1, source_target_pairs={{0,1},{1,0},{2,3},{3,2},{4,5},{5,4},{6,7},{7,6},{8,9},{9,8},{10,11... | collective-permute-start | bytes 3145736 | tf_op jit(solution)/shard_map/ppermute | solution.py:25
  130.0 17.6 %collective-permute-start.79 = (bf16[4,704,128]{2,1,0:T(8,128)(2,1)}, bf16[4,704,128]{2,1,0:T(8,128)(2,1)}, u32[]{:S(2)}, u32[]{:S(2)}) collective-permute-start(bf16[4,704,128]{2,1,0:T(8,128)(2,1)} %slice.121), channel_id=1, source_target_pairs={{0,8},{1,9},{2,10},{3,11},{4,12},{5,13},{6,14},{7,15},{8,0},{9,1},... | collective-permute-start | bytes 2162696 | tf_op jit(solution)/shard_map/ppermute | solution.py:25
  132.0 20.9 %collective-permute-start.22 = (bf16[256,1024]{1,0:T(8,128)(2,1)}, bf16[256,1024]{1,0:T(8,128)(2,1)}, u32[]{:S(2)}, u32[]{:S(2)}) collective-permute-start(bf16[256,1024]{1,0:T(8,128)(2,1)} %get-tuple-element.149), channel_id=1, source_target_pairs={{0,2},{1,3},{2,0},{3,1},{4,6},{5,7},{6,4},{7,5},{8,10},{9,11},{10,... | collective-permute-start | bytes 1572872 | tf_op jit(solution)/shard_map/ppermute | solution.py:25
  134.5 23.1 %collective-permute-start.21 = (bf16[256,1024]{1,0:T(8,128)(2,1)}, bf16[256,1024]{1,0:T(8,128)(2,1)}, u32[]{:S(2)}, u32[]{:S(2)}) collective-permute-start(bf16[256,1024]{1,0:T(8,128)(2,1)} %get-tuple-element.147), channel_id=1, source_target_pairs={{0,2},{1,3},{2,0},{3,1},{4,6},{5,7},{6,4},{7,5},{8,10},{9,11},{10,... | collective-permute-start | bytes 1572872 | tf_op jit(solution)/shard_map/ppermute | solution.py:25
  147.6 48.1 %collective-permute-start.76 = (bf16[4,2,704,128]{3,2,1,0:T(8,128)(2,1)S(1)}, bf16[4,2,704,128]{3,2,1,0:T(8,128)(2,1)S(1)}, u32[]{:S(2)}, u32[]{:S(2)}) collective-permute-start(bf16[4,2,704,128]{3,2,1,0:T(8,128)(2,1)S(1)} %slice.113), channel_id=1, source_target_pairs={{0,4},{1,5},{2,6},{3,7},{4,0},{5,1},{6,2},{7,3},{8,12},{9,13},{10,... | collective-permute-start | bytes 4325384 | tf_op jit(solution)/shard_map/ppermute | solution.py:25
  150.5 18.1 %collective-permute-start.80 = (bf16[2,704,128]{2,1,0:T(8,128)(2,1)S(1)}, bf16[2,704,128]{2,1,0:T(8,128)(2,1)S(1)}, u32[]{:S(2)}, u32[]{:S(2)}) collective-permute-start(bf16[2,704,128]{2,1,0:T(8,128)(2,1)S(1)} %slice.144), channel_id=1, source_target_pairs={{0,16},{1,17},{2,18},{3,19},{4,20},{5,21},{6,22},{7,23},{8,24},{9,... | collective-permute-start | bytes 1081352 | tf_op jit(solution)/shard_map/ppermute | solution.py:25
  163.0 68.4 %collective-permute-start.20 = (bf16[256,1024]{1,0:T(8,128)(2,1)}, bf16[256,1024]{1,0:T(8,128)(2,1)}, u32[]{:S(2)}, u32[]{:S(2)}) collective-permute-start(bf16[256,1024]{1,0:T(8,128)(2,1)} %get-tuple-element.150), channel_id=1, source_target_pairs={{0,2},{1,3},{2,0},{3,1},{4,6},{5,7},{6,4},{7,5},{8,10},{9,11},{10,... | collective-permute-start | bytes 1572872 | tf_op jit(solution)/shard_map/ppermute | solution.py:25
  164.3 68.8 %collective-permute-start.14 = (bf16[256,1024]{1,0:T(8,128)(2,1)}, bf16[256,1024]{1,0:T(8,128)(2,1)}, u32[]{:S(2)}, u32[]{:S(2)}) collective-permute-start(bf16[256,1024]{1,0:T(8,128)(2,1)} %get-tuple-element.148), channel_id=1, source_target_pairs={{0,2},{1,3},{2,0},{3,1},{4,6},{5,7},{6,4},{7,5},{8,10},{9,11},{10,... | collective-permute-start | bytes 1572872 | tf_op jit(solution)/shard_map/ppermute | solution.py:25
  164.7 25.3 %collective-permute-start.24 = (bf16[4,128,128]{2,1,0:T(8,128)(2,1)S(1)}, bf16[4,128,128]{2,1,0:T(8,128)(2,1)S(1)}, u32[]{:S(2)}, u32[]{:S(2)}) collective-permute-start(bf16[4,128,128]{2,1,0:T(8,128)(2,1)S(1)} %fusion.71), channel_id=1, source_target_pairs={{0,2},{1,3},{2,0},{3,1},{4,6},{5,7},{6,4},{7,5},{8,10},{9,11},{10,... | collective-permute-start | bytes 393224 | tf_op jit(solution)/shard_map/ppermute | solution.py:25
  168.7 21.7 %collective-permute-start.81 = (bf16[1,704,128]{2,1,0:T(8,128)(2,1)S(1)}, bf16[1,704,128]{2,1,0:T(8,128)(2,1)S(1)}, u32[]{:S(2)}, u32[]{:S(2)}) collective-permute-start(bf16[1,704,128]{2,1,0:T(8,128)(2,1)S(1)} %slice.146), channel_id=1, source_target_pairs={{0,4},{1,5},{2,6},{3,7},{4,0},{5,1},{6,2},{7,3},{8,12},{9,13},{10,... | collective-permute-start | bytes 540680 | tf_op jit(solution)/shard_map/ppermute | solution.py:25
  197.0 38.9 %collective-permute-start.77 = (bf16[2,2,704,128]{3,2,1,0:T(8,128)(2,1)}, bf16[2,2,704,128]{3,2,1,0:T(8,128)(2,1)S(1)}, u32[]{:S(2)}, u32[]{:S(2)}) collective-permute-start(bf16[2,2,704,128]{3,2,1,0:T(8,128)(2,1)} %slice.138), channel_id=1, source_target_pairs={{0,8},{1,9},{2,10},{3,11},{4,12},{5,13},{6,14},{7,15},{8,0},{9,1},... | collective-permute-start | bytes 2162696 | tf_op jit(solution)/shard_map/ppermute | solution.py:25
  198.1 16.0 %collective-permute-start.27 = (bf16[4,128,128]{2,1,0:T(8,128)(2,1)S(1)}, bf16[4,128,128]{2,1,0:T(8,128)(2,1)S(1)}, u32[]{:S(2)}, u32[]{:S(2)}) collective-permute-start(bf16[4,128,128]{2,1,0:T(8,128)(2,1)S(1)} %fusion.48), channel_id=1, source_target_pairs={{0,16},{1,17},{2,18},{3,19},{4,20},{5,21},{6,22},{7,23},{8,24},{9,... | collective-permute-start | bytes 393224 | tf_op jit(solution)/shard_map/ppermute | solution.py:25
  214.5 9.1 %collective-permute-start.28 = (bf16[4,128,128]{2,1,0:T(8,128)(2,1)S(1)}, bf16[4,128,128]{2,1,0:T(8,128)(2,1)S(1)}, u32[]{:S(2)}, u32[]{:S(2)}) collective-permute-start(bf16[4,128,128]{2,1,0:T(8,128)(2,1)S(1)} %get-tuple-element.134), channel_id=1, source_target_pairs={{0,1},{1,0},{2,3},{3,2},{4,5},{5,4},{6,7},{7,6},{8,9},{9,8},{10,11... | collective-permute-start | bytes 393224 | tf_op jit(solution)/shard_map/ppermute | solution.py:25
  223.5 35.8 %collective-permute-start.29 = (bf16[3,512,1024]{2,1,0:T(8,128)(2,1)S(1)}, bf16[3,512,1024]{2,1,0:T(8,128)(2,1)S(1)}, u32[]{:S(2)}, u32[]{:S(2)}) collective-permute-start(bf16[3,512,1024]{2,1,0:T(8,128)(2,1)S(1)} %get-tuple-element.117), channel_id=1, source_target_pairs={{0,1},{1,0},{2,3},{3,2},{4,5},{5,4},{6,7},{7,6},{8,9},{9,8},{10,11... | collective-permute-start | bytes 9437192 | tf_op jit(solution)/shard_map/ppermute | solution.py:25
  231.3 25.1 %collective-permute-start.39 = (bf16[2,512,1024]{2,1,0:T(8,128)(2,1)S(1)}, bf16[2,512,1024]{2,1,0:T(8,128)(2,1)S(1)}, u32[]{:S(2)}, u32[]{:S(2)}) collective-permute-start(bf16[2,512,1024]{2,1,0:T(8,128)(2,1)S(1)} %get-tuple-element.119), channel_id=1, source_target_pairs={{0,1},{1,0},{2,3},{3,2},{4,5},{5,4},{6,7},{7,6},{8,9},{9,8},{10,11... | collective-permute-start | bytes 6291464 | tf_op jit(solution)/shard_map/ppermute | solution.py:25
  236.1 19.3 %collective-permute-start.78 = (bf16[1,2,704,128]{3,2,1,0:T(8,128)(2,1)S(1)}, bf16[1,2,704,128]{3,2,1,0:T(8,128)(2,1)S(1)}, u32[]{:S(2)}, u32[]{:S(2)}) collective-permute-start(bf16[1,2,704,128]{3,2,1,0:T(8,128)(2,1)S(1)} %slice.140), channel_id=1, source_target_pairs={{0,16},{1,17},{2,18},{3,19},{4,20},{5,21},{6,22},{7,23},{8,24},{9,... | collective-permute-start | bytes 1081352 | tf_op jit(solution)/shard_map/ppermute | solution.py:25
  257.7 12.5 %collective-permute-start.40 = (bf16[256,1024]{1,0:T(8,128)(2,1)S(1)}, bf16[256,1024]{1,0:T(8,128)(2,1)S(1)}, u32[]{:S(2)}, u32[]{:S(2)}) collective-permute-start(bf16[256,1024]{1,0:T(8,128)(2,1)S(1)} %dynamic-slice_bitcast_fusion.3), channel_id=1, source_target_pairs={{0,2},{1,3},{2,0},{3,1},{4,6},{5,7},{6,4},{7,5},{8,10},{9,11},{10,... | collective-permute-start | bytes 1572872 | tf_op jit(solution)/shard_map/ppermute | solution.py:25
  259.0 12.2 %collective-permute-start.49 = (bf16[256,1024]{1,0:T(8,128)(2,1)S(1)}, bf16[256,1024]{1,0:T(8,128)(2,1)S(1)}, u32[]{:S(2)}, u32[]{:S(2)}) collective-permute-start(bf16[256,1024]{1,0:T(8,128)(2,1)S(1)} %dynamic-slice_bitcast_fusion.2), channel_id=1, source_target_pairs={{0,4},{1,5},{2,6},{3,7},{4,0},{5,1},{6,2},{7,3},{8,12},{9,13},{10,... | collective-permute-start | bytes 1572872 | tf_op jit(solution)/shard_map/ppermute | solution.py:25
  261.3 11.9 %collective-permute-start.30 = (bf16[256,1024]{1,0:T(8,128)(2,1)S(1)}, bf16[256,1024]{1,0:T(8,128)(2,1)S(1)}, u32[]{:S(2)}, u32[]{:S(2)}) collective-permute-start(bf16[256,1024]{1,0:T(8,128)(2,1)S(1)} %dynamic-slice_bitcast_fusion.4), channel_id=1, source_target_pairs={{0,8},{1,9},{2,10},{3,11},{4,12},{5,13},{6,14},{7,15},{8,0},{9,1},... | collective-permute-start | bytes 1572872 | tf_op jit(solution)/shard_map/ppermute | solution.py:25
  261.4 28.8 %collective-permute-start.58 = (bf16[256,1024]{1,0:T(8,128)(2,1)S(1)}, bf16[256,1024]{1,0:T(8,128)(2,1)S(1)}, u32[]{:S(2)}, u32[]{:S(2)}) collective-permute-start(bf16[256,1024]{1,0:T(8,128)(2,1)S(1)} %dynamic-slice_bitcast_fusion.1), channel_id=1, source_target_pairs={{0,4},{1,5},{2,6},{3,7},{4,0},{5,1},{6,2},{7,3},{8,12},{9,13},{10,... | collective-permute-start | bytes 1572872 | tf_op jit(solution)/shard_map/ppermute | solution.py:25
  262.8 27.8 %collective-permute-start.67 = (bf16[256,1024]{1,0:T(8,128)(2,1)S(1)}, bf16[256,1024]{1,0:T(8,128)(2,1)S(1)}, u32[]{:S(2)}, u32[]{:S(2)}) collective-permute-start(bf16[256,1024]{1,0:T(8,128)(2,1)S(1)} %dynamic-slice_bitcast_fusion), channel_id=1, source_target_pairs={{0,2},{1,3},{2,0},{3,1},{4,6},{5,7},{6,4},{7,5},{8,10},{9,11},{10,... | collective-permute-start | bytes 1572872 | tf_op jit(solution)/shard_map/ppermute | solution.py:25
  270.4 17.6 %collective-permute-start.41 = (bf16[128,1024]{1,0:T(8,128)(2,1)S(1)}, bf16[128,1024]{1,0:T(8,128)(2,1)S(1)}, u32[]{:S(2)}, u32[]{:S(2)}) collective-permute-start(bf16[128,1024]{1,0:T(8,128)(2,1)S(1)} %dynamic-slice_bitcast_fusion.8), channel_id=1, source_target_pairs={{0,4},{1,5},{2,6},{3,7},{4,0},{5,1},{6,2},{7,3},{8,12},{9,13},{10,... | collective-permute-start | bytes 786440 | tf_op jit(solution)/shard_map/ppermute | solution.py:25
  271.4 16.8 %collective-permute-start.50 = (bf16[128,1024]{1,0:T(8,128)(2,1)S(1)}, bf16[128,1024]{1,0:T(8,128)(2,1)S(1)}, u32[]{:S(2)}, u32[]{:S(2)}) collective-permute-start(bf16[128,1024]{1,0:T(8,128)(2,1)S(1)} %dynamic-slice_bitcast_fusion.7), channel_id=1, source_target_pairs={{0,8},{1,9},{2,10},{3,11},{4,12},{5,13},{6,14},{7,15},{8,0},{9,1},... | collective-permute-start | bytes 786440 | tf_op jit(solution)/shard_map/ppermute | solution.py:25
  273.5 30.1 %collective-permute-start.31 = (bf16[128,1024]{1,0:T(8,128)(2,1)S(1)}, bf16[128,1024]{1,0:T(8,128)(2,1)S(1)}, u32[]{:S(2)}, u32[]{:S(2)}) collective-permute-start(bf16[128,1024]{1,0:T(8,128)(2,1)S(1)} %dynamic-slice_bitcast_fusion.9), channel_id=1, source_target_pairs={{0,16},{1,17},{2,18},{3,19},{4,20},{5,21},{6,22},{7,23},{8,24},{9,... | collective-permute-start | bytes 786440 | tf_op jit(solution)/shard_map/ppermute | solution.py:25
  290.5 17.2 %collective-permute-start.59 = (bf16[128,1024]{1,0:T(8,128)(2,1)S(1)}, bf16[128,1024]{1,0:T(8,128)(2,1)S(1)}, u32[]{:S(2)}, u32[]{:S(2)}) collective-permute-start(bf16[128,1024]{1,0:T(8,128)(2,1)S(1)} %dynamic-slice_bitcast_fusion.6), channel_id=1, source_target_pairs={{0,8},{1,9},{2,10},{3,11},{4,12},{5,13},{6,14},{7,15},{8,0},{9,1},... | collective-permute-start | bytes 786440 | tf_op jit(solution)/shard_map/ppermute | solution.py:25
  290.8 19.1 %collective-permute-start.68 = (bf16[128,1024]{1,0:T(8,128)(2,1)S(1)}, bf16[128,1024]{1,0:T(8,128)(2,1)S(1)}, u32[]{:S(2)}, u32[]{:S(2)}) collective-permute-start(bf16[128,1024]{1,0:T(8,128)(2,1)S(1)} %dynamic-slice_bitcast_fusion.5), channel_id=1, source_target_pairs={{0,4},{1,5},{2,6},{3,7},{4,0},{5,1},{6,2},{7,3},{8,12},{9,13},{10,... | collective-permute-start | bytes 786440 | tf_op jit(solution)/shard_map/ppermute | solution.py:25
  293.3 7.0 %collective-permute-start.43 = (bf16[32,1024]{1,0:T(8,128)(2,1)S(1)}, bf16[32,1024]{1,0:T(8,128)(2,1)S(1)}, u32[]{:S(2)}, u32[]{:S(2)}) collective-permute-start(bf16[32,1024]{1,0:T(8,128)(2,1)S(1)} %dynamic-slice_bitcast_fusion.18), channel_id=1, source_target_pairs={{0,16},{1,17},{2,18},{3,19},{4,20},{5,21},{6,22},{7,23},{8,24},{9,... | collective-permute-start | bytes 196616 | tf_op jit(solution)/shard_map/ppermute | solution.py:25
  293.7 9.5 %collective-permute-start.52 = (bf16[32,1024]{1,0:T(8,128)(2,1)S(1)}, bf16[32,1024]{1,0:T(8,128)(2,1)S(1)}, u32[]{:S(2)}, u32[]{:S(2)}) collective-permute-start(bf16[32,1024]{1,0:T(8,128)(2,1)S(1)} %dynamic-slice_bitcast_fusion.17), channel_id=1, source_target_pairs={{0,2},{1,3},{2,0},{3,1},{4,6},{5,7},{6,4},{7,5},{8,10},{9,11},{10,... | collective-permute-start | bytes 196616 | tf_op jit(solution)/shard_map/ppermute | solution.py:25
  303.6 6.4 %collective-permute-start.32 = (bf16[64,1024]{1,0:T(8,128)(2,1)S(1)}, bf16[64,1024]{1,0:T(8,128)(2,1)S(1)}, u32[]{:S(2)}, u32[]{:S(2)}) collective-permute-start(bf16[64,1024]{1,0:T(8,128)(2,1)S(1)} %dynamic-slice_bitcast_fusion.14), channel_id=1, source_target_pairs={{0,2},{1,3},{2,0},{3,1},{4,6},{5,7},{6,4},{7,5},{8,10},{9,11},{10,... | collective-permute-start | bytes 393224 | tf_op jit(solution)/shard_map/ppermute | solution.py:25
  307.3 7.7 %collective-permute-start.54 = (bf16[64,1024]{1,0:T(8,128)(2,1)S(1)}, bf16[64,1024]{1,0:T(8,128)(2,1)S(1)}, u32[]{:S(2)}, u32[]{:S(2)}) collective-permute-start(bf16[64,1024]{1,0:T(8,128)(2,1)S(1)} %pad_maximum_fusion.24), channel_id=1, source_target_pairs={{0,16},{1,17},{2,18},{3,19},{4,20},{5,21},{6,22},{7,23},{8,24},{9,... | collective-permute-start | bytes 393224 | tf_op jit(solution)/shard_map/ppermute | solution.py:25
  307.8 11.2 %collective-permute-start.60 = (bf16[64,1024]{1,0:T(8,128)(2,1)S(1)}, bf16[64,1024]{1,0:T(8,128)(2,1)S(1)}, u32[]{:S(2)}, u32[]{:S(2)}) collective-permute-start(bf16[64,1024]{1,0:T(8,128)(2,1)S(1)} %dynamic-slice_bitcast_fusion.11), channel_id=1, source_target_pairs={{0,16},{1,17},{2,18},{3,19},{4,20},{5,21},{6,22},{7,23},{8,24},{9,... | collective-permute-start | bytes 393224 | tf_op jit(solution)/shard_map/ppermute | solution.py:25
  310.0 9.4 %collective-permute-start.69 = (bf16[64,1024]{1,0:T(8,128)(2,1)S(1)}, bf16[64,1024]{1,0:T(8,128)(2,1)S(1)}, u32[]{:S(2)}, u32[]{:S(2)}) collective-permute-start(bf16[64,1024]{1,0:T(8,128)(2,1)S(1)} %dynamic-slice_bitcast_fusion.10), channel_id=1, source_target_pairs={{0,8},{1,9},{2,10},{3,11},{4,12},{5,13},{6,14},{7,15},{8,0},{9,1},... | collective-permute-start | bytes 393224 | tf_op jit(solution)/shard_map/ppermute | solution.py:25
  310.1 9.4 %collective-permute-start.33 = (bf16[32,1024]{1,0:T(8,128)(2,1)S(1)}, bf16[32,1024]{1,0:T(8,128)(2,1)S(1)}, u32[]{:S(2)}, u32[]{:S(2)}) collective-permute-start(bf16[32,1024]{1,0:T(8,128)(2,1)S(1)} %dynamic-slice_bitcast_fusion.19), channel_id=1, source_target_pairs={{0,4},{1,5},{2,6},{3,7},{4,0},{5,1},{6,2},{7,3},{8,12},{9,13},{10,... | collective-permute-start | bytes 196616 | tf_op jit(solution)/shard_map/ppermute | solution.py:25
  310.7 20.0 %collective-permute-start.46 = (bf16[128,1024]{1,0:T(8,128)(2,1)S(1)}, bf16[128,1024]{1,0:T(8,128)(2,1)S(1)}, u32[]{:S(2)}, u32[]{:S(2)}) collective-permute-start(bf16[128,1024]{1,0:T(8,128)(2,1)S(1)} %pad_maximum_fusion.18), channel_id=1, source_target_pairs={{0,4},{1,5},{2,6},{3,7},{4,0},{5,1},{6,2},{7,3},{8,12},{9,13},{10,... | collective-permute-start | bytes 786440 | tf_op jit(solution)/shard_map/ppermute | solution.py:25
  315.0 18.0 %collective-permute-start.55 = (bf16[128,1024]{1,0:T(8,128)(2,1)S(1)}, bf16[128,1024]{1,0:T(8,128)(2,1)S(1)}, u32[]{:S(2)}, u32[]{:S(2)}) collective-permute-start(bf16[128,1024]{1,0:T(8,128)(2,1)S(1)} %pad_maximum_fusion.19), channel_id=1, source_target_pairs={{0,8},{1,9},{2,10},{3,11},{4,12},{5,13},{6,14},{7,15},{8,0},{9,1},... | collective-permute-start | bytes 786440 | tf_op jit(solution)/shard_map/ppermute | solution.py:25
  326.2 8.7 %collective-permute-start.63 = (bf16[64,1024]{1,0:T(8,128)(2,1)S(1)}, bf16[64,1024]{1,0:T(8,128)(2,1)S(1)}, u32[]{:S(2)}, u32[]{:S(2)}) collective-permute-start(bf16[64,1024]{1,0:T(8,128)(2,1)S(1)} %pad_maximum_fusion.25), channel_id=1, source_target_pairs={{0,16},{1,17},{2,18},{3,19},{4,20},{5,21},{6,22},{7,23},{8,24},{9,... | collective-permute-start | bytes 393224 | tf_op jit(solution)/shard_map/ppermute | solution.py:25
  328.1 7.0 %collective-permute-start.72 = (bf16[64,1024]{1,0:T(8,128)(2,1)S(1)}, bf16[64,1024]{1,0:T(8,128)(2,1)S(1)}, u32[]{:S(2)}, u32[]{:S(2)}) collective-permute-start(bf16[64,1024]{1,0:T(8,128)(2,1)S(1)} %pad_maximum_fusion.26), channel_id=1, source_target_pairs={{0,8},{1,9},{2,10},{3,11},{4,12},{5,13},{6,14},{7,15},{8,0},{9,1},... | collective-permute-start | bytes 393224 | tf_op jit(solution)/shard_map/ppermute | solution.py:25
  329.6 12.0 %collective-permute-start.36 = (bf16[128,1024]{1,0:T(8,128)(2,1)S(1)}, bf16[128,1024]{1,0:T(8,128)(2,1)S(1)}, u32[]{:S(2)}, u32[]{:S(2)}) collective-permute-start(bf16[128,1024]{1,0:T(8,128)(2,1)S(1)} %pad_maximum_fusion.17), channel_id=1, source_target_pairs={{0,16},{1,17},{2,18},{3,19},{4,20},{5,21},{6,22},{7,23},{8,24},{9,... | collective-permute-start | bytes 786440 | tf_op jit(solution)/shard_map/ppermute | solution.py:25
  330.8 14.4 %collective-permute-start.47 = (bf16[256,1024]{1,0:T(8,128)(2,1)S(1)}, bf16[256,1024]{1,0:T(8,128)(2,1)S(1)}, u32[]{:S(2)}, u32[]{:S(2)}) collective-permute-start(bf16[256,1024]{1,0:T(8,128)(2,1)S(1)} %pad_maximum_fusion.11), channel_id=1, source_target_pairs={{0,2},{1,3},{2,0},{3,1},{4,6},{5,7},{6,4},{7,5},{8,10},{9,11},{10,... | collective-permute-start | bytes 1572872 | tf_op jit(solution)/shard_map/ppermute | solution.py:25
  333.2 29.8 %collective-permute-start.56 = (bf16[256,1024]{1,0:T(8,128)(2,1)S(1)}, bf16[256,1024]{1,0:T(8,128)(2,1)S(1)}, u32[]{:S(2)}, u32[]{:S(2)}) collective-permute-start(bf16[256,1024]{1,0:T(8,128)(2,1)S(1)} %pad_maximum_fusion.12), channel_id=1, source_target_pairs={{0,4},{1,5},{2,6},{3,7},{4,0},{5,1},{6,2},{7,3},{8,12},{9,13},{10,... | collective-permute-start | bytes 1572872 | tf_op jit(solution)/shard_map/ppermute | solution.py:25
  335.0 9.2 %collective-permute-start.64 = (bf16[128,1024]{1,0:T(8,128)(2,1)S(1)}, bf16[128,1024]{1,0:T(8,128)(2,1)S(1)}, u32[]{:S(2)}, u32[]{:S(2)}) collective-permute-start(bf16[128,1024]{1,0:T(8,128)(2,1)S(1)} %pad_maximum_fusion.20), channel_id=1, source_target_pairs={{0,8},{1,9},{2,10},{3,11},{4,12},{5,13},{6,14},{7,15},{8,0},{9,1},... | collective-permute-start | bytes 786440 | tf_op jit(solution)/shard_map/ppermute | solution.py:25
  335.2 9.4 %collective-permute-start.73 = (bf16[128,1024]{1,0:T(8,128)(2,1)S(1)}, bf16[128,1024]{1,0:T(8,128)(2,1)S(1)}, u32[]{:S(2)}, u32[]{:S(2)}) collective-permute-start(bf16[128,1024]{1,0:T(8,128)(2,1)S(1)} %pad_maximum_fusion.21), channel_id=1, source_target_pairs={{0,4},{1,5},{2,6},{3,7},{4,0},{5,1},{6,2},{7,3},{8,12},{9,13},{10,... | collective-permute-start | bytes 786440 | tf_op jit(solution)/shard_map/ppermute | solution.py:25
  341.8 21.6 %collective-permute-start.37 = (bf16[256,1024]{1,0:T(8,128)(2,1)S(1)}, bf16[256,1024]{1,0:T(8,128)(2,1)S(1)}, u32[]{:S(2)}, u32[]{:S(2)}) collective-permute-start(bf16[256,1024]{1,0:T(8,128)(2,1)S(1)} %pad_maximum_fusion.10), channel_id=1, source_target_pairs={{0,8},{1,9},{2,10},{3,11},{4,12},{5,13},{6,14},{7,15},{8,0},{9,1},... | collective-permute-start | bytes 1572872 | tf_op jit(solution)/shard_map/ppermute | solution.py:25
  344.4 19.9 %collective-permute-start.65 = (bf16[256,1024]{1,0:T(8,128)(2,1)S(1)}, bf16[256,1024]{1,0:T(8,128)(2,1)S(1)}, u32[]{:S(2)}, u32[]{:S(2)}) collective-permute-start(bf16[256,1024]{1,0:T(8,128)(2,1)S(1)} %pad_maximum_fusion.13), channel_id=1, source_target_pairs={{0,4},{1,5},{2,6},{3,7},{4,0},{5,1},{6,2},{7,3},{8,12},{9,13},{10,... | collective-permute-start | bytes 1572872 | tf_op jit(solution)/shard_map/ppermute | solution.py:25
  344.7 22.9 %collective-permute-start.74 = (bf16[256,1024]{1,0:T(8,128)(2,1)S(1)}, bf16[256,1024]{1,0:T(8,128)(2,1)S(1)}, u32[]{:S(2)}, u32[]{:S(2)}) collective-permute-start(bf16[256,1024]{1,0:T(8,128)(2,1)S(1)} %pad_maximum_fusion.14), channel_id=1, source_target_pairs={{0,2},{1,3},{2,0},{3,1},{4,6},{5,7},{6,4},{7,5},{8,10},{9,11},{10,... | collective-permute-start | bytes 1572872 | tf_op jit(solution)/shard_map/ppermute | solution.py:25
  345.5 25.9 %collective-permute-start.48 = (bf16[512,1024]{1,0:T(8,128)(2,1)S(1)}, bf16[512,1024]{1,0:T(8,128)(2,1)S(1)}, u32[]{:S(2)}, u32[]{:S(2)}) collective-permute-start(bf16[512,1024]{1,0:T(8,128)(2,1)S(1)} %pad_maximum_fusion.4), channel_id=1, source_target_pairs={{0,1},{1,0},{2,3},{3,2},{4,5},{5,4},{6,7},{7,6},{8,9},{9,8},{10,11... | collective-permute-start | bytes 3145736 | tf_op jit(solution)/shard_map/ppermute | solution.py:25
  363.3 11.1 %collective-permute-start.57 = (bf16[512,1024]{1,0:T(8,128)(2,1)S(1)}, bf16[512,1024]{1,0:T(8,128)(2,1)S(1)}, u32[]{:S(2)}, u32[]{:S(2)}) collective-permute-start(bf16[512,1024]{1,0:T(8,128)(2,1)S(1)} %pad_maximum_fusion.5), channel_id=1, source_target_pairs={{0,1},{1,0},{2,3},{3,2},{4,5},{5,4},{6,7},{7,6},{8,9},{9,8},{10,11... | collective-permute-start | bytes 3145736 | tf_op jit(solution)/shard_map/ppermute | solution.py:25
  363.7 13.8 %collective-permute-start.38 = (bf16[512,1024]{1,0:T(8,128)(2,1)S(1)}, bf16[512,1024]{1,0:T(8,128)(2,1)S(1)}, u32[]{:S(2)}, u32[]{:S(2)}) collective-permute-start(bf16[512,1024]{1,0:T(8,128)(2,1)S(1)} %pad_maximum_fusion.3), channel_id=1, source_target_pairs={{0,1},{1,0},{2,3},{3,2},{4,5},{5,4},{6,7},{7,6},{8,9},{9,8},{10,11... | collective-permute-start | bytes 3145736 | tf_op jit(solution)/shard_map/ppermute | solution.py:25
  364.6 15.9 %collective-permute-start.66 = (bf16[512,1024]{1,0:T(8,128)(2,1)S(1)}, bf16[512,1024]{1,0:T(8,128)(2,1)S(1)}, u32[]{:S(2)}, u32[]{:S(2)}) collective-permute-start(bf16[512,1024]{1,0:T(8,128)(2,1)S(1)} %pad_maximum_fusion.6), channel_id=1, source_target_pairs={{0,1},{1,0},{2,3},{3,2},{4,5},{5,4},{6,7},{7,6},{8,9},{9,8},{10,11... | collective-permute-start | bytes 3145736 | tf_op jit(solution)/shard_map/ppermute | solution.py:25
  367.9 15.7 %collective-permute-start.75 = (bf16[512,1024]{1,0:T(8,128)(2,1)S(1)}, bf16[512,1024]{1,0:T(8,128)(2,1)S(1)}, u32[]{:S(2)}, u32[]{:S(2)}) collective-permute-start(bf16[512,1024]{1,0:T(8,128)(2,1)S(1)} %pad_maximum_fusion.7), channel_id=1, source_target_pairs={{0,1},{1,0},{2,3},{3,2},{4,5},{5,4},{6,7},{7,6},{8,9},{9,8},{10,11... | collective-permute-start | bytes 3145736 | tf_op jit(solution)/shard_map/ppermute | solution.py:25
  (86 other events, 530.8 us)
